TPU v7x, 256 devices: a whole 4x4x8 slice. The times are simulated.
256 devices in a mesh: fsdp: 64 (over z, x, core), tp: 4 (over y).
Axes of the slice: x: 4, y: 4, z: 8, core: 2. Of those that a mesh axis runs over, the one named last changes fastest.
Arguments:
- activations: bfloat16 [8192, 5120], P('fsdp', 'tp'), may hold values from -6 to 6
- out_grad: bfloat16 [8192, 5120], P('fsdp'), may hold values from -0.1875 to 0.1875
- momentum: float32 [5120, 5120], P('fsdp', 'tp'), may hold values from -6 to 6
- right_prev: float32 [5120, 256], P('tp'), may hold values from -6 to 6
Outputs:
- new_momentum: float32 [5120, 5120], P('fsdp', 'tp')
- update: float32 [5120, 5120], P('fsdp', 'tp')
- right_next: float32 [5120, 256], P('tp', 'fsdp')
All inputs are finite; a program needn't handle non-finite values.
Results may differ from a plain program's by a relative error of at most 0.0003.
Values sent between devices are 32-bit elements; how exact they have to be, the bound alone decides.
No kernel may reach another device: no remote copies, remote signals or barrier semaphores. Data moves between devices by JAX's collectives and lax.ppermute only.
A program may use at most 128 MiB of HBM per device.

v0:
```python
import math

import jax
import jax.numpy as jnp
from jax import lax
from jax.sharding import Mesh
from jax.sharding import PartitionSpec as P

D = 5120
R = 256
FSDP = ("fsdp_0", "fsdp_1", "fsdp_2")


momentum_decay = 0.95


def from_everyone(x, axis):
    length = lax.axis_size(axis)
    return lax.all_to_all(jnp.broadcast_to(x[None], (length, *x.shape)), axis, 0, 0, tiled=True)


def over_copies(x, axis):
    everything = from_everyone(x, axis)
    return jnp.sum(everything, axis=0)


def filled_up(lines, length):
    spare = -lines.shape[0] % length
    if not spare:
        return lines
    return jnp.concatenate([lines, jnp.zeros((spare, *lines.shape[1:]), lines.dtype)])


def in_order(blocks, dim):
    lengths = list(blocks.shape[1:])
    lengths[dim] *= blocks.shape[0]
    return jnp.moveaxis(blocks, 0, dim).reshape(lengths)


def gather_axes(x, axes, dim):
    far, near = axes
    blocks = from_everyone(from_everyone(x, far), near)
    return in_order(blocks.swapaxes(0, 1).reshape(-1, *x.shape), dim)


def in_blocks(x, dim, length):
    lengths = x.shape
    blocks = x.reshape(*lengths[:dim], length, lengths[dim] // length, *lengths[dim + 1 :])
    return jnp.moveaxis(blocks, dim, 0)


def summed_on_arrival(x, axis, dim):
    length = lax.axis_size(axis)
    blocks = lax.all_to_all(in_blocks(x, dim, length), axis, 0, 0, tiled=True)
    return jnp.sum(blocks, axis=0)


def sum_in_two_steps(x, axes, dim):
    far, near = axes
    blocks = in_blocks(x, dim, lax.axis_size(far))
    nearer = summed_on_arrival(blocks, near, dim + 1)
    arrived = lax.all_to_all(nearer, far, split_axis=0, concat_axis=0, tiled=True)
    return arrived.sum(axis=0)


def nested_sum(x, axes):
    lines = x.reshape(-1, x.shape[-1])
    padded = filled_up(lines, lax.axis_size(axes[0]) * lax.axis_size(axes[1]))
    whole = gather_axes(sum_in_two_steps(padded, axes, 0), axes, 0)
    return lax.slice_in_dim(whole, 0, len(lines)).reshape(x.shape)


def token_product(out_grad, columns_in):
    return lax.dot_general(
        out_grad, columns_in, (((0,), (0,)), ((), ())), preferred_element_type=jnp.float32
    )


def on_device(activations, out_grad, momentum, right_prev):
    high = lax.Precision.HIGHEST
    grad = lax.psum_scatter(
        token_product(out_grad, activations), FSDP, scatter_dimension=0, tiled=True
    )
    buffer = momentum + grad
    partial_left = jnp.dot(buffer, right_prev, precision=high)
    left = over_copies(partial_left, "tp")
    gram = nested_sum(jnp.dot(left.T, left, precision=high), (("fsdp_0", "fsdp_1"), "fsdp_2"))
    lower = jnp.linalg.cholesky(gram)
    basis = lax.linalg.triangular_solve(lower, left, left_side=False, lower=True, transpose_a=True)
    partial_right = jnp.dot(buffer.T, basis, precision=high)
    right = nested_sum(partial_right, (("fsdp_0", "fsdp_1"), "fsdp_2"))
    squares = over_copies(jnp.sum(right * right, axis=0), "tp")
    factor = lax.rsqrt(squares / D + 1e-06)
    right_next = right * factor[None, :]
    new_momentum = buffer - (1.0 - momentum_decay) * jnp.dot(basis, right.T, precision=high)
    update = math.sqrt(D / R) * jnp.dot(basis, right_next.T, precision=high)
    own_columns = right_next.shape[1] // lax.axis_size(FSDP)
    first_column = lax.axis_index(FSDP) * own_columns
    right_owned = lax.dynamic_slice_in_dim(right_next, first_column, own_columns, 1)
    return (new_momentum, update, right_owned)


def solution(mesh):
    finer = Mesh(
        mesh.devices.reshape(8, 4, 2, mesh.shape["tp"]), ("fsdp_0", "fsdp_1", "fsdp_2", "tp")
    )
    in_specs = (P(FSDP, "tp"), P(FSDP, None), P(FSDP, "tp"), P("tp", None))
    out_specs = (P(FSDP, "tp"), P(FSDP, "tp"), P("tp", FSDP))
    return jax.shard_map(
        on_device, mesh=finer, in_specs=in_specs, out_specs=out_specs, check_vma=False
    )
```

profile of v0, /device:TPU:2, one launch (start us, length us, event | category | flops | bytes accessed | tf_op | source)
XLA Modules:
  0.0 459.2 jit_solution(4135622952621200800)
XLA Ops:
  7.2 1.3 copy-done
  8.5 11.5 %fusion.16 = f32[5120,1280]{1,0:T(8,128)} fusion(bf16[128,5120]{1,0:T(8,128)(2,1)S(1)} %copy-done, bf16[128,1280]{1,0:T(8,128)(2,1)} %param.4), kind=kOutput, calls=%fused_computation.43 | convolution fusion | flops 1677721600 | bytes 27852800 | tf_op jit(solution)/shard_map/dot_general | solution.py:74
  20.0 226.7 %reduce-scatter.2.cloned.1.call-done = f32[80,1280]{1,0:T(8,128)} async-done(((f32[5120,1280]{1,0:T(8,128)}), f32[80,1280]{1,0:T(8,128)}) %reduce-scatter.2.cloned.1.call-update) | async-done | bytes 409616 | tf_op jit(solution)/shard_map/reduce_scatter | solution.py:81
  248.6 11.1 %all_to_all.51 = f32[4,80,256]{2,1,0:T(8,128)S(1)} all-to-all(f32[4,80,256]{2,1,0:T(8,128)S(1)} %broadcast_in_dim.14), channel_id=1, replica_groups=mesh['fsdp_0'=8,'fsdp_1'=4,'fsdp_2'=2,'tp'=4] {'tp'}, dimensions={0} | all-to-all | bytes 655360 | tf_op jit(solution)/shard_map/all_to_all | solution.py:19
  260.2 3.9 all_to_all.52
  264.3 17.0 %all_to_all.53 = f32[32,4,256]{2,1,0:T(4,128)S(1)} all-to-all(f32[32,4,256]{2,1,0:T(4,128)S(1)} %copy.50), channel_id=1, replica_groups=mesh['fsdp_0'=8,'fsdp_1'=4,'fsdp_2'=2,'tp'=4] {'fsdp_0','fsdp_1'}, dimensions={0} | all-to-all | bytes 262144 | tf_op jit(solution)/shard_map/all_to_all | solution.py:62
  282.0 5.5 %all-to-all-start.3 = ((f32[32,4,256]{2,1,0:T(4,128)}), f32[32,4,256]{2,1,0:T(4,128)S(1)}, u32[]{:S(2)}, u32[]{:S(2)}) async-start(f32[32,4,256]{2,1,0:T(4,128)} %broadcast_in_dim.15), calls=%async_computation.4 | async-start | bytes 262144 | tf_op jit(solution)/shard_map/all_to_all | solution.py:19
  287.5 8.9 %all-to-all-done.3 = f32[32,4,256]{2,1,0:T(4,128)S(1)} async-done(((f32[32,4,256]{2,1,0:T(4,128)}), f32[32,4,256]{2,1,0:T(4,128)S(1)}, u32[]{:S(2)}, u32[]{:S(2)}) %all-to-all-start.3) | async-done | bytes 131104 | tf_op jit(solution)/shard_map/all_to_all | solution.py:19
  296.4 3.9 all_to_all.54
  300.7 11.7 %cholesky.50 = f32[128,128]{1,0:T(8,128)S(1)} custom-call(f32[128,128]{1,0:T(8,128)S(1)} %cholesky.118), custom_call_target="Cholesky" | custom-call | tf_op jit(solution)/shard_map/jit(cholesky)/cholesky | solution.py:88
  312.5 9.8 %custom-call.14 = f32[1,128,128]{1,2,0:T(8,128)S(1)} custom-call(f32[1,128,128]{2,1,0:T(8,128)S(1)} %get-tuple-element.42), custom_call_target="InvertDiagBlocksLowerTriangular" | custom-call | tf_op jit(solution)/shard_map/jit(cholesky)/cholesky | solution.py:88
  322.8 11.7 %cholesky.105 = f32[128,128]{1,0:T(8,128)S(1)} custom-call(f32[128,128]{1,0:T(8,128)S(1)} %convolution_subtract_fusion), custom_call_target="Cholesky" | custom-call | tf_op jit(solution)/shard_map/jit(cholesky)/cholesky | solution.py:88
  336.6 4.0 while.1
  337.2 1.4 bitcast_dynamic-update-slice_fusion.2
  339.2 1.4 bitcast_dynamic-update-slice_fusion.2
  340.6 19.9 %custom-call.15 = f32[2,128,128]{1,2,0:T(8,128)S(1)} custom-call(f32[2,128,128]{2,1,0:T(8,128)S(1)} %get-tuple-element.10), custom_call_target="InvertDiagBlocksLowerTriangular" | custom-call | tf_op jit(solution)/shard_map/triangular_solve | solution.py:89
  361.1 2.3 fusion.10
  363.4 1.4 reshape_reshape.11
  365.6 4.8 %all_to_all.55 = f32[2,32,20,256]{3,1,2,0:T(8,128)S(1)} all-to-all(f32[2,32,20,256]{3,1,2,0:T(8,128)S(1)} %copy.53), channel_id=1, replica_groups=mesh['fsdp_0'=8,'fsdp_1'=4,'fsdp_2'=2,'tp'=4] {'fsdp_2'}, dimensions={0} | all-to-all | bytes 2621440 | tf_op jit(solution)/shard_map/all_to_all | solution.py:54
  371.3 1.5 copy.54
  372.8 27.8 %all_to_all.56 = f32[32,20,256]{2,1,0:T(8,128)S(1)} all-to-all(f32[32,20,256]{2,1,0:T(8,128)S(1)} %copy.54), channel_id=1, replica_groups=mesh['fsdp_0'=8,'fsdp_1'=4,'fsdp_2'=2,'tp'=4] {'fsdp_0','fsdp_1'}, dimensions={0} | all-to-all | bytes 1310720 | tf_op jit(solution)/shard_map/all_to_all | solution.py:62
  401.6 5.6 %all-to-all-start.7 = ((f32[32,20,256]{2,1,0:T(8,128)}), f32[32,20,256]{2,1,0:T(8,128)S(1)}, u32[]{:S(2)}, u32[]{:S(2)}) async-start(f32[32,20,256]{2,1,0:T(8,128)} %broadcast_in_dim.17), calls=%async_computation.8 | async-start | bytes 1572864 | tf_op jit(solution)/shard_map/all_to_all | solution.py:19
  407.2 21.7 %all-to-all-done.7 = f32[32,20,256]{2,1,0:T(8,128)S(1)} async-done(((f32[32,20,256]{2,1,0:T(8,128)}), f32[32,20,256]{2,1,0:T(8,128)S(1)}, u32[]{:S(2)}, u32[]{:S(2)}) %all-to-all-start.7) | async-done | bytes 655392 | tf_op jit(solution)/shard_map/all_to_all | solution.py:19
  429.2 4.8 %all_to_all.57 = f32[2,32,20,256]{3,1,2,0:T(8,128)S(1)} all-to-all(f32[2,32,20,256]{3,1,2,0:T(8,128)S(1)} %broadcast_in_dim.18), channel_id=1, replica_groups=mesh['fsdp_0'=8,'fsdp_1'=4,'fsdp_2'=2,'tp'=4] {'fsdp_2'}, dimensions={0} | all-to-all | bytes 2621440 | tf_op jit(solution)/shard_map/all_to_all | solution.py:19
  434.0 1.1 copy-done.1
  435.1 1.9 copy.56
  437.0 1.5 reshape_reshape.12
  438.4 1.5 multiply_reduce_fusion
  440.6 3.2 all-to-all-start.9
  443.8 2.1 fusion
  445.9 3.1 all-to-all-done.9
  449.2 2.1 convolution_multiply_fusion
  (53 shorter events, 11.5 us)
Async XLA Ops:
  7.2 1.3 copy-start
  7.2 239.6 %reduce-scatter.2.cloned.1.call-start = ((), (), s32[]{:S(2)}) async-start(), calls=%async_computation.11 | async-start | bytes 26624000 | tf_op jit(solution)/shard_map/reduce_scatter | solution.py:81
  20.0 226.8 %copy-start.3 = (f32[80,1280]{1,0:T(8,128)S(1)}, f32[80,1280]{1,0:T(8,128)}, u32[]{:S(2)}) copy-start(f32[80,1280]{1,0:T(8,128)} %param.6) | copy-start | bytes 1228804
  20.0 227.8 %copy-start.2 = (f32[1280,256]{1,0:T(8,128)S(1)}, f32[1280,256]{1,0:T(8,128)}, u32[]{:S(2)}) copy-start(f32[1280,256]{1,0:T(8,128)} %param.7) | copy-start | bytes 3932164
  282.0 14.4 %all-to-all-start.3 = ((f32[32,4,256]{2,1,0:T(4,128)}), f32[32,4,256]{2,1,0:T(4,128)S(1)}, u32[]{:S(2)}, u32[]{:S(2)}) async-start(f32[32,4,256]{2,1,0:T(4,128)} %broadcast_in_dim.15), calls=%async_computation.4 | async-start | bytes 262144 | tf_op jit(solution)/shard_map/all_to_all | solution.py:19
  401.6 27.3 %all-to-all-start.7 = ((f32[32,20,256]{2,1,0:T(8,128)}), f32[32,20,256]{2,1,0:T(8,128)S(1)}, u32[]{:S(2)}, u32[]{:S(2)}) async-start(f32[32,20,256]{2,1,0:T(8,128)} %broadcast_in_dim.17), calls=%async_computation.8 | async-start | bytes 1572864 | tf_op jit(solution)/shard_map/all_to_all | solution.py:19
  434.0 1.1 copy-start.1
  440.6 8.5 %all-to-all-start.9 = ((f32[4,1,256]{2,1,0:T(1,128)}), f32[4,1,256]{2,1,0:T(1,128)S(1)}, u32[]{:S(2)}, u32[]{:S(2)}) async-start(f32[4,1,256]{2,1,0:T(1,128)} %broadcast_in_dim.19), calls=%async_computation.10 | async-start | bytes 8192 | tf_op jit(solution)/shard_map/all_to_all | solution.py:19
Sparse Core Ops, SparseCore 0:
  20.1 226.5 reduce-scatter.1
where the time goes:
time: 460 us; the launch traced here: 459 us
  waiting for transfers between devices  260 us (57%)
  blocking collectives  73.3 us (16%)
  other arithmetic  57.7 us (13%)
  matrix products  20.3 us (4%)
  local copies, waits for them, and re-layouts  17.5 us (4%)
  between operations  15.6 us (3%)
  starting transfers between devices  14.3 us (3%)
    reduce_scatter x1, waiting for transfers between devices, on_device(): lax.psum_scatter(token_product(out_grad, activations), FSDP, scatter_dime...  227 us
    all_to_all x2, blocking collectives, sum_in_two_steps(): lax.all_to_all(nearer, far, split_axis=0, concat_axis=0, tiled=True)  44.7 us
    another operation x6, other arithmetic, on_device(): lower = jnp.linalg.cholesky(gram)  33.9 us
    all_to_all x3, waiting for transfers between devices, from_everyone(): lax.all_to_all(jnp.broadcast_to(x[None], (length, *x.shape)), axis, 0, 0,...  33.7 us
    another operation x3, other arithmetic, on_device(): lax.linalg.triangular_solve(lower, left, left_side=False, lower=True, tra...  19.9 us
    all_to_all x3, blocking collectives, from_everyone(): lax.all_to_all(jnp.broadcast_to(x[None], (length, *x.shape)), axis, 0, 0,...  19.8 us
    all_to_all x3, starting transfers between devices, from_everyone(): lax.all_to_all(jnp.broadcast_to(x[None], (length, *x.shape)), axis, 0, 0,...  14.3 us
    dot_general x1, matrix products, token_product(): lax.dot_general(out_grad, columns_in, (((0,), (0,)), ((), ())), preferred...  11.5 us
  transfers between devices with their start and end apart: 4, of which 4 were waited for; matrix products, arithmetic and copies ran while one was open for 0% of the time, Pallas kernels for 0%

commit v1 on v0

v1 whole, which is shorter than its diff:
```python
import math

import jax
import jax.numpy as jnp
from jax import lax
from jax.experimental import pallas as pl
from jax.experimental.pallas import tpu as pltpu
from jax.sharding import Mesh
from jax.sharding import PartitionSpec as P

D = 5120
R = 256
NZ, NX, NC, NY = 8, 4, 2, 4
FSDP = ("z", "x", "c")
TOKENS = 128
ROWS = D // (NZ * NX * NC)
COLS = D // NY
HALF = COLS // NC
PART = HALF // NX
PAIR = NZ // NY
EDGE = 32
STEP = 128
BLOCKS = R // EDGE
F32 = jnp.float32

momentum_decay = 0.95


def shape(*dims):
    return jax.ShapeDtypeStruct(dims, F32)


def shifted(v, axis, n, k):
    return lax.ppermute(v, axis, [(i, (i + k) % n) for i in range(n)])


def other_core(v):
    return lax.ppermute(v, "c", [(0, 1), (1, 0)])


def over_tp(v):
    total = v
    for k in range(1, NY):
        total = total + shifted(v, "tp", NY, k)
    return total


def plain(a, b, dims):
    return lax.dot_general(a, b, (dims, ((), ())), preferred_element_type=F32)


def full(a, b, dims):
    return lax.dot_general(
        a, b, (dims, ((), ())), precision=lax.Precision.HIGHEST, preferred_element_type=F32
    )


def split(v):
    one = v.astype(jnp.bfloat16)
    rest = v - one.astype(F32)
    two = rest.astype(jnp.bfloat16)
    three = (rest - two.astype(F32)).astype(jnp.bfloat16)
    return three, two, one


def narrow_times(a, parts, dims):
    total = None
    for part in parts:
        term = plain(a, part, dims)
        total = term if total is None else total + term
    return total


def call(kernel, scalars, out_shape, in_specs, *args, out_specs=None, grid=(1,), scratch=()):
    if out_specs is None:
        leaves = out_shape if isinstance(out_shape, tuple) else (out_shape,)
        specs = tuple(whole(s.shape) for s in leaves)
        out_specs = specs if isinstance(out_shape, tuple) else specs[0]
    return pl.pallas_call(
        kernel,
        out_shape=out_shape,
        grid_spec=pltpu.PrefetchScalarGridSpec(
            num_scalar_prefetch=1,
            grid=grid,
            in_specs=in_specs,
            out_specs=out_specs,
            scratch_shapes=scratch,
        ),
    )(scalars, *args)


def whole(dims):
    zeros = (0,) * len(dims)
    return pl.BlockSpec(tuple(dims), lambda i, at: zeros)


X, C, T, FIRST = range(4)


def first_kernel(at, acts, momentum, right, out):
    out[...] = jnp.zeros((TOKENS + ROWS, R), F32)

    def step(i, _):
        here = pl.ds(pl.multiple_of(i * 2 * STEP, STEP), 2 * STEP)
        block = right[here, :]
        out[:TOKENS, :] += narrow_times(acts[:, here], split(block), ((1,), (0,)))
        out[TOKENS:, :] += full(momentum[:, here], block, ((1,), (0,)))
        return 0

    lax.fori_loop(0, COLS // (2 * STEP), step, 0)


def turn_kernel(at, outs, out):
    out[...] = outs[...].astype(F32).T.reshape(NX, 1, NC * ROWS, TOKENS)


def left_kernel(at, near_outs, far_outs, v, kept, given):
    parts = split(v[:TOKENS, :])
    kept[...] = narrow_times(near_outs[...], parts, ((0,), (0,)))
    given[...] = narrow_times(far_outs[...], parts, ((0,), (0,)))
    first = at[FIRST]
    inside = (first >= 0) & (first < COLS)
    in_half = first // HALF
    for half, out in ((at[C], kept), (1 - at[C], given)):

        @pl.when(inside & (in_half == half))
        def _():
            here = pl.ds(pl.multiple_of(first - half * HALF, 8), ROWS)
            out[here, :] = out[here, :] + v[TOKENS:, :]


def seen_kernel(at, near_outs, far_outs, near, far, out):
    out[:TOKENS, :] = narrow_times(
        near_outs[...], split(near[...]), ((1,), (0,))
    ) + narrow_times(far_outs[...], split(far[...]), ((1,), (0,)))
    out[TOKENS:, :] = jnp.zeros((ROWS, R), F32)
    first = at[FIRST]
    inside = (first >= 0) & (first < COLS)
    in_half = first // HALF
    for half, source in ((at[C], near), (1 - at[C], far)):

        @pl.when(inside & (in_half == half))
        def _():
            here = pl.ds(pl.multiple_of(first - half * HALF, 8), ROWS)
            out[TOKENS:, :] = source[here, :]


def gram_kernel(at, near, far, out):
    out[...] = jnp.zeros((R, R), F32)

    def step(i, _):
        here = pl.ds(pl.multiple_of(i * STEP, STEP), STEP)
        block = jnp.concatenate([near[here, :], far[here, :]], axis=0)
        out[...] += full(block, block, ((0,), (0,)))
        return 0

    lax.fori_loop(0, HALF // STEP, step, 0)


def raw_kernel(at, near_acts, far_acts, near_mom, far_mom, v, kept, given):
    parts = split(v[:TOKENS, :])
    low = v[TOKENS:, :]

    def step(i, _):
        here = pl.ds(pl.multiple_of(i * STEP, STEP), STEP)
        for acts, mom, out in ((near_acts, near_mom, kept), (far_acts, far_mom, given)):
            top = narrow_times(acts[:, here], parts, ((0,), (0,)))
            out[here, :] = top + full(mom[:, here], low, ((0,), (0,)))
        return 0

    lax.fori_loop(0, HALF // STEP, step, 0)


def share_kernel(at, kept, arrived, *outs):
    for k, out in enumerate(outs):
        here = pl.ds(pl.multiple_of(((at[X] + k) & (NX - 1)) * PART, 8), PART)
        out[...] = kept[here, :] + arrived[here, :]


def gather_kernel(at, *refs):
    out = refs[-1]
    for k, ref in enumerate(refs[:-1]):
        here = pl.ds(pl.multiple_of(((at[X] - k) & (NX - 1)) * PART, 8), PART)
        out[here, :] = ref[...]


def right_kernel(at, near, far, inverse, out, squares):
    n = inverse[...]

    def step(i, total):
        here = pl.ds(pl.multiple_of(i * STEP, STEP), STEP)
        block = jnp.concatenate([near[here, :], far[here, :]], axis=0)
        value = full(block, n, ((1,), (1,)))
        for k, half in enumerate((at[C], 1 - at[C])):
            there = pl.ds(pl.multiple_of(half * HALF + i * STEP, STEP), STEP)
            out[there, :] = value[k * STEP : (k + 1) * STEP, :]
        return total + jnp.sum(value * value, axis=0, keepdims=True)

    total = lax.fori_loop(0, HALF // STEP, step, jnp.zeros((1, R), F32))
    squares[...] = jnp.broadcast_to(total, (8, R))


def update_kernel(at, basis, right, factor, change, update):
    left = jnp.concatenate([basis[...], basis[...] * factor[:1, :]], axis=0)

    def step(i, _):
        here = pl.ds(pl.multiple_of(i * 2 * STEP, STEP), 2 * STEP)
        value = full(left, right[here, :], ((1,), (1,)))
        change[:, here] = (1.0 - momentum_decay) * value[:ROWS, :]
        update[:, here] = math.sqrt(D / R) * value[ROWS:, :]
        return 0

    lax.fori_loop(0, COLS // (2 * STEP), step, 0)


def eliminate(first_block, count, work_ref, out_ref):
    rows = lax.broadcasted_iota(jnp.int32, (EDGE, 2 * EDGE), 0)
    lanes = lax.broadcasted_iota(jnp.int32, (EDGE, 2 * EDGE), 1)
    eye = (rows + EDGE == lanes).astype(F32)
    rest_lanes = lax.broadcasted_iota(jnp.int32, (EDGE, R), 1)

    def step(i, _):
        here = pl.ds(pl.multiple_of(i * EDGE, EDGE), EDGE)
        state = jnp.where(lanes < EDGE, work_ref[here, : 2 * EDGE], eye)
        pivots = jnp.zeros((EDGE, 2 * EDGE), F32)
        for k in range(EDGE):
            column = jnp.broadcast_to(state[:, k : k + 1], (EDGE, 2 * EDGE))
            pivot = column[k : k + 1, :]
            line = state[k : k + 1, :] / pivot
            pivots = jnp.where(rows == k, jnp.broadcast_to(pivot, rows.shape), pivots)
            if k < EDGE - 1:
                state = state - jnp.where(rows > k, column, 0.0) * line
        inverse = (state * lax.rsqrt(pivots))[:, EDGE:]
        upper = full(inverse, work_ref[here, :], ((1,), (0,)))
        out_ref[here, :] = pltpu.roll(upper, i * EDGE, 1)[:, R:]
        rest = jnp.where(rest_lanes < (BLOCKS - i) * EDGE, upper[:, :R], 0.0)
        change = full(rest, upper, ((0,), (0,)))
        for r in range(1, BLOCKS):
            there = pl.ds(pl.multiple_of(((i + r) % BLOCKS) * EDGE, EDGE), EDGE)
            left = work_ref[there, :] - change[r * EDGE : (r + 1) * EDGE, :]
            work_ref[there, :] = pltpu.roll(left, 2 * R - EDGE, 1)
        return 0

    lax.fori_loop(first_block, first_block + count, step, 0)


def early_kernel(at, gram, work, out):
    all_rows = lax.broadcasted_iota(jnp.int32, (R, R), 0)
    all_lanes = lax.broadcasted_iota(jnp.int32, (R, R), 1)
    work[:, :R] = gram[...]
    work[:, R:] = (all_rows == all_lanes).astype(F32)
    out[...] = jnp.zeros((R, R), F32)
    eliminate(0, BLOCKS // 2, work, out)


def late_kernel(at, work, done, out, held):
    held[...] = work[...]
    out[...] = done[...]
    eliminate(BLOCKS // 2, BLOCKS // 2, held, out)


def product_kernel(at, outs, acts, kept, given, joined):
    @pl.when(pl.program_id(0) == 0)
    def _():
        joined[...] = acts[...].astype(jnp.bfloat16)

    lhs = jnp.concatenate([outs[0, k].astype(jnp.bfloat16) for k in range(NX)], axis=1)
    total = plain(lhs, joined[...], ((1,), (0,)))
    first = at[C] == 0
    for i in range(PAIR):
        near = total[NC * i * ROWS : (NC * i + 1) * ROWS]
        far = total[(NC * i + 1) * ROWS : (NC * i + 2) * ROWS]
        kept[i * ROWS : (i + 1) * ROWS, :] = jnp.where(first, near, far)
        given[i * ROWS : (i + 1) * ROWS, :] = jnp.where(first, far, near)


def core_products(at, outs, acts):
    half = shape(NZ * ROWS, COLS)
    half_spec = pl.BlockSpec((PAIR * ROWS, COLS), lambda i, at: (i, 0))
    outs_spec = pl.BlockSpec((1, NX, PAIR * NC * ROWS, TOKENS), lambda i, at: (i, 0, 0, 0))
    return call(
        product_kernel, at, (half, half), [outs_spec, whole(acts.shape)],
        outs, acts, out_specs=(half_spec, half_spec), grid=(NY,),
        scratch=[pltpu.VMEM(acts.shape, jnp.bfloat16)],
    )


def half_blocks(rows, quarter):
    scale = NC if quarter else 0
    near = pl.BlockSpec((rows, HALF), lambda i, at: (0, scale * at[T] + at[C]))
    far = pl.BlockSpec((rows, HALF), lambda i, at: (0, scale * at[T] + 1 - at[C]))
    return [near, far]


def summed_piece(at, kept, given, beside=None):
    arrived = other_core(given)
    blocks = call(share_kernel, at, (shape(PART, R),) * NX, [whole((HALF, R))] * 2, kept, arrived)
    total = blocks[0]
    for k in range(1, NX):
        total = total + shifted(blocks[k], "x", NX, k)
    if beside is not None:
        total, beside = lax.optimization_barrier((total, beside))
    pieces = total.reshape(NZ, PART // NZ, R)
    arrived = lax.all_to_all(pieces, "z", 0, 0, tiled=True)
    return jnp.sum(arrived, axis=0), beside


def whole_of(at, piece):
    copies = jnp.broadcast_to(piece[None], (NZ, *piece.shape))
    part = lax.all_to_all(copies, "z", 0, 0, tiled=True)
    part = part.reshape(PART, R)
    arrived = [part] + [shifted(part, "x", NX, k) for k in range(1, NX)]
    near = call(gather_kernel, at, shape(HALF, R), [whole((PART, R))] * NX, *arrived)
    return near, other_core(near)


def on_device(activations, out_grad, momentum, right_prev):
    z, x, c = lax.axis_index("z"), lax.axis_index("x"), lax.axis_index("c")
    t = lax.axis_index("tp")
    mine = (z * NX + x) * NC + c
    at = jnp.stack([x, c, t, mine * ROWS - t * COLS]).astype(jnp.int32)
    outs_halves, acts_halves = half_blocks(TOKENS, True), half_blocks(TOKENS, False)
    mom_halves = half_blocks(ROWS, False)
    two_halves = (shape(HALF, R),) * 2
    tall = shape(TOKENS + ROWS, R)

    first = call(
        first_kernel, at, tall,
        [whole((TOKENS, COLS)), whole((ROWS, COLS)), whole((COLS, R))],
        activations, momentum, right_prev,
    )
    first = over_tp(first)

    acts = lax.all_gather(activations.astype(F32), "x", axis=0, tiled=True)
    turned = call(
        turn_kernel, at, shape(NX, PAIR, NC * ROWS, TOKENS),
        [pl.BlockSpec((TOKENS, D // NZ), lambda i, at: (0, PAIR * at[T] + i))], out_grad,
        out_specs=pl.BlockSpec((NX, 1, NC * ROWS, TOKENS), lambda i, at: (0, i, 0, 0)),
        grid=(PAIR,),
    )
    turned = turned.reshape(NX, PAIR * NC * ROWS, TOKENS)
    outs = lax.all_to_all(turned, "x", 0, 0, tiled=True)
    outs = lax.all_gather(outs, "tp", axis=0, tiled=False)

    kept, given = call(
        left_kernel, at, two_halves, [*outs_halves, whole(tall.shape)],
        out_grad, out_grad, first,
    )
    piece, _ = summed_piece(at, kept, given)
    near, far = whole_of(at, piece)
    seen = call(
        seen_kernel, at, tall, [*outs_halves, whole((HALF, R)), whole((HALF, R))],
        out_grad, out_grad, near, far,
    )
    seen, at_seen = lax.optimization_barrier((seen, at))
    second = over_tp(seen)

    kept_grad, given_grad = core_products(at_seen, outs, acts)
    gram = call(gram_kernel, at, shape(R, R), [whole((HALF, R))] * 2, near, far)
    kept_grad, gram, second = lax.optimization_barrier((kept_grad, gram, second))
    summed_grad = kept_grad + other_core(given_grad)
    grad = lax.psum_scatter(summed_grad, "z", scatter_dimension=0, tiled=True)
    gram = over_tp(gram)

    kept, given = call(
        raw_kernel, at, two_halves, [*acts_halves, *mom_halves, whole(tall.shape)],
        activations, activations, momentum, momentum, second,
    )
    piece, gram = summed_piece(at, kept, given, gram)
    work, done = call(early_kernel, at, (shape(R, 2 * R), shape(R, R)), [whole((R, R))], gram)
    piece, work = lax.optimization_barrier((piece, work))
    near, far = whole_of(at, piece)
    inverse = call(
        late_kernel, at, shape(R, R), [whole((R, 2 * R)), whole((R, R))], work, done,
        scratch=[pltpu.VMEM((R, 2 * R), F32)],
    )
    basis = lax.dot_general(
        second[TOKENS:], inverse, (((1,), (1,)), ((), ())), precision=lax.Precision.HIGHEST
    )
    right, squares = call(
        right_kernel, at, (shape(COLS, R), shape(8, R)),
        [whole((HALF, R)), whole((HALF, R)), whole((R, R))], near, far, inverse,
    )
    squares = over_tp(squares)
    factor = lax.rsqrt(squares / D + 1e-06)
    change, update = call(
        update_kernel, at, (shape(ROWS, COLS),) * 2,
        [whole((ROWS, R)), whole((COLS, R)), whole((8, R))], basis, right, factor,
    )
    new_momentum = (momentum + grad) - change
    own = R // (NZ * NX * NC)
    right_owned = lax.dynamic_slice_in_dim(right, mine * own, own, 1)
    right_owned = right_owned * lax.dynamic_slice_in_dim(factor[:1], mine * own, own, 1)
    return (new_momentum, update, right_owned)


def solution(mesh):
    finer = Mesh(mesh.devices.reshape(NZ, NX, NC, mesh.shape["tp"]), ("z", "x", "c", "tp"))
    in_specs = (P(FSDP, "tp"), P(FSDP, None), P(FSDP, "tp"), P("tp", None))
    out_specs = (P(FSDP, "tp"), P(FSDP, "tp"), P("tp", FSDP))
    return jax.shard_map(
        on_device, mesh=finer, in_specs=in_specs, out_specs=out_specs, check_vma=False
    )
```

time: 460 us -> 280 us (0.61)
  waiting for transfers between devices: 260 us -> 45.3 us
  Pallas kernels: 0 us -> 90.9 us
  other arithmetic: 57.7 us -> 16.7 us
  starting transfers between devices: 14.3 us -> 38.5 us
  matrix products: 20.3 us -> 1.99 us
  local copies, waits for them, and re-layouts: 17.5 us -> 6.47 us
  blocking collectives: 73.3 us -> 62.8 us
    reduce_scatter x1, waiting for transfers between devices: 227 us -> 0.01 us  [on_device(): grad = lax.psum_scatter(summed_grad, 'z', scatter_dimension=0, tiled=True)]
    pallas_call x0 -> x15, Pallas kernels: none -> 90.9 us  [call(): pl.pallas_call(kernel, out_shape=out_shape, grid_spec=pltpu.PrefetchScala...]
    another operation x9 -> x1, other arithmetic: 53.9 us -> 0.65 us  [on_device(): at = jnp.stack([x, c, t, mine * ROWS - t * COLS]).astype(jnp.int32)]
    ppermute x0 -> x29, waiting for transfers between devices: none -> 45.2 us  [the longest x24 40.4 us: shifted(): return lax.ppermute(v, axis, [(i, (i + k) % n) for i in range(n)])]
    ppermute x0 -> x29, starting transfers between devices: none -> 35 us  [the longest x24 34.9 us: shifted(): return lax.ppermute(v, axis, [(i, (i + k) % n) for i in range(n)])]
    all_to_all x3 -> x1, waiting for transfers between devices: 33.7 us -> 0.01 us  [summed_piece(): arrived = lax.all_to_all(pieces, 'z', 0, 0, tiled=True)]
    dot_general x6 -> x1, matrix products: 19.2 us -> 1.99 us  [on_device(): lax.dot_general(second[TOKENS:], inverse, (((1,), (1,)), ((), ())), preci...]
    all_to_all x3 -> x1, starting transfers between devices: 14.3 us -> 3.39 us  [summed_piece(): arrived = lax.all_to_all(pieces, 'z', 0, 0, tiled=True)]
  transfers between devices with their start and end apart: 4 -> 33, of which waited for: 4 -> 22; matrix products, arithmetic and copies ran while one was open for 0% -> 5% of each run, Pallas kernels for 0% -> 30%
where the time goes in v1:
time: 280 us; the launch traced here: 277 us
  Pallas kernels  90.9 us (32%)
  blocking collectives  62.8 us (22%)
  waiting for transfers between devices  45.3 us (16%)
  starting transfers between devices  38.5 us (14%)
  other arithmetic  16.7 us (6%)
  between operations  13.9 us (5%)
  local copies, waits for them, and re-layouts  6.47 us (2%)
    pallas_call x15, Pallas kernels, call(): pl.pallas_call(kernel, out_shape=out_shape, grid_spec=pltpu.PrefetchScala...  90.9 us
    ppermute x24, waiting for transfers between devices, shifted(): return lax.ppermute(v, axis, [(i, (i + k) % n) for i in range(n)])  40.4 us
    ppermute x24, starting transfers between devices, shifted(): return lax.ppermute(v, axis, [(i, (i + k) % n) for i in range(n)])  34.9 us
    all_to_all x2, blocking collectives, whole_of(): part = lax.all_to_all(copies, 'z', 0, 0, tiled=True)  29.6 us
    all_to_all x1, blocking collectives, summed_piece(): arrived = lax.all_to_all(pieces, 'z', 0, 0, tiled=True)  18.9 us
    all_to_all x1, blocking collectives, on_device(): outs = lax.all_to_all(turned, 'x', 0, 0, tiled=True)  14.4 us
  transfers between devices with their start and end apart: 33, of which 22 were waited for; matrix products, arithmetic and copies ran while one was open for 5% of the time, Pallas kernels for 30%

profile of v1, /device:TPU:2, one launch (start us, length us, event | category | flops | bytes accessed | tf_op | source)
XLA Modules:
  0.0 276.7 jit_solution(17596909648048034576)
XLA Ops:
  9.8 2.6 shard_map.72
  12.4 14.4 %all_to_all.25 = f32[4,320,128]{2,1,0:T(8,128)} all-to-all(f32[4,320,128]{2,1,0:T(8,128)} %bitcast.9), channel_id=1, replica_groups=mesh['z'=8,'x'=4,'c'=2,'tp'=4] {'x'}, dimensions={0} | all-to-all | bytes 1310720 | tf_op jit(solution)/shard_map/all_to_all | solution.py:342
  26.9 4.8 %shard_map.67 = f32[208,256]{1,0:T(8,128)} custom-call(s32[4]{0:T(128)} %pad_add_fusion.at, bf16[128,1280]{1,0:T(8,128)(2,1)} %far_acts.1, f32[80,1280]{1,0:T(8,128)} %far_mom.1, f32[1280,256]{1,0:T(8,128)} %right.1), custom_call_target="tpu_custom_call" | custom-call | tf_op jit(solution)/shard_map/pallas_call | solution.py:79
  31.7 3.1 %collective-permute-start.2 = (f32[208,256]{1,0:T(8,128)}, f32[208,256]{1,0:T(8,128)S(1)}, u32[]{:S(2)}, u32[]{:S(2)}) collective-permute-start(f32[208,256]{1,0:T(8,128)} %shard_map.67), channel_id=1, source_target_pairs={{0,3},{1,0},{2,1},{3,2},{4,7},{5,4},{6,5},{7,6},{8,11},{9,8},{10,9... | collective-permute-start | bytes 638984 | tf_op jit(solution)/shard_map/ppermute | solution.py:34
  36.4 6.6 %collective-permute-done.2 = f32[208,256]{1,0:T(8,128)S(1)} collective-permute-done((f32[208,256]{1,0:T(8,128)}, f32[208,256]{1,0:T(8,128)S(1)}, u32[]{:S(2)}, u32[]{:S(2)}) %collective-permute-start.2) | collective-permute-done | bytes 213024 | tf_op jit(solution)/shard_map/ppermute | solution.py:34
  48.3 3.5 %shard_map.68 = (f32[640,256]{1,0:T(8,128)}, f32[640,256]{1,0:T(8,128)}) custom-call(s32[4]{0:T(128)} %pad_add_fusion.at, bf16[128,5120]{1,0:T(8,128)(2,1)} %outs.1, bf16[128,5120]{1,0:T(8,128)(2,1)} %outs.1, f32[208,256]{1,0:T(8,128)} %add_add_fusion.2.v), custom_call_target="tpu_custom_call" | custom-call | tf_op jit(solution)/shard_map/pallas_call | solution.py:79
  51.8 2.3 collective-permute-done.3.arrived
  54.9 2.8 %shard_map.69 = (f32[160,256]{1,0:T(8,128)}, f32[160,256]{1,0:T(8,128)}, f32[160,256]{1,0:T(8,128)}, f32[160,256]{1,0:T(8,128)}) custom-call(s32[4]{0:T(128)} %pad_add_fusion.at, f32[640,256]{1,0:T(8,128)} %get-tuple-element.32.kept, f32[640,256]{1,0:T(8,128)} %copy-done.8), custom_call_target="tpu_custom_call" | custom-call | tf_op jit(solution)/shard_map/pallas_call | solution.py:79
  58.0 3.3 %collective-permute-start.5 = (f32[160,256]{1,0:T(8,128)}, f32[160,256]{1,0:T(8,128)S(1)}, u32[]{:S(2)}, u32[]{:S(2)}) collective-permute-start(f32[160,256]{1,0:T(8,128)} %get-tuple-element.36), channel_id=1, source_target_pairs={{0,16},{8,24},{16,0},{24,8},{1,17},{9,25},{17,1},{25,9},{2,18},{10... | collective-permute-start | bytes 491528 | tf_op jit(solution)/shard_map/ppermute | solution.py:34
  62.0 3.0 %collective-permute-done.4 = f32[160,256]{1,0:T(8,128)S(1)} collective-permute-done((f32[160,256]{1,0:T(8,128)}, f32[160,256]{1,0:T(8,128)S(1)}, u32[]{:S(2)}, u32[]{:S(2)}) %collective-permute-start.4) | collective-permute-done | bytes 163872 | tf_op jit(solution)/shard_map/ppermute | solution.py:34
  66.8 2.5 collective-permute-done.6
  70.2 18.9 %all_to_all.26 = f32[8,20,256]{2,1,0:T(8,128)S(1)} all-to-all(f32[8,20,256]{2,1,0:T(8,128)S(1)} %reshape.23), channel_id=1, replica_groups=mesh['z'=8,'x'=4,'c'=2,'tp'=4] {'z'}, dimensions={0} | all-to-all | bytes 327680 | tf_op jit(solution)/shard_map/all_to_all | solution.py:304
  89.2 12.2 %all_to_all.27 = f32[8,20,256]{2,1,0:T(8,128)S(1)} all-to-all(f32[8,20,256]{2,1,0:T(8,128)S(1)} %broadcast_in_dim.4), channel_id=1, replica_groups=mesh['z'=8,'x'=4,'c'=2,'tp'=4] {'z'}, dimensions={0} | all-to-all | bytes 327680 | tf_op jit(solution)/shard_map/all_to_all | solution.py:310
  104.3 2.5 collective-permute-start.7
  111.3 2.7 shard_map.70.near
  117.2 3.3 %shard_map.71 = f32[208,256]{1,0:T(8,128)} custom-call(s32[4]{0:T(128)} %pad_add_fusion.at, bf16[128,5120]{1,0:T(8,128)(2,1)} %outs.1, bf16[128,5120]{1,0:T(8,128)(2,1)} %outs.1, f32[640,256]{1,0:T(8,128)} %shard_map.70.near, f32[640,256]{1,0:T(8,128)} %copy-done.1), custom_call_target="tpu_custom_call" | custom-call | tf_op jit(solution)/shard_map/pallas_call | solution.py:79
  120.5 7.8 %shard_map.73 = (f32[640,1280]{1,0:T(8,128)}, f32[640,1280]{1,0:T(8,128)}) custom-call(s32[4]{0:T(128)} %pad_add_fusion.at, f32[4,4,320,128]{3,2,1,0:T(8,128)} %bitcast.10, f32[512,1280]{1,0:T(8,128)} %all-gather.4.cloned.1.call-done.acts), custom_call_target="tpu_custom_call" | custom-call | tf_op jit(solution)/shard_map/pallas_call | solution.py:79
  130.4 4.8 %shard_map.74 = f32[256,256]{1,0:T(8,128)} custom-call(s32[4]{0:T(128)} %pad_add_fusion.at, f32[640,256]{1,0:T(8,128)} %shard_map.70.near, f32[640,256]{1,0:T(8,128)} %copy-done.1), custom_call_target="tpu_custom_call" | custom-call | tf_op jit(solution)/shard_map/pallas_call | solution.py:79
  138.8 3.6 %collective-permute-done.11 = f32[208,256]{1,0:T(8,128)} collective-permute-done((f32[208,256]{1,0:T(8,128)S(1)}, f32[208,256]{1,0:T(8,128)}, u32[]{:S(2)}, u32[]{:S(2)}) %collective-permute-start.11) | collective-permute-done | bytes 213024 | tf_op jit(solution)/shard_map/ppermute | solution.py:34
  144.3 4.0 %add.89 = f32[640,1280]{1,0:T(8,128)} add(f32[640,1280]{1,0:T(8,128)} %get-tuple-element.41, f32[640,1280]{1,0:T(8,128)S(1)} %collective-permute-done.14) | non-fusion elementwise | flops 819200 | bytes 9830400 | tf_op jit(solution)/shard_map/add | solution.py:361
  148.3 5.6 %shard_map.75 = (f32[640,256]{1,0:T(8,128)}, f32[640,256]{1,0:T(8,128)}) custom-call(s32[4]{0:T(128)} %pad_add_fusion.at, bf16[128,1280]{1,0:T(8,128)(2,1)} %far_acts.1, bf16[128,1280]{1,0:T(8,128)(2,1)} %far_acts.1, f32[80,1280]{1,0:T(8,128)} %far_mom.1, f32[80,1280]{1,0:T(8,128)} %far_mom.1, f32[208,256]{1,0:T(8,128)} %add_add_fusion.1.v), custom_call_target="tpu_custom_call" | custom-call | tf_op jit(solution)/shard_map/pallas_call | solution.py:79
  157.0 2.9 %shard_map.76 = (f32[160,256]{1,0:T(8,128)}, f32[160,256]{1,0:T(8,128)}, f32[160,256]{1,0:T(8,128)}, f32[160,256]{1,0:T(8,128)}) custom-call(s32[4]{0:T(128)} %pad_add_fusion.at, f32[640,256]{1,0:T(8,128)} %get-tuple-element.44.kept, f32[640,256]{1,0:T(8,128)} %copy-done.6), custom_call_target="tpu_custom_call" | custom-call | tf_op jit(solution)/shard_map/pallas_call | solution.py:79
  161.5 3.7 %collective-permute-start.17 = (f32[160,256]{1,0:T(8,128)}, f32[160,256]{1,0:T(8,128)S(1)}, u32[]{:S(2)}, u32[]{:S(2)}) collective-permute-start(f32[160,256]{1,0:T(8,128)} %get-tuple-element.48), channel_id=1, source_target_pairs={{0,16},{8,24},{16,0},{24,8},{1,17},{9,25},{17,1},{25,9},{2,18},{10... | collective-permute-start | bytes 491528 | tf_op jit(solution)/shard_map/ppermute | solution.py:34
  166.4 3.9 %collective-permute-done.19 = f32[256,256]{1,0:T(8,128)S(1)} collective-permute-done((f32[256,256]{1,0:T(8,128)S(1)}, f32[256,256]{1,0:T(8,128)S(1)}, u32[]{:S(2)}, u32[]{:S(2)}) %collective-permute-start.19) | collective-permute-done | bytes 262176 | tf_op jit(solution)/shard_map/ppermute | solution.py:34
  174.8 3.4 %all-to-all-start.3 = ((f32[8,20,256]{2,1,0:T(8,128)}), f32[8,20,256]{2,1,0:T(8,128)S(1)}, u32[]{:S(2)}, u32[]{:S(2)}) async-start(f32[8,20,256]{2,1,0:T(8,128)} %reshape.26), calls=%async_computation.4 | async-start | bytes 393216 | tf_op jit(solution)/shard_map/all_to_all | solution.py:304
  178.2 18.6 %shard_map.77 = (f32[256,512]{1,0:T(8,128)}, f32[256,256]{1,0:T(8,128)}) custom-call(s32[4]{0:T(128)} %pad_add_fusion.at, f32[256,256]{1,0:T(8,128)} %add_add_fusion.gram), custom_call_target="tpu_custom_call" | custom-call | tf_op jit(solution)/shard_map/pallas_call | solution.py:79
  196.9 17.4 %all_to_all.28 = f32[8,20,256]{2,1,0:T(8,128)S(1)} all-to-all(f32[8,20,256]{2,1,0:T(8,128)S(1)} %broadcast_in_dim.5), channel_id=1, replica_groups=mesh['z'=8,'x'=4,'c'=2,'tp'=4] {'z'}, dimensions={0} | all-to-all | bytes 327680 | tf_op jit(solution)/shard_map/all_to_all | solution.py:310
  217.2 2.5 collective-permute-start.22
  224.6 2.7 shard_map.79.near
  227.3 18.6 %shard_map.78.inverse = f32[256,256]{1,0:T(8,128)} custom-call(s32[4]{0:T(128)} %pad_add_fusion.at, f32[256,512]{1,0:T(8,128)} %get-tuple-element.54.work, f32[256,256]{1,0:T(8,128)} %get-tuple-element.55.done), custom_call_target="tpu_custom_call" | custom-call | tf_op jit(solution)/shard_map/pallas_call | solution.py:79
  246.7 5.2 %shard_map.80 = (f32[1280,256]{1,0:T(8,128)}, f32[8,256]{1,0:T(8,128)}) custom-call(s32[4]{0:T(128)} %pad_add_fusion.at, f32[640,256]{1,0:T(8,128)} %shard_map.79.near, f32[640,256]{1,0:T(8,128)} %copy-done.7, f32[256,256]{1,0:T(8,128)} %shard_map.78.inverse), custom_call_target="tpu_custom_call" | custom-call | tf_op jit(solution)/shard_map/pallas_call | solution.py:79
  263.3 5.0 %shard_map.81 = (f32[80,1280]{1,0:T(8,128)}, f32[80,1280]{1,0:T(8,128)}) custom-call(s32[4]{0:T(128)} %pad_add_fusion.at, f32[80,256]{1,0:T(8,128)} %fusion.basis, f32[1280,256]{1,0:T(8,128)} %get-tuple-element.57.right, f32[8,256]{1,0:T(8,128)} %copy-done.15), custom_call_target="tpu_custom_call" | custom-call | tf_op jit(solution)/shard_map/pallas_call | solution.py:79
  (111 shorter events, 64.5 us)
Async XLA Ops:
  7.2 113.3 %all-gather.4.cloned.1.call-start = ((), (), s32[]{:S(2)}) async-start(), calls=%async_computation.6 | async-start | bytes 3276800 | tf_op jit(solution)/shard_map/all_gather | solution.py:334
  9.1 111.4 %all-gather.6.cloned.1.call-start = ((), (), s32[]{:S(2)}) async-start(), calls=%async_computation.8 | async-start | bytes 3276800 | tf_op jit(solution)/shard_map/all_gather | solution.py:343
  26.8 241.4 %reduce-scatter.2.cloned.1.call-start = ((), (), s32[]{:S(2)}) async-start(), calls=%async_computation.7 | async-start | bytes 3686400 | tf_op jit(solution)/shard_map/reduce_scatter | solution.py:362
  31.7 11.3 %collective-permute-start.2 = (f32[208,256]{1,0:T(8,128)}, f32[208,256]{1,0:T(8,128)S(1)}, u32[]{:S(2)}, u32[]{:S(2)}) collective-permute-start(f32[208,256]{1,0:T(8,128)} %shard_map.67), channel_id=1, source_target_pairs={{0,3},{1,0},{2,1},{3,2},{4,7},{5,4},{6,5},{7,6},{8,11},{9,8},{10,9... | collective-permute-start | bytes 638984 | tf_op jit(solution)/shard_map/ppermute | solution.py:34
  34.8 9.6 %collective-permute-start.1 = (f32[208,256]{1,0:T(8,128)}, f32[208,256]{1,0:T(8,128)S(1)}, u32[]{:S(2)}, u32[]{:S(2)}) collective-permute-start(f32[208,256]{1,0:T(8,128)} %shard_map.67), channel_id=1, source_target_pairs={{0,2},{1,3},{2,0},{3,1},{4,6},{5,7},{6,4},{7,5},{8,10},{9,11},{10,... | collective-permute-start | bytes 638984 | tf_op jit(solution)/shard_map/ppermute | solution.py:34
  35.4 11.2 %collective-permute-start = (f32[208,256]{1,0:T(8,128)}, f32[208,256]{1,0:T(8,128)S(1)}, u32[]{:S(2)}, u32[]{:S(2)}) collective-permute-start(f32[208,256]{1,0:T(8,128)} %shard_map.67), channel_id=1, source_target_pairs={{0,1},{1,2},{2,3},{3,0},{4,5},{5,6},{6,7},{7,4},{8,9},{9,10},{10,1... | collective-permute-start | bytes 638984 | tf_op jit(solution)/shard_map/ppermute | solution.py:34
  51.8 2.3 collective-permute-start.3
  57.8 7.3 %collective-permute-start.4 = (f32[160,256]{1,0:T(8,128)}, f32[160,256]{1,0:T(8,128)S(1)}, u32[]{:S(2)}, u32[]{:S(2)}) collective-permute-start(f32[160,256]{1,0:T(8,128)} %get-tuple-element.35), channel_id=1, source_target_pairs={{0,8},{8,16},{16,24},{24,0},{1,9},{9,17},{17,25},{25,1},{2,10},{10... | collective-permute-start | bytes 491528 | tf_op jit(solution)/shard_map/ppermute | solution.py:34
  58.0 8.8 %collective-permute-start.5 = (f32[160,256]{1,0:T(8,128)}, f32[160,256]{1,0:T(8,128)S(1)}, u32[]{:S(2)}, u32[]{:S(2)}) collective-permute-start(f32[160,256]{1,0:T(8,128)} %get-tuple-element.36), channel_id=1, source_target_pairs={{0,16},{8,24},{16,0},{24,8},{1,17},{9,25},{17,1},{25,9},{2,18},{10... | collective-permute-start | bytes 491528 | tf_op jit(solution)/shard_map/ppermute | solution.py:34
  61.3 8.0 %collective-permute-start.6 = (f32[160,256]{1,0:T(8,128)}, f32[160,256]{1,0:T(8,128)S(1)}, u32[]{:S(2)}, u32[]{:S(2)}) collective-permute-start(f32[160,256]{1,0:T(8,128)} %get-tuple-element.37), channel_id=1, source_target_pairs={{0,24},{8,0},{16,8},{24,16},{1,25},{9,1},{17,9},{25,17},{2,26},{10... | collective-permute-start | bytes 491528 | tf_op jit(solution)/shard_map/ppermute | solution.py:34
  101.4 6.5 %collective-permute-start.9 = (f32[160,256]{1,0:T(8,128)S(1)}, f32[160,256]{1,0:T(8,128)S(1)}, u32[]{:S(2)}, u32[]{:S(2)}) collective-permute-start(f32[160,256]{1,0:T(8,128)S(1)} %reshape.24.refs_0_), channel_id=1, source_target_pairs={{0,24},{8,0},{16,8},{24,16},{1,25},{9,1},{17,9},{25,17},{2,26},{10... | collective-permute-start | bytes 491528 | tf_op jit(solution)/shard_map/ppermute | solution.py:34
  102.4 7.2 %collective-permute-start.8 = (f32[160,256]{1,0:T(8,128)S(1)}, f32[160,256]{1,0:T(8,128)S(1)}, u32[]{:S(2)}, u32[]{:S(2)}) collective-permute-start(f32[160,256]{1,0:T(8,128)S(1)} %reshape.24.refs_0_), channel_id=1, source_target_pairs={{0,16},{8,24},{16,0},{24,8},{1,17},{9,25},{17,1},{25,9},{2,18},{10... | collective-permute-start | bytes 491528 | tf_op jit(solution)/shard_map/ppermute | solution.py:34
  104.3 6.3 %collective-permute-start.7 = (f32[160,256]{1,0:T(8,128)S(1)}, f32[160,256]{1,0:T(8,128)S(1)}, u32[]{:S(2)}, u32[]{:S(2)}) collective-permute-start(f32[160,256]{1,0:T(8,128)S(1)} %reshape.24.refs_0_), channel_id=1, source_target_pairs={{0,8},{8,16},{16,24},{24,0},{1,9},{9,17},{17,25},{25,1},{2,10},{10... | collective-permute-start | bytes 491528 | tf_op jit(solution)/shard_map/ppermute | solution.py:34
  114.0 2.3 collective-permute-start.10
  128.3 16.1 %collective-permute-start.14 = (f32[640,1280]{1,0:T(8,128)}, f32[640,1280]{1,0:T(8,128)S(1)}, u32[]{:S(2)}, u32[]{:S(2)}) collective-permute-start(f32[640,1280]{1,0:T(8,128)} %get-tuple-element.42), channel_id=1, source_target_pairs={{0,4},{4,0},{1,5},{5,1},{2,6},{6,2},{3,7},{7,3},{8,12},{12,8},{9,1... | collective-permute-start | bytes 9830408 | tf_op jit(solution)/shard_map/ppermute | solution.py:38
  128.4 8.2 %collective-permute-start.13 = (f32[208,256]{1,0:T(8,128)S(1)}, f32[208,256]{1,0:T(8,128)}, u32[]{:S(2)}, u32[]{:S(2)}) collective-permute-start(f32[208,256]{1,0:T(8,128)S(1)} %copy-done.3), channel_id=1, source_target_pairs={{0,3},{1,0},{2,1},{3,2},{4,7},{5,4},{6,5},{7,6},{8,11},{9,8},{10,9... | collective-permute-start | bytes 638984 | tf_op jit(solution)/shard_map/ppermute | solution.py:34
  129.0 9.8 %collective-permute-start.12 = (f32[208,256]{1,0:T(8,128)S(1)}, f32[208,256]{1,0:T(8,128)}, u32[]{:S(2)}, u32[]{:S(2)}) collective-permute-start(f32[208,256]{1,0:T(8,128)S(1)} %copy-done.3), channel_id=1, source_target_pairs={{0,2},{1,3},{2,0},{3,1},{4,6},{5,7},{6,4},{7,5},{8,10},{9,11},{10,... | collective-permute-start | bytes 638984 | tf_op jit(solution)/shard_map/ppermute | solution.py:34
  129.6 12.9 %collective-permute-start.11 = (f32[208,256]{1,0:T(8,128)S(1)}, f32[208,256]{1,0:T(8,128)}, u32[]{:S(2)}, u32[]{:S(2)}) collective-permute-start(f32[208,256]{1,0:T(8,128)S(1)} %copy-done.3), channel_id=1, source_target_pairs={{0,1},{1,2},{2,3},{3,0},{4,5},{5,6},{6,7},{7,4},{8,9},{9,10},{10,1... | collective-permute-start | bytes 638984 | tf_op jit(solution)/shard_map/ppermute | solution.py:34
  153.9 11.3 %collective-permute-start.21 = (f32[256,256]{1,0:T(8,128)S(1)}, f32[256,256]{1,0:T(8,128)S(1)}, u32[]{:S(2)}, u32[]{:S(2)}) collective-permute-start(f32[256,256]{1,0:T(8,128)S(1)} %copy-done.2), channel_id=1, source_target_pairs={{0,3},{1,0},{2,1},{3,2},{4,7},{5,4},{6,5},{7,6},{8,11},{9,8},{10,9... | collective-permute-start | bytes 786440 | tf_op jit(solution)/shard_map/ppermute | solution.py:34
  154.8 11.6 %collective-permute-start.20 = (f32[256,256]{1,0:T(8,128)S(1)}, f32[256,256]{1,0:T(8,128)S(1)}, u32[]{:S(2)}, u32[]{:S(2)}) collective-permute-start(f32[256,256]{1,0:T(8,128)S(1)} %copy-done.2), channel_id=1, source_target_pairs={{0,2},{1,3},{2,0},{3,1},{4,6},{5,7},{6,4},{7,5},{8,10},{9,11},{10,... | collective-permute-start | bytes 786440 | tf_op jit(solution)/shard_map/ppermute | solution.py:34
  155.1 15.2 %collective-permute-start.19 = (f32[256,256]{1,0:T(8,128)S(1)}, f32[256,256]{1,0:T(8,128)S(1)}, u32[]{:S(2)}, u32[]{:S(2)}) collective-permute-start(f32[256,256]{1,0:T(8,128)S(1)} %copy-done.2), channel_id=1, source_target_pairs={{0,1},{1,2},{2,3},{3,0},{4,5},{5,6},{6,7},{7,4},{8,9},{9,10},{10,1... | collective-permute-start | bytes 786440 | tf_op jit(solution)/shard_map/ppermute | solution.py:34
  159.9 11.2 %collective-permute-start.16 = (f32[160,256]{1,0:T(8,128)}, f32[160,256]{1,0:T(8,128)S(1)}, u32[]{:S(2)}, u32[]{:S(2)}) collective-permute-start(f32[160,256]{1,0:T(8,128)} %get-tuple-element.47), channel_id=1, source_target_pairs={{0,8},{8,16},{16,24},{24,0},{1,9},{9,17},{17,25},{25,1},{2,10},{10... | collective-permute-start | bytes 491528 | tf_op jit(solution)/shard_map/ppermute | solution.py:34
  161.5 9.6 %collective-permute-start.17 = (f32[160,256]{1,0:T(8,128)}, f32[160,256]{1,0:T(8,128)S(1)}, u32[]{:S(2)}, u32[]{:S(2)}) collective-permute-start(f32[160,256]{1,0:T(8,128)} %get-tuple-element.48), channel_id=1, source_target_pairs={{0,16},{8,24},{16,0},{24,8},{1,17},{9,25},{17,1},{25,9},{2,18},{10... | collective-permute-start | bytes 491528 | tf_op jit(solution)/shard_map/ppermute | solution.py:34
  165.2 7.9 %collective-permute-start.18 = (f32[160,256]{1,0:T(8,128)}, f32[160,256]{1,0:T(8,128)S(1)}, u32[]{:S(2)}, u32[]{:S(2)}) collective-permute-start(f32[160,256]{1,0:T(8,128)} %get-tuple-element.49), channel_id=1, source_target_pairs={{0,24},{8,0},{16,8},{24,16},{1,25},{9,1},{17,9},{25,17},{2,26},{10... | collective-permute-start | bytes 491528 | tf_op jit(solution)/shard_map/ppermute | solution.py:34
  174.8 22.0 %all-to-all-start.3 = ((f32[8,20,256]{2,1,0:T(8,128)}), f32[8,20,256]{2,1,0:T(8,128)S(1)}, u32[]{:S(2)}, u32[]{:S(2)}) async-start(f32[8,20,256]{2,1,0:T(8,128)} %reshape.26), calls=%async_computation.4 | async-start | bytes 393216 | tf_op jit(solution)/shard_map/all_to_all | solution.py:304
  214.3 6.6 %collective-permute-start.24 = (f32[160,256]{1,0:T(8,128)S(1)}, f32[160,256]{1,0:T(8,128)S(1)}, u32[]{:S(2)}, u32[]{:S(2)}) collective-permute-start(f32[160,256]{1,0:T(8,128)S(1)} %reshape.27.refs_0_), channel_id=1, source_target_pairs={{0,24},{8,0},{16,8},{24,16},{1,25},{9,1},{17,9},{25,17},{2,26},{10... | collective-permute-start | bytes 491528 | tf_op jit(solution)/shard_map/ppermute | solution.py:34
  215.6 7.1 %collective-permute-start.23 = (f32[160,256]{1,0:T(8,128)S(1)}, f32[160,256]{1,0:T(8,128)S(1)}, u32[]{:S(2)}, u32[]{:S(2)}) collective-permute-start(f32[160,256]{1,0:T(8,128)S(1)} %reshape.27.refs_0_), channel_id=1, source_target_pairs={{0,16},{8,24},{16,0},{24,8},{1,17},{9,25},{17,1},{25,9},{2,18},{10... | collective-permute-start | bytes 491528 | tf_op jit(solution)/shard_map/ppermute | solution.py:34
  217.2 6.7 %collective-permute-start.22 = (f32[160,256]{1,0:T(8,128)S(1)}, f32[160,256]{1,0:T(8,128)S(1)}, u32[]{:S(2)}, u32[]{:S(2)}) collective-permute-start(f32[160,256]{1,0:T(8,128)S(1)} %reshape.27.refs_0_), channel_id=1, source_target_pairs={{0,8},{8,16},{16,24},{24,0},{1,9},{9,17},{17,25},{25,1},{2,10},{10... | collective-permute-start | bytes 491528 | tf_op jit(solution)/shard_map/ppermute | solution.py:34
  227.3 18.6 %collective-permute-start.25 = (f32[640,256]{1,0:T(8,128)}, f32[640,256]{1,0:T(8,128)S(1)}, u32[]{:S(2)}, u32[]{:S(2)}) collective-permute-start(f32[640,256]{1,0:T(8,128)} %shard_map.79.near), channel_id=1, source_target_pairs={{0,4},{4,0},{1,5},{5,1},{2,6},{6,2},{3,7},{7,3},{8,12},{12,8},{9,1... | collective-permute-start | bytes 1966088 | tf_op jit(solution)/shard_map/ppermute | solution.py:38
  251.9 6.4 %collective-permute-start.28 = (f32[8,256]{1,0:T(8,128)}, f32[8,256]{1,0:T(8,128)S(1)}, u32[]{:S(2)}, u32[]{:S(2)}) collective-permute-start(f32[8,256]{1,0:T(8,128)} %get-tuple-element.58), channel_id=1, source_target_pairs={{0,3},{1,0},{2,1},{3,2},{4,7},{5,4},{6,5},{7,6},{8,11},{9,8},{10,9... | collective-permute-start | bytes 24584 | tf_op jit(solution)/shard_map/ppermute | solution.py:34
  253.8 5.4 %collective-permute-start.27 = (f32[8,256]{1,0:T(8,128)}, f32[8,256]{1,0:T(8,128)S(1)}, u32[]{:S(2)}, u32[]{:S(2)}) collective-permute-start(f32[8,256]{1,0:T(8,128)} %get-tuple-element.58), channel_id=1, source_target_pairs={{0,2},{1,3},{2,0},{3,1},{4,6},{5,7},{6,4},{7,5},{8,10},{9,11},{10,... | collective-permute-start | bytes 24584 | tf_op jit(solution)/shard_map/ppermute | solution.py:34
  255.2 5.1 %collective-permute-start.26 = (f32[8,256]{1,0:T(8,128)}, f32[8,256]{1,0:T(8,128)S(1)}, u32[]{:S(2)}, u32[]{:S(2)}) collective-permute-start(f32[8,256]{1,0:T(8,128)} %get-tuple-element.58), channel_id=1, source_target_pairs={{0,1},{1,2},{2,3},{3,0},{4,5},{5,6},{6,7},{7,4},{8,9},{9,10},{10,1... | collective-permute-start | bytes 24584 | tf_op jit(solution)/shard_map/ppermute | solution.py:34
  (17 other events, 71.9 us)
Sparse Core Ops, SparseCore 0:
  9.8 39.7 all-gather.3
  51.4 38.6 all-gather.5
  148.4 46.1 reduce-scatter.1

commit v2 on v1

v2 whole, which is shorter than its diff:
```python
import math

import jax
import jax.numpy as jnp
from jax import lax
from jax.experimental import pallas as pl
from jax.experimental.pallas import tpu as pltpu
from jax.sharding import Mesh
from jax.sharding import PartitionSpec as P

D = 5120
R = 256
NZ, NX, NC, NY = 8, 4, 2, 4
FSDP = ("z", "x", "c")
TOKENS = 128
ROWS = D // (NZ * NX * NC)
COLS = D // NY
HALF = COLS // NC
PAIR = NZ // NY
EDGE = 64
BLOCKS = R // EDGE
F32 = jnp.float32

momentum_decay = 0.95


def shape(*dims):
    return jax.ShapeDtypeStruct(dims, F32)


def shifted(v, axis, n, k):
    return lax.ppermute(v, axis, [(i, (i + k) % n) for i in range(n)])


def other_core(v):
    return lax.ppermute(v, "c", [(0, 1), (1, 0)])


def over_tp(v):
    total = v
    for k in range(1, NY):
        total = total + shifted(v, "tp", NY, k)
    return total


def plain(a, b, dims):
    return lax.dot_general(a, b, (dims, ((), ())), preferred_element_type=F32)


def full(a, b, dims):
    return lax.dot_general(
        a, b, (dims, ((), ())), precision=lax.Precision.HIGHEST, preferred_element_type=F32
    )


def near_dot(a, b, dims):
    return lax.dot_general(
        a, b, (dims, ((), ())), precision=lax.Precision.HIGH, preferred_element_type=F32
    )


def call(kernel, scalars, out_shape, in_specs, *args, out_specs=None, grid=(1,), scratch=()):
    if out_specs is None:
        leaves = out_shape if isinstance(out_shape, tuple) else (out_shape,)
        specs = tuple(whole(s.shape) for s in leaves)
        out_specs = specs if isinstance(out_shape, tuple) else specs[0]
    return pl.pallas_call(
        kernel,
        out_shape=out_shape,
        grid_spec=pltpu.PrefetchScalarGridSpec(
            num_scalar_prefetch=1,
            grid=grid,
            in_specs=in_specs,
            out_specs=out_specs,
            scratch_shapes=scratch,
        ),
    )(scalars, *args)


def whole(dims):
    zeros = (0,) * len(dims)
    return pl.BlockSpec(tuple(dims), lambda i, at: zeros)


C, T = range(2)


def turn_kernel(at, outs, out):
    out[...] = outs[...].astype(F32).T.reshape(NX, 1, NC * ROWS, TOKENS)


def eliminate(first_block, count, work_ref, out_ref):
    rows = lax.broadcasted_iota(jnp.int32, (EDGE, 2 * EDGE), 0)
    lanes = lax.broadcasted_iota(jnp.int32, (EDGE, 2 * EDGE), 1)
    eye = (rows + EDGE == lanes).astype(F32)
    rest_lanes = lax.broadcasted_iota(jnp.int32, (EDGE, R), 1)

    def step(i, _):
        here = pl.ds(pl.multiple_of(i * EDGE, EDGE), EDGE)
        state = jnp.where(lanes < EDGE, work_ref[here, : 2 * EDGE], eye)
        pivots = jnp.zeros((EDGE, 2 * EDGE), F32)
        for k in range(EDGE):
            column = jnp.broadcast_to(state[:, k : k + 1], (EDGE, 2 * EDGE))
            pivot = column[k : k + 1, :]
            line = state[k : k + 1, :] / pivot
            pivots = jnp.where(rows == k, jnp.broadcast_to(pivot, rows.shape), pivots)
            if k < EDGE - 1:
                state = state - jnp.where(rows > k, column, 0.0) * line
        inverse = (state * lax.rsqrt(pivots))[:, EDGE:]
        upper = full(inverse, work_ref[here, :], ((1,), (0,)))
        out_ref[here, :] = pltpu.roll(upper, i * EDGE, 1)[:, R:]
        rest = jnp.where(rest_lanes < (BLOCKS - i) * EDGE, upper[:, :R], 0.0)
        change = full(rest, upper, ((0,), (0,)))
        for r in range(1, BLOCKS):
            there = pl.ds(pl.multiple_of(((i + r) % BLOCKS) * EDGE, EDGE), EDGE)
            left = work_ref[there, :] - change[r * EDGE : (r + 1) * EDGE, :]
            work_ref[there, :] = pltpu.roll(left, 2 * R - EDGE, 1)
        return 0

    lax.fori_loop(first_block, first_block + count, step, 0)


def early_kernel(at, gram, work, out):
    all_rows = lax.broadcasted_iota(jnp.int32, (R, R), 0)
    all_lanes = lax.broadcasted_iota(jnp.int32, (R, R), 1)
    work[:, :R] = gram[...]
    work[:, R:] = (all_rows == all_lanes).astype(F32)
    out[...] = jnp.zeros((R, R), F32)
    eliminate(0, BLOCKS // 2, work, out)


def late_kernel(at, work, done, out, held):
    held[...] = work[...]
    out[...] = done[...]
    eliminate(BLOCKS // 2, BLOCKS // 2, held, out)


def product_kernel(at, outs, acts, kept, given, joined):
    @pl.when(pl.program_id(0) == 0)
    def _():
        joined[...] = acts[...].astype(jnp.bfloat16)

    lhs = jnp.concatenate([outs[0, k].astype(jnp.bfloat16) for k in range(NX)], axis=1)
    total = plain(lhs, joined[...], ((1,), (0,)))
    first = at[C] == 0
    for i in range(PAIR):
        near = total[NC * i * ROWS : (NC * i + 1) * ROWS]
        far = total[(NC * i + 1) * ROWS : (NC * i + 2) * ROWS]
        kept[i * ROWS : (i + 1) * ROWS, :] = jnp.where(first, near, far)
        given[i * ROWS : (i + 1) * ROWS, :] = jnp.where(first, far, near)


def core_products(at, outs, acts):
    half = shape(NZ * ROWS, COLS)
    half_spec = pl.BlockSpec((PAIR * ROWS, COLS), lambda i, at: (i, 0))
    outs_spec = pl.BlockSpec((1, NX, PAIR * NC * ROWS, TOKENS), lambda i, at: (i, 0, 0, 0))
    return call(
        product_kernel, at, (half, half), [outs_spec, whole(acts.shape)],
        outs, acts, out_specs=(half_spec, half_spec), grid=(NY,),
        scratch=[pltpu.VMEM(acts.shape, jnp.bfloat16)],
    )


def summed_piece(kept, given):
    pieces = (kept + other_core(given)).reshape(NX * NZ, HALF // (NX * NZ), R)
    arrived = lax.all_to_all(pieces, ("x", "z"), 0, 0, tiled=True)
    return jnp.sum(arrived, axis=0)


def spread_over(v, axis, n):
    copies = jnp.broadcast_to(v[None], (n, *v.shape))
    return lax.all_to_all(copies, axis, 0, 0, tiled=True).reshape(-1, v.shape[1])


def gathered(piece):
    part = spread_over(piece, "z", NZ)
    near = spread_over(part, "x", NX)
    return near, other_core(near)


def on_device(activations, out_grad, momentum, right_prev):
    z, x, c = lax.axis_index("z"), lax.axis_index("x"), lax.axis_index("c")
    t = lax.axis_index("tp")
    mine = (z * NX + x) * NC + c
    at = jnp.stack([c, t]).astype(jnp.int32)

    held = jnp.concatenate([activations.astype(F32), momentum])
    first = near_dot(held, right_prev, ((1,), (0,)))
    first, activations, out_grad = lax.optimization_barrier((first, activations, out_grad))
    first = over_tp(first)

    acts = lax.all_gather(activations.astype(F32), "x", axis=0, tiled=True)
    turned = call(
        turn_kernel, at, shape(NX, PAIR, NC * ROWS, TOKENS),
        [pl.BlockSpec((TOKENS, D // NZ), lambda i, at: (0, PAIR * at[T] + i))], out_grad,
        out_specs=pl.BlockSpec((NX, 1, NC * ROWS, TOKENS), lambda i, at: (0, i, 0, 0)),
        grid=(PAIR,),
    )
    turned = turned.reshape(NX, PAIR * NC * ROWS, TOKENS)
    outs = lax.all_to_all(turned, "x", 0, 0, tiled=True)
    outs = lax.all_gather(outs, "tp", axis=0, tiled=False)

    helds, spreads = [], []
    for half in (c, 1 - c):
        helds.append(lax.dynamic_slice_in_dim(held, half * HALF, HALF, 1))
        start = t * COLS + half * HALF
        place = lax.broadcasted_iota(jnp.int32, (ROWS, HALF), 0) + (mine * ROWS - start)
        place = place == lax.broadcasted_iota(jnp.int32, (ROWS, HALF), 1)
        part = lax.dynamic_slice_in_dim(out_grad, start, HALF, 1)
        spreads.append(jnp.concatenate([part.astype(F32), place.astype(F32)]))

    given = near_dot(spreads[1], first, ((0,), (0,)))
    kept = near_dot(spreads[0], first, ((0,), (0,)))
    piece = summed_piece(kept, given)
    near, far = gathered(piece)
    seen = near_dot(spreads[0], near, ((1,), (0,))) + near_dot(spreads[1], far, ((1,), (0,)))
    second = over_tp(seen)

    gram = full(near, near, ((0,), (0,))) + full(far, far, ((0,), (0,)))
    gram, second = lax.optimization_barrier((gram, second))
    gram = over_tp(gram)

    given = near_dot(helds[1], second, ((0,), (0,)))
    kept = near_dot(helds[0], second, ((0,), (0,)))
    given, at_right = lax.optimization_barrier((given, at))
    piece = summed_piece(kept, given)
    kept_grad, given_grad = core_products(at_right, outs, acts)
    summed_grad = kept_grad + other_core(given_grad)
    grad = lax.psum_scatter(summed_grad, "z", scatter_dimension=0, tiled=True)
    work, done = call(early_kernel, at, (shape(R, 2 * R), shape(R, R)), [whole((R, R))], gram)
    near, far = gathered(piece)
    inverse = call(
        late_kernel, at, shape(R, R), [whole((R, 2 * R)), whole((R, R))], work, done,
        scratch=[pltpu.VMEM((R, 2 * R), F32)],
    )
    basis = near_dot(second[TOKENS:], inverse, ((1,), (1,)))
    rights = [near_dot(v, inverse, ((1,), (1,))) for v in (near, far)]
    squares = sum(jnp.sum(v * v, axis=0) for v in rights)
    squares = over_tp(jnp.broadcast_to(squares[None], (8, R)))[:1]
    factor = lax.rsqrt(squares / D + 1e-06)

    def in_order(pair, axis):
        return jnp.concatenate(
            [jnp.where(c == 0, pair[0], pair[1]), jnp.where(c == 0, pair[1], pair[0])], axis=axis
        )

    change = in_order([near_dot(basis, v, ((1,), (1,))) for v in rights], 1)
    update = in_order([near_dot(basis * factor, v, ((1,), (1,))) for v in rights], 1)
    new_momentum = (momentum + grad) - (1.0 - momentum_decay) * change
    own = R // (NZ * NX * NC)
    owned = in_order([lax.dynamic_slice_in_dim(v, mine * own, own, 1) for v in rights], 0)
    owned = owned * lax.dynamic_slice_in_dim(factor, mine * own, own, 1)
    return (new_momentum, math.sqrt(D / R) * update, owned)


def solution(mesh):
    finer = Mesh(mesh.devices.reshape(NZ, NX, NC, mesh.shape["tp"]), ("z", "x", "c", "tp"))
    in_specs = (P(FSDP, "tp"), P(FSDP, None), P(FSDP, "tp"), P("tp", None))
    out_specs = (P(FSDP, "tp"), P(FSDP, "tp"), P("tp", FSDP))
    return jax.shard_map(
        on_device, mesh=finer, in_specs=in_specs, out_specs=out_specs, check_vma=False
    )
```

time: 280 us -> 285 us (1.018)
  Pallas kernels: 90.9 us -> 41.1 us
  blocking collectives: 62.8 us -> 109 us
  starting transfers between devices: 38.5 us -> 21.4 us
  matrix products: 1.99 us -> 18.5 us
  waiting for transfers between devices: 45.3 us -> 60.9 us
    pallas_call x15 -> x4, Pallas kernels: 90.9 us -> 41.1 us  [call(): pl.pallas_call(kernel, out_shape=out_shape, grid_spec=pltpu.PrefetchScala...]
    all_to_all x4 -> x5, blocking collectives: 62.8 us -> 109 us  [the longest x2 65.3 us: summed_piece(): arrived = lax.all_to_all(pieces, ('x', 'z'), 0, 0, tiled=True)]
    all_to_all x1 -> x2, waiting for transfers between devices: 0.01 us -> 23.4 us  [the longest x1 17.6 us: on_device(): outs = lax.all_to_all(turned, 'x', 0, 0, tiled=True)]
    ppermute x24 -> x12, starting transfers between devices: 34.9 us -> 11.7 us  [shifted(): return lax.ppermute(v, axis, [(i, (i + k) % n) for i in range(n)])]
    dot_general x1 -> x16, matrix products: 1.99 us -> 18.5 us  [the longest x14 15.3 us: near_dot(): lax.dot_general(a, b, (dims, ((), ())), precision=lax.Precision.HIGH, pre...]
    ppermute x24 -> x12, waiting for transfers between devices: 40.4 us -> 28.9 us  [shifted(): return lax.ppermute(v, axis, [(i, (i + k) % n) for i in range(n)])]
    all_to_all x1 -> x2, starting transfers between devices: 3.39 us -> 9.37 us  [the longest x1 4.83 us: on_device(): outs = lax.all_to_all(turned, 'x', 0, 0, tiled=True)]
    unnamed x33 -> x28, local copies, waits for them, and re-layouts: 5.59 us -> 1.14 us
  transfers between devices with their start and end apart: 33 -> 22, of which waited for: 22 -> 16; matrix products, arithmetic and copies ran while one was open for 5% -> 9% of each run, Pallas kernels for 30% -> 12%
where the time goes in v2:
time: 285 us; the launch traced here: 284 us
  blocking collectives  109 us (38%)
  waiting for transfers between devices  60.9 us (21%)
  Pallas kernels  41.1 us (14%)
  starting transfers between devices  21.4 us (8%)
  matrix products  18.5 us (6%)
  other arithmetic  14.2 us (5%)
  between operations  14.1 us (5%)
  local copies, waits for them, and re-layouts  4.32 us (2%)
    all_to_all x2, blocking collectives, summed_piece(): arrived = lax.all_to_all(pieces, ('x', 'z'), 0, 0, tiled=True)  65.3 us
    all_to_all x3, blocking collectives, spread_over(): lax.all_to_all(copies, axis, 0, 0, tiled=True).reshape(-1, v.shape[1])  44.1 us
    pallas_call x4, Pallas kernels, call(): pl.pallas_call(kernel, out_shape=out_shape, grid_spec=pltpu.PrefetchScala...  41.1 us
    ppermute x12, waiting for transfers between devices, shifted(): return lax.ppermute(v, axis, [(i, (i + k) % n) for i in range(n)])  28.9 us
    all_to_all x1, waiting for transfers between devices, on_device(): outs = lax.all_to_all(turned, 'x', 0, 0, tiled=True)  17.6 us
    dot_general x14, matrix products, near_dot(): lax.dot_general(a, b, (dims, ((), ())), precision=lax.Precision.HIGH, pre...  15.3 us
    ppermute x12, starting transfers between devices, shifted(): return lax.ppermute(v, axis, [(i, (i + k) % n) for i in range(n)])  11.7 us
    ppermute x5, waiting for transfers between devices, other_core(): return lax.ppermute(v, 'c', [(0, 1), (1, 0)])  8.5 us
  transfers between devices with their start and end apart: 22, of which 16 were waited for; matrix products, arithmetic and copies ran while one was open for 9% of the time, Pallas kernels for 12%

profile of v2, /device:TPU:2, one launch (start us, length us, event | category | flops | bytes accessed | tf_op | source)
XLA Modules:
  0.0 284.0 jit_solution(5033482314270707317)
XLA Ops:
  8.6 1.7 fusion
  11.2 3.1 %collective-permute-start.2 = (f32[208,256]{1,0:T(8,128)S(1)}, f32[208,256]{1,0:T(8,128)S(1)}, u32[]{:S(2)}, u32[]{:S(2)}) collective-permute-start(f32[208,256]{1,0:T(8,128)S(1)} %fusion), channel_id=1, source_target_pairs={{0,3},{1,0},{2,1},{3,2},{4,7},{5,4},{6,5},{7,6},{8,11},{9,8},{10,9... | collective-permute-start | bytes 638984 | tf_op jit(solution)/shard_map/ppermute | solution.py:32
  17.1 6.3 %collective-permute-done.2 = f32[208,256]{1,0:T(8,128)S(1)} collective-permute-done((f32[208,256]{1,0:T(8,128)S(1)}, f32[208,256]{1,0:T(8,128)S(1)}, u32[]{:S(2)}, u32[]{:S(2)}) %collective-permute-start.2) | collective-permute-done | bytes 213024 | tf_op jit(solution)/shard_map/ppermute | solution.py:32
  24.0 3.2 %collective-permute-done = f32[208,256]{1,0:T(8,128)} collective-permute-done((f32[208,256]{1,0:T(8,128)S(1)}, f32[208,256]{1,0:T(8,128)}, u32[]{:S(2)}, u32[]{:S(2)}) %collective-permute-start) | collective-permute-done | bytes 213024 | tf_op jit(solution)/shard_map/ppermute | solution.py:32
  30.4 2.6 shard_map.67
  33.0 4.8 %all-to-all-start.3 = ((f32[4,320,128]{2,1,0:T(8,128)}), f32[4,320,128]{2,1,0:T(8,128)S(1)}, u32[]{:S(2)}, u32[]{:S(2)}) async-start(f32[4,320,128]{2,1,0:T(8,128)} %bitcast.37), calls=%async_computation.3 | async-start | bytes 1310720 | tf_op jit(solution)/shard_map/all_to_all | solution.py:200
  38.0 17.6 %all-to-all-done.3 = f32[4,320,128]{2,1,0:T(8,128)S(1)} async-done(((f32[4,320,128]{2,1,0:T(8,128)}), f32[4,320,128]{2,1,0:T(8,128)S(1)}, u32[]{:S(2)}, u32[]{:S(2)}) %all-to-all-start.3) | async-done | bytes 655392 | tf_op jit(solution)/shard_map/all_to_all | solution.py:200
  56.5 2.7 convolution_add_fusion.1
  60.3 31.0 %all_to_all.35 = f32[32,20,256]{2,1,0:T(8,128)S(1)} all-to-all(f32[32,20,256]{2,1,0:T(8,128)S(1)} %reshape.30), channel_id=1, replica_groups=mesh['z'=8,'x'=4,'c'=2,'tp'=4] {'x','z'}, dimensions={0} | all-to-all | bytes 1310720 | tf_op jit(solution)/shard_map/all_to_all | solution.py:166
  91.4 14.3 %all_to_all.36 = f32[8,20,256]{2,1,0:T(8,128)S(1)} all-to-all(f32[8,20,256]{2,1,0:T(8,128)S(1)} %broadcast_in_dim.14), channel_id=1, replica_groups=mesh['z'=8,'x'=4,'c'=2,'tp'=4] {'z'}, dimensions={0} | all-to-all | bytes 327680 | tf_op jit(solution)/shard_map/all_to_all | solution.py:172
  105.8 11.5 %all_to_all.37 = f32[4,160,256]{2,1,0:T(8,128)S(1)} all-to-all(f32[4,160,256]{2,1,0:T(8,128)S(1)} %broadcast_in_dim.16), channel_id=1, replica_groups=mesh['z'=8,'x'=4,'c'=2,'tp'=4] {'x'}, dimensions={0} | all-to-all | bytes 1310720 | tf_op jit(solution)/shard_map/all_to_all | solution.py:172
  122.0 1.9 convolution_add_fusion.2
  124.0 4.1 %collective-permute-done.7 = f32[208,256]{1,0:T(8,128)S(1)} collective-permute-done((f32[208,256]{1,0:T(8,128)S(1)}, f32[208,256]{1,0:T(8,128)S(1)}, u32[]{:S(2)}, u32[]{:S(2)}) %collective-permute-start.7) | collective-permute-done | bytes 213024 | tf_op jit(solution)/shard_map/ppermute | solution.py:32
  128.1 2.2 collective-permute-done.6
  130.3 3.4 %collective-permute-done.5 = f32[208,256]{1,0:T(8,128)S(1)} collective-permute-done((f32[208,256]{1,0:T(8,128)S(1)}, f32[208,256]{1,0:T(8,128)S(1)}, u32[]{:S(2)}, u32[]{:S(2)}) %collective-permute-start.5) | collective-permute-done | bytes 213024 | tf_op jit(solution)/shard_map/ppermute | solution.py:32
  134.6 7.7 %shard_map.68 = (f32[640,1280]{1,0:T(8,128)}, f32[640,1280]{1,0:T(8,128)}) custom-call(s32[2]{0:T(128)} %pad_add_fusion.at, f32[4,4,320,128]{3,2,1,0:T(8,128)} %bitcast.38, f32[512,1280]{1,0:T(8,128)} %all-gather.4.cloned.1.call-done.acts), custom_call_target="tpu_custom_call" | custom-call | tf_op jit(solution)/shard_map/pallas_call | solution.py:67
  142.3 6.0 %collective-permute-done.8 = f32[640,1280]{1,0:T(8,128)S(1)} collective-permute-done((f32[640,1280]{1,0:T(8,128)}, f32[640,1280]{1,0:T(8,128)S(1)}, u32[]{:S(2)}, u32[]{:S(2)}) %collective-permute-start.8) | collective-permute-done | bytes 3276832 | tf_op jit(solution)/shard_map/ppermute | solution.py:36
  148.3 4.0 %add.132 = f32[640,1280]{1,0:T(8,128)} add(f32[640,1280]{1,0:T(8,128)} %get-tuple-element.19, f32[640,1280]{1,0:T(8,128)S(1)} %collective-permute-done.8) | non-fusion elementwise | flops 819200 | bytes 9830400 | tf_op jit(solution)/shard_map/add | solution.py:228
  152.6 2.1 collective-permute-done.12
  154.7 1.9 convolution_add_fusion
  157.5 34.3 %all_to_all.38 = f32[32,20,256]{2,1,0:T(8,128)S(1)} all-to-all(f32[32,20,256]{2,1,0:T(8,128)} %reshape.33), channel_id=1, replica_groups=mesh['z'=8,'x'=4,'c'=2,'tp'=4] {'x','z'}, dimensions={0} | all-to-all | bytes 1310720 | tf_op jit(solution)/shard_map/all_to_all | solution.py:166
  191.9 18.3 %all_to_all.39 = f32[8,20,256]{2,1,0:T(8,128)S(1)} all-to-all(f32[8,20,256]{2,1,0:T(8,128)S(1)} %broadcast_in_dim.17), channel_id=1, replica_groups=mesh['z'=8,'x'=4,'c'=2,'tp'=4] {'z'}, dimensions={0} | all-to-all | bytes 327680 | tf_op jit(solution)/shard_map/all_to_all | solution.py:172
  211.1 4.5 %all-to-all-start.6 = ((f32[4,160,256]{2,1,0:T(8,128)}), f32[4,160,256]{2,1,0:T(8,128)S(1)}, u32[]{:S(2)}, u32[]{:S(2)}) async-start(f32[4,160,256]{2,1,0:T(8,128)} %broadcast_in_dim.37), calls=%async_computation.7 | async-start | bytes 1310720 | tf_op jit(solution)/shard_map/all_to_all | solution.py:172
  217.7 5.8 %all-to-all-done.6 = f32[4,160,256]{2,1,0:T(8,128)S(1)} async-done(((f32[4,160,256]{2,1,0:T(8,128)}), f32[4,160,256]{2,1,0:T(8,128)S(1)}, u32[]{:S(2)}, u32[]{:S(2)}) %all-to-all-start.6) | async-done | bytes 655392 | tf_op jit(solution)/shard_map/all_to_all | solution.py:172
  224.5 2.1 collective-permute-done.10
  226.6 2.8 collective-permute-done.9
  229.4 1.8 add_add_fusion.gram
  231.2 15.4 %shard_map.69 = (f32[256,512]{1,0:T(8,128)}, f32[256,256]{1,0:T(8,128)}) custom-call(s32[2]{0:T(128)} %pad_add_fusion.at, f32[256,256]{1,0:T(8,128)} %add_add_fusion.gram), custom_call_target="tpu_custom_call" | custom-call | tf_op jit(solution)/shard_map/pallas_call | solution.py:67
  246.6 15.4 %shard_map.70 = f32[256,256]{1,0:T(8,128)} custom-call(s32[2]{0:T(128)} %pad_add_fusion.at, f32[256,512]{1,0:T(8,128)} %get-tuple-element.22.work, f32[256,256]{1,0:T(8,128)} %get-tuple-element.23.done), custom_call_target="tpu_custom_call" | custom-call | tf_op jit(solution)/shard_map/pallas_call | solution.py:67
  264.9 1.7 multiply_reduce_fusion
  270.1 1.8 collective-permute-done.15
  275.6 1.8 fusion.8
  (98 shorter events, 31.9 us)
Async XLA Ops:
  7.2 127.4 %all-gather.4.cloned.1.call-start = ((), (), s32[]{:S(2)}) async-start(), calls=%async_computation.8 | async-start | bytes 3276800 | tf_op jit(solution)/shard_map/all_gather | solution.py:192
  11.2 12.2 %collective-permute-start.2 = (f32[208,256]{1,0:T(8,128)S(1)}, f32[208,256]{1,0:T(8,128)S(1)}, u32[]{:S(2)}, u32[]{:S(2)}) collective-permute-start(f32[208,256]{1,0:T(8,128)S(1)} %fusion), channel_id=1, source_target_pairs={{0,3},{1,0},{2,1},{3,2},{4,7},{5,4},{6,5},{7,6},{8,11},{9,8},{10,9... | collective-permute-start | bytes 638984 | tf_op jit(solution)/shard_map/ppermute | solution.py:32
  14.3 9.7 %collective-permute-start.1 = (f32[208,256]{1,0:T(8,128)S(1)}, f32[208,256]{1,0:T(8,128)S(1)}, u32[]{:S(2)}, u32[]{:S(2)}) collective-permute-start(f32[208,256]{1,0:T(8,128)S(1)} %fusion), channel_id=1, source_target_pairs={{0,2},{1,3},{2,0},{3,1},{4,6},{5,7},{6,4},{7,5},{8,10},{9,11},{10,... | collective-permute-start | bytes 638984 | tf_op jit(solution)/shard_map/ppermute | solution.py:32
  14.9 12.3 %collective-permute-start = (f32[208,256]{1,0:T(8,128)S(1)}, f32[208,256]{1,0:T(8,128)}, u32[]{:S(2)}, u32[]{:S(2)}) collective-permute-start(f32[208,256]{1,0:T(8,128)S(1)} %fusion), channel_id=1, source_target_pairs={{0,1},{1,2},{2,3},{3,0},{4,5},{5,6},{6,7},{7,4},{8,9},{9,10},{10,1... | collective-permute-start | bytes 638984 | tf_op jit(solution)/shard_map/ppermute | solution.py:32
  16.9 12.9 %copy-start.5 = (f32[128,640]{1,0:T(8,128)}, f32[128,640]{1,0:T(8,128)S(1)}, u32[]{:S(2)}) copy-start(f32[128,640]{1,0:T(8,128)S(1)} %get-tuple-element.28) | copy-start | bytes 983044
  16.9 39.5 %copy-start.3 = (f32[128,640]{1,0:T(8,128)}, f32[128,640]{1,0:T(8,128)S(1)}, u32[]{:S(2)}) copy-start(f32[128,640]{1,0:T(8,128)S(1)} %get-tuple-element.27) | copy-start | bytes 983044
  17.0 16.0 %copy-start.8 = (f32[80,640]{1,0:T(8,128)}, f32[80,640]{1,0:T(8,128)S(1)}, u32[]{:S(2)}) copy-start(f32[80,640]{1,0:T(8,128)S(1)} %fusion.10) | copy-start | bytes 614404
  29.8 26.6 %collective-permute-start.3 = (f32[640,256]{1,0:T(8,128)}, f32[640,256]{1,0:T(8,128)}, u32[]{:S(2)}, u32[]{:S(2)}) collective-permute-start(f32[640,256]{1,0:T(8,128)} %fusion.6), channel_id=1, source_target_pairs={{0,4},{4,0},{1,5},{5,1},{2,6},{6,2},{3,7},{7,3},{8,12},{12,8},{9,1... | collective-permute-start | bytes 1966088 | tf_op jit(solution)/shard_map/ppermute | solution.py:36
  33.0 22.5 %all-to-all-start.3 = ((f32[4,320,128]{2,1,0:T(8,128)}), f32[4,320,128]{2,1,0:T(8,128)S(1)}, u32[]{:S(2)}, u32[]{:S(2)}) async-start(f32[4,320,128]{2,1,0:T(8,128)} %bitcast.37), calls=%async_computation.3 | async-start | bytes 1310720 | tf_op jit(solution)/shard_map/all_to_all | solution.py:200
  37.8 96.8 %all-gather.6.cloned.1.call-start = ((), (), s32[]{:S(2)}) async-start(), calls=%async_computation.10 | async-start | bytes 3276800 | tf_op jit(solution)/shard_map/all_gather | solution.py:201
  37.9 18.5 %copy-start.10 = (f32[80,640]{1,0:T(8,128)}, f32[80,640]{1,0:T(8,128)S(1)}, u32[]{:S(2)}) copy-start(f32[80,640]{1,0:T(8,128)S(1)} %fusion.9) | copy-start | bytes 614404
  56.4 219.2 %reduce-scatter.2.cloned.1.call-start = ((), (), s32[]{:S(2)}) async-start(), calls=%async_computation.9 | async-start | bytes 3686400 | tf_op jit(solution)/shard_map/reduce_scatter | solution.py:229
  105.8 12.8 %copy-start.11 = (f32[80,640]{1,0:T(8,128)S(1)}, f32[80,640]{1,0:T(8,128)}, u32[]{:S(2)}) copy-start(f32[80,640]{1,0:T(8,128)} %copy-done.10) | copy-start | bytes 614404
  117.3 2.1 collective-permute-start.4
  117.3 2.1 copy-start.6
  117.3 2.1 copy-start.9
  119.9 13.9 %copy-start.1 = (f32[80,1280]{1,0:T(8,128)S(1)}, f32[80,1280]{1,0:T(8,128)}, u32[]{:S(2)}) copy-start(f32[80,1280]{1,0:T(8,128)} %param.6) | copy-start | bytes 1228804
  119.9 8.2 %collective-permute-start.7 = (f32[208,256]{1,0:T(8,128)S(1)}, f32[208,256]{1,0:T(8,128)S(1)}, u32[]{:S(2)}, u32[]{:S(2)}) collective-permute-start(f32[208,256]{1,0:T(8,128)S(1)} %convolution_add_fusion.3), channel_id=1, source_target_pairs={{0,3},{1,0},{2,1},{3,2},{4,7},{5,4},{6,5},{7,6},{8,11},{9,8},{10,9... | collective-permute-start | bytes 638984 | tf_op jit(solution)/shard_map/ppermute | solution.py:32
  120.6 9.7 %collective-permute-start.6 = (f32[208,256]{1,0:T(8,128)S(1)}, f32[208,256]{1,0:T(8,128)S(1)}, u32[]{:S(2)}, u32[]{:S(2)}) collective-permute-start(f32[208,256]{1,0:T(8,128)S(1)} %convolution_add_fusion.3), channel_id=1, source_target_pairs={{0,2},{1,3},{2,0},{3,1},{4,6},{5,7},{6,4},{7,5},{8,10},{9,11},{10,... | collective-permute-start | bytes 638984 | tf_op jit(solution)/shard_map/ppermute | solution.py:32
  121.2 12.5 %collective-permute-start.5 = (f32[208,256]{1,0:T(8,128)S(1)}, f32[208,256]{1,0:T(8,128)S(1)}, u32[]{:S(2)}, u32[]{:S(2)}) collective-permute-start(f32[208,256]{1,0:T(8,128)S(1)} %convolution_add_fusion.3), channel_id=1, source_target_pairs={{0,1},{1,2},{2,3},{3,0},{4,5},{5,6},{6,7},{7,4},{8,9},{9,10},{10,1... | collective-permute-start | bytes 638984 | tf_op jit(solution)/shard_map/ppermute | solution.py:32
  142.3 6.1 %collective-permute-start.8 = (f32[640,1280]{1,0:T(8,128)}, f32[640,1280]{1,0:T(8,128)S(1)}, u32[]{:S(2)}, u32[]{:S(2)}) collective-permute-start(f32[640,1280]{1,0:T(8,128)} %get-tuple-element.20), channel_id=1, source_target_pairs={{0,4},{4,0},{1,5},{5,1},{2,6},{6,2},{3,7},{7,3},{8,12},{12,8},{9,1... | collective-permute-start | bytes 9830408 | tf_op jit(solution)/shard_map/ppermute | solution.py:36
  152.4 2.3 collective-permute-start.12
  210.2 5.5 %copy-start.13 = (f32[256,256]{1,0:T(8,128)S(1)}, f32[256,256]{1,0:T(8,128)}, u32[]{:S(2)}) copy-start(f32[256,256]{1,0:T(8,128)} %convolution_add_fusion.2) | copy-start | bytes 786436
  211.1 12.5 %all-to-all-start.6 = ((f32[4,160,256]{2,1,0:T(8,128)}), f32[4,160,256]{2,1,0:T(8,128)S(1)}, u32[]{:S(2)}, u32[]{:S(2)}) async-start(f32[4,160,256]{2,1,0:T(8,128)} %broadcast_in_dim.37), calls=%async_computation.7 | async-start | bytes 1310720 | tf_op jit(solution)/shard_map/all_to_all | solution.py:172
  215.6 8.8 %collective-permute-start.11 = (f32[256,256]{1,0:T(8,128)S(1)}, f32[256,256]{1,0:T(8,128)S(1)}, u32[]{:S(2)}, u32[]{:S(2)}) collective-permute-start(f32[256,256]{1,0:T(8,128)S(1)} %copy-done.13), channel_id=1, source_target_pairs={{0,3},{1,0},{2,1},{3,2},{4,7},{5,4},{6,5},{7,6},{8,11},{9,8},{10,9... | collective-permute-start | bytes 786440 | tf_op jit(solution)/shard_map/ppermute | solution.py:32
  216.4 10.2 %collective-permute-start.10 = (f32[256,256]{1,0:T(8,128)S(1)}, f32[256,256]{1,0:T(8,128)}, u32[]{:S(2)}, u32[]{:S(2)}) collective-permute-start(f32[256,256]{1,0:T(8,128)S(1)} %copy-done.13), channel_id=1, source_target_pairs={{0,2},{1,3},{2,0},{3,1},{4,6},{5,7},{6,4},{7,5},{8,10},{9,11},{10,... | collective-permute-start | bytes 786440 | tf_op jit(solution)/shard_map/ppermute | solution.py:32
  216.9 12.4 %collective-permute-start.9 = (f32[256,256]{1,0:T(8,128)S(1)}, f32[256,256]{1,0:T(8,128)}, u32[]{:S(2)}, u32[]{:S(2)}) collective-permute-start(f32[256,256]{1,0:T(8,128)S(1)} %copy-done.13), channel_id=1, source_target_pairs={{0,1},{1,2},{2,3},{3,0},{4,5},{5,6},{6,7},{7,4},{8,9},{9,10},{10,1... | collective-permute-start | bytes 786440 | tf_op jit(solution)/shard_map/ppermute | solution.py:32
  223.6 41.3 %collective-permute-start.13 = (f32[640,256]{1,0:T(8,128)S(1)}, f32[640,256]{1,0:T(8,128)}, u32[]{:S(2)}, u32[]{:S(2)}) collective-permute-start(f32[640,256]{1,0:T(8,128)S(1)} %bitcast.35), channel_id=1, source_target_pairs={{0,4},{4,0},{1,5},{5,1},{2,6},{6,2},{3,7},{7,3},{8,12},{12,8},{9,1... | collective-permute-start | bytes 1966088 | tf_op jit(solution)/shard_map/ppermute | solution.py:36
  262.0 2.9 %copy-start.2 = (f32[256,256]{1,0:T(8,128)S(1)}, f32[256,256]{1,0:T(8,128)}, u32[]{:S(2)}) copy-start(f32[256,256]{1,0:T(8,128)} %shard_map.70) | copy-start | bytes 786436
  266.6 5.2 %collective-permute-start.15 = (f32[8,256]{1,0:T(8,128)S(1)}, f32[8,256]{1,0:T(8,128)S(1)}, u32[]{:S(2)}, u32[]{:S(2)}) collective-permute-start(f32[8,256]{1,0:T(8,128)S(1)} %broadcast_in_dim.38), channel_id=1, source_target_pairs={{0,2},{1,3},{2,0},{3,1},{4,6},{5,7},{6,4},{7,5},{8,10},{9,11},{10,... | collective-permute-start | bytes 24584 | tf_op jit(solution)/shard_map/ppermute | solution.py:32
  267.4 4.5 %collective-permute-start.16 = (f32[8,256]{1,0:T(8,128)S(1)}, f32[8,256]{1,0:T(8,128)S(1)}, u32[]{:S(2)}, u32[]{:S(2)}) collective-permute-start(f32[8,256]{1,0:T(8,128)S(1)} %broadcast_in_dim.38), channel_id=1, source_target_pairs={{0,3},{1,0},{2,1},{3,2},{4,7},{5,4},{6,5},{7,6},{8,11},{9,8},{10,9... | collective-permute-start | bytes 24584 | tf_op jit(solution)/shard_map/ppermute | solution.py:32
  268.6 4.9 %collective-permute-start.14 = (f32[8,256]{1,0:T(8,128)S(1)}, f32[8,256]{1,0:T(8,128)S(1)}, u32[]{:S(2)}, u32[]{:S(2)}) collective-permute-start(f32[8,256]{1,0:T(8,128)S(1)} %broadcast_in_dim.38), channel_id=1, source_target_pairs={{0,1},{1,2},{2,3},{3,0},{4,5},{5,6},{6,7},{7,4},{8,9},{9,10},{10,1... | collective-permute-start | bytes 24584 | tf_op jit(solution)/shard_map/ppermute | solution.py:32
  (4 other events, 5.2 us)
Sparse Core Ops, SparseCore 0:
  11.3 46.7 all-gather.3
  59.9 38.6 all-gather.5
  152.5 61.4 reduce-scatter.1

commit v3 on v2

--- a/solution.py
+++ b/solution.py
@@ -17,7 +17,9 @@
 COLS = D // NY
 HALF = COLS // NC
 PAIR = NZ // NY
+STEP = 128
 EDGE = 64
+GROUP = 8
 BLOCKS = R // EDGE
 F32 = jnp.float32
 
@@ -82,31 +84,54 @@
     return pl.BlockSpec(tuple(dims), lambda i, at: zeros)
 
 
-C, T = range(2)
+C, T, X = range(3)
+
+
+def gram_kernel(at, near, far, out):
+    out[...] = jnp.zeros((R, R), F32)
+
+    def step(i, _):
+        here = pl.ds(pl.multiple_of(i * STEP, STEP), STEP)
+        block = jnp.concatenate([near[here, :], far[here, :]], axis=0)
+        out[...] += full(block, block, ((0,), (0,)))
+        return 0
+
+    lax.fori_loop(0, HALF // STEP, step, 0)
 
 
 def turn_kernel(at, outs, out):
     out[...] = outs[...].astype(F32).T.reshape(NX, 1, NC * ROWS, TOKENS)
 
 
-def eliminate(first_block, count, work_ref, out_ref):
+def factor_kernel(at, work_in, done, work_ref, out_ref):
+    work_ref[...] = work_in[...]
+    out_ref[...] = done[...]
     rows = lax.broadcasted_iota(jnp.int32, (EDGE, 2 * EDGE), 0)
     lanes = lax.broadcasted_iota(jnp.int32, (EDGE, 2 * EDGE), 1)
     eye = (rows + EDGE == lanes).astype(F32)
     rest_lanes = lax.broadcasted_iota(jnp.int32, (EDGE, R), 1)
 
-    def step(i, _):
+    def step(j, _):
+        i = at[0] + j
         here = pl.ds(pl.multiple_of(i * EDGE, EDGE), EDGE)
         state = jnp.where(lanes < EDGE, work_ref[here, : 2 * EDGE], eye)
         pivots = jnp.zeros((EDGE, 2 * EDGE), F32)
-        for k in range(EDGE):
-            column = jnp.broadcast_to(state[:, k : k + 1], (EDGE, 2 * EDGE))
-            pivot = column[k : k + 1, :]
-            line = state[k : k + 1, :] / pivot
-            pivots = jnp.where(rows == k, jnp.broadcast_to(pivot, rows.shape), pivots)
-            if k < EDGE - 1:
-                state = state - jnp.where(rows > k, column, 0.0) * line
-        inverse = (state * lax.rsqrt(pivots))[:, EDGE:]
+
+        def group(g, carry):
+            state, pivots = carry
+            live = rows < EDGE - GROUP * g
+            for k in range(GROUP):
+                column = jnp.broadcast_to(state[:, k : k + 1], (EDGE, 2 * EDGE))
+                pivot = column[k : k + 1, :]
+                line = state[k : k + 1, :] / pivot
+                pivots = jnp.where(rows == k, jnp.broadcast_to(pivot, rows.shape), pivots)
+                state = state - jnp.where((rows > k) & live, column, 0.0) * line
+            state = jnp.concatenate([state[GROUP:], state[:GROUP]], axis=0)
+            pivots = jnp.concatenate([pivots[GROUP:], pivots[:GROUP]], axis=0)
+            return pltpu.roll(state, 2 * EDGE - GROUP, 1), pivots
+
+        state, pivots = lax.fori_loop(0, EDGE // GROUP, group, (state, pivots))
+        inverse = (state * lax.rsqrt(pivots))[:, :EDGE]
         upper = full(inverse, work_ref[here, :], ((1,), (0,)))
         out_ref[here, :] = pltpu.roll(upper, i * EDGE, 1)[:, R:]
         rest = jnp.where(rest_lanes < (BLOCKS - i) * EDGE, upper[:, :R], 0.0)
@@ -117,31 +142,33 @@
             work_ref[there, :] = pltpu.roll(left, 2 * R - EDGE, 1)
         return 0
 
-    lax.fori_loop(first_block, first_block + count, step, 0)
-
-
-def early_kernel(at, gram, work, out):
-    all_rows = lax.broadcasted_iota(jnp.int32, (R, R), 0)
-    all_lanes = lax.broadcasted_iota(jnp.int32, (R, R), 1)
-    work[:, :R] = gram[...]
-    work[:, R:] = (all_rows == all_lanes).astype(F32)
-    out[...] = jnp.zeros((R, R), F32)
-    eliminate(0, BLOCKS // 2, work, out)
-
-
-def late_kernel(at, work, done, out, held):
-    held[...] = work[...]
-    out[...] = done[...]
-    eliminate(BLOCKS // 2, BLOCKS // 2, held, out)
-
-
-def product_kernel(at, outs, acts, kept, given, joined):
+    lax.fori_loop(0, BLOCKS // 2, step, 0)
+
+
+def factor_step(first_block, work, done):
+    return call(
+        factor_kernel, jnp.full((1,), first_block, jnp.int32),
+        (shape(R, 2 * R), shape(R, R)), [whole((R, 2 * R)), whole((R, R))], work, done,
+    )
+
+
+def product_kernel(at, *refs):
+    sources, (acts, kept, given, joined, lhs) = refs[:NY], refs[NY:]
+
     @pl.when(pl.program_id(0) == 0)
     def _():
-        joined[...] = acts[...].astype(jnp.bfloat16)
-
-    lhs = jnp.concatenate([outs[0, k].astype(jnp.bfloat16) for k in range(NX)], axis=1)
-    total = plain(lhs, joined[...], ((1,), (0,)))
+        for k in range(NX):
+            here = pl.ds(pl.multiple_of(((at[X] - k) & (NX - 1)) * TOKENS, TOKENS), TOKENS)
+            joined[k * TOKENS : (k + 1) * TOKENS, :] = acts[here, :].astype(jnp.bfloat16)
+
+    for j, source in enumerate(sources):
+
+        @pl.when(((at[T] - pl.program_id(0)) & (NY - 1)) == j)
+        def _():
+            for k in range(NX):
+                lhs[:, k * TOKENS : (k + 1) * TOKENS] = source[k].astype(jnp.bfloat16)
+
+    total = plain(lhs[...], joined[...], ((1,), (0,)))
     first = at[C] == 0
     for i in range(PAIR):
         near = total[NC * i * ROWS : (NC * i + 1) * ROWS]
@@ -153,11 +180,14 @@
 def core_products(at, outs, acts):
     half = shape(NZ * ROWS, COLS)
     half_spec = pl.BlockSpec((PAIR * ROWS, COLS), lambda i, at: (i, 0))
-    outs_spec = pl.BlockSpec((1, NX, PAIR * NC * ROWS, TOKENS), lambda i, at: (i, 0, 0, 0))
     return call(
-        product_kernel, at, (half, half), [outs_spec, whole(acts.shape)],
-        outs, acts, out_specs=(half_spec, half_spec), grid=(NY,),
-        scratch=[pltpu.VMEM(acts.shape, jnp.bfloat16)],
+        product_kernel, at, (half, half),
+        [whole(v.shape) for v in outs] + [whole(acts.shape)], *outs, acts,
+        out_specs=(half_spec, half_spec), grid=(NY,),
+        scratch=[
+            pltpu.VMEM(acts.shape, jnp.bfloat16),
+            pltpu.VMEM((PAIR * NC * ROWS, NX * TOKENS), jnp.bfloat16),
+        ],
     )
 
 
@@ -182,7 +212,7 @@
     z, x, c = lax.axis_index("z"), lax.axis_index("x"), lax.axis_index("c")
     t = lax.axis_index("tp")
     mine = (z * NX + x) * NC + c
-    at = jnp.stack([c, t]).astype(jnp.int32)
+    at = jnp.stack([c, t, x]).astype(jnp.int32)
 
     held = jnp.concatenate([activations.astype(F32), momentum])
     first = near_dot(held, right_prev, ((1,), (0,)))
@@ -197,8 +227,12 @@
         grid=(PAIR,),
     )
     turned = turned.reshape(NX, PAIR * NC * ROWS, TOKENS)
-    outs = lax.all_to_all(turned, "x", 0, 0, tiled=True)
-    outs = lax.all_gather(outs, "tp", axis=0, tiled=False)
+    outs = []
+    for k in range(NX):
+        block = lax.dynamic_index_in_dim(turned, (x + k) & (NX - 1), 0, keepdims=False)
+        outs.append(shifted(block, "x", NX, k) if k else block)
+    outs = jnp.stack(outs)
+    outs = [outs] + [shifted(outs, "tp", NY, k) for k in range(1, NY)]
 
     helds, spreads = [], []
     for half in (c, 1 - c):
@@ -212,27 +246,25 @@
     given = near_dot(spreads[1], first, ((0,), (0,)))
     kept = near_dot(spreads[0], first, ((0,), (0,)))
     piece = summed_piece(kept, given)
+    piece, at_left = lax.optimization_barrier((piece, at))
+    kept_grad, given_grad = core_products(at_left, outs, acts)
     near, far = gathered(piece)
+    summed_grad = kept_grad + other_core(given_grad)
+    grad = lax.psum_scatter(summed_grad, "z", scatter_dimension=0, tiled=True)
     seen = near_dot(spreads[0], near, ((1,), (0,))) + near_dot(spreads[1], far, ((1,), (0,)))
     second = over_tp(seen)
 
-    gram = full(near, near, ((0,), (0,))) + full(far, far, ((0,), (0,)))
+    gram = call(gram_kernel, at, shape(R, R), [whole((HALF, R))] * 2, near, far)
     gram, second = lax.optimization_barrier((gram, second))
     gram = over_tp(gram)
 
     given = near_dot(helds[1], second, ((0,), (0,)))
     kept = near_dot(helds[0], second, ((0,), (0,)))
-    given, at_right = lax.optimization_barrier((given, at))
     piece = summed_piece(kept, given)
-    kept_grad, given_grad = core_products(at_right, outs, acts)
-    summed_grad = kept_grad + other_core(given_grad)
-    grad = lax.psum_scatter(summed_grad, "z", scatter_dimension=0, tiled=True)
-    work, done = call(early_kernel, at, (shape(R, 2 * R), shape(R, R)), [whole((R, R))], gram)
+    work = jnp.concatenate([gram, jnp.eye(R, dtype=F32)], axis=1)
+    work, done = factor_step(0, work, jnp.zeros((R, R), F32))
     near, far = gathered(piece)
-    inverse = call(
-        late_kernel, at, shape(R, R), [whole((R, 2 * R)), whole((R, R))], work, done,
-        scratch=[pltpu.VMEM((R, 2 * R), F32)],
-    )
+    _, inverse = factor_step(BLOCKS // 2, work, done)
     basis = near_dot(second[TOKENS:], inverse, ((1,), (1,)))
     rights = [near_dot(v, inverse, ((1,), (1,))) for v in (near, far)]
     squares = sum(jnp.sum(v * v, axis=0) for v in rights)

time: 285 us -> 297 us (1.042)
  blocking collectives: 109 us -> 83.8 us
  starting transfers between devices: 21.4 us -> 39.9 us
  waiting for transfers between devices: 60.9 us -> 72.9 us
  Pallas kernels: 41.1 us -> 46.9 us
  matrix products: 18.5 us -> 14.5 us
  other arithmetic: 14.2 us -> 17.5 us
    ppermute x12 -> x18, waiting for transfers between devices: 28.9 us -> 62.9 us  [shifted(): return lax.ppermute(v, axis, [(i, (i + k) % n) for i in range(n)])]
    all_to_all x2 -> x1, blocking collectives: 65.3 us -> 34.9 us  [summed_piece(): arrived = lax.all_to_all(pieces, ('x', 'z'), 0, 0, tiled=True)]
    all_to_all x1, waiting for transfers between devices: 17.6 us -> 0.01 us  [summed_piece(): arrived = lax.all_to_all(pieces, ('x', 'z'), 0, 0, tiled=True)]
    ppermute x12 -> x18, starting transfers between devices: 11.7 us -> 23.5 us  [shifted(): return lax.ppermute(v, axis, [(i, (i + k) % n) for i in range(n)])]
    all_to_all x1, starting transfers between devices: 4.83 us -> 11.6 us  [summed_piece(): arrived = lax.all_to_all(pieces, ('x', 'z'), 0, 0, tiled=True)]
    pallas_call x4 -> x5, Pallas kernels: 41.1 us -> 46.9 us  [call(): pl.pallas_call(kernel, out_shape=out_shape, grid_spec=pltpu.PrefetchScala...]
    all_to_all x3, blocking collectives: 44.1 us -> 48.9 us  [spread_over(): lax.all_to_all(copies, axis, 0, 0, tiled=True).reshape(-1, v.shape[1])]
    dot_general x2 -> x0, matrix products: 3.19 us -> none  [full(): lax.dot_general(a, b, (dims, ((), ())), precision=lax.Precision.HIGHEST,...]
  transfers between devices with their start and end apart: 22 -> 27, of which waited for: 16 -> 18; matrix products, arithmetic and copies ran while one was open for 9% -> 11% of each run, Pallas kernels for 12% -> 13%
where the time goes in v3:
time: 297 us; the launch traced here: 296 us
  blocking collectives  83.8 us (28%)
  waiting for transfers between devices  72.9 us (25%)
  Pallas kernels  46.9 us (16%)
  starting transfers between devices  39.9 us (13%)
  other arithmetic  17.5 us (6%)
  matrix products  14.5 us (5%)
  between operations  14.4 us (5%)
  local copies, waits for them, and re-layouts  5.86 us (2%)
    ppermute x18, waiting for transfers between devices, shifted(): return lax.ppermute(v, axis, [(i, (i + k) % n) for i in range(n)])  62.9 us
    all_to_all x3, blocking collectives, spread_over(): lax.all_to_all(copies, axis, 0, 0, tiled=True).reshape(-1, v.shape[1])  48.9 us
    pallas_call x5, Pallas kernels, call(): pl.pallas_call(kernel, out_shape=out_shape, grid_spec=pltpu.PrefetchScala...  46.9 us
    all_to_all x1, blocking collectives, summed_piece(): arrived = lax.all_to_all(pieces, ('x', 'z'), 0, 0, tiled=True)  34.9 us
    ppermute x18, starting transfers between devices, shifted(): return lax.ppermute(v, axis, [(i, (i + k) % n) for i in range(n)])  23.5 us
    dot_general x14, matrix products, near_dot(): lax.dot_general(a, b, (dims, ((), ())), precision=lax.Precision.HIGH, pre...  14.5 us
    all_to_all x1, starting transfers between devices, summed_piece(): arrived = lax.all_to_all(pieces, ('x', 'z'), 0, 0, tiled=True)  11.6 us
    ppermute x5, waiting for transfers between devices, other_core(): return lax.ppermute(v, 'c', [(0, 1), (1, 0)])  6.17 us
  transfers between devices with their start and end apart: 27, of which 18 were waited for; matrix products, arithmetic and copies ran while one was open for 11% of the time, Pallas kernels for 13%

profile of v3, /device:TPU:2, one launch (start us, length us, event | category | flops | bytes accessed | tf_op | source)
XLA Modules:
  0.0 295.7 jit_solution(7392704543796696894)
XLA Ops:
  11.2 3.1 %collective-permute-start.2 = (f32[208,256]{1,0:T(8,128)S(1)}, f32[208,256]{1,0:T(8,128)S(1)}, u32[]{:S(2)}, u32[]{:S(2)}) collective-permute-start(f32[208,256]{1,0:T(8,128)S(1)} %fusion), channel_id=1, source_target_pairs={{0,3},{1,0},{2,1},{3,2},{4,7},{5,4},{6,5},{7,6},{8,11},{9,8},{10,9... | collective-permute-start | bytes 638984 | tf_op jit(solution)/shard_map/ppermute | solution.py:34
  17.1 6.3 %collective-permute-done.2 = f32[208,256]{1,0:T(8,128)S(1)} collective-permute-done((f32[208,256]{1,0:T(8,128)S(1)}, f32[208,256]{1,0:T(8,128)S(1)}, u32[]{:S(2)}, u32[]{:S(2)}) %collective-permute-start.2) | collective-permute-done | bytes 213024 | tf_op jit(solution)/shard_map/ppermute | solution.py:34
  24.1 3.1 %collective-permute-done = f32[208,256]{1,0:T(8,128)} collective-permute-done((f32[208,256]{1,0:T(8,128)S(1)}, f32[208,256]{1,0:T(8,128)}, u32[]{:S(2)}, u32[]{:S(2)}) %collective-permute-start) | collective-permute-done | bytes 213024 | tf_op jit(solution)/shard_map/ppermute | solution.py:34
  30.1 2.3 collective-permute-done.3
  32.4 1.9 convolution_add_fusion.1
  35.2 11.6 %all-to-all-start = ((f32[32,20,256]{2,1,0:T(8,128)}), f32[32,20,256]{2,1,0:T(8,128)S(1)}, u32[]{:S(2)}, u32[]{:S(2)}) async-start(f32[32,20,256]{2,1,0:T(8,128)} %reshape.30), calls=%async_computation | async-start | bytes 1572864 | tf_op jit(solution)/shard_map/all_to_all | solution.py:196
  47.5 2.6 shard_map.67
  51.6 2.7 collective-permute-start.5
  54.3 1.8 collective-permute-start.4
  56.1 4.2 %collective-permute-done.6 = f32[320,128]{1,0:T(8,128)S(1)} collective-permute-done((f32[320,128]{1,0:T(8,128)S(1)}, f32[320,128]{1,0:T(8,128)S(1)}, u32[]{:S(2)}, u32[]{:S(2)}) %collective-permute-start.6) | collective-permute-done | bytes 163872 | tf_op jit(solution)/shard_map/ppermute | solution.py:34
  60.3 7.4 %collective-permute-done.5 = f32[320,128]{1,0:T(8,128)S(1)} collective-permute-done((f32[320,128]{1,0:T(8,128)S(1)}, f32[320,128]{1,0:T(8,128)S(1)}, u32[]{:S(2)}, u32[]{:S(2)}) %collective-permute-start.5) | collective-permute-done | bytes 163872 | tf_op jit(solution)/shard_map/ppermute | solution.py:34
  68.6 1.9 collective-permute-start.9
  72.2 26.6 %collective-permute-done.9.refs_3_ = f32[4,320,128]{2,1,0:T(8,128)} collective-permute-done((f32[4,320,128]{2,1,0:T(8,128)}, f32[4,320,128]{2,1,0:T(8,128)}, u32[]{:S(2)}, u32[]{:S(2)}) %collective-permute-start.9) | collective-permute-done | bytes 655392 | tf_op jit(solution)/shard_map/ppermute | solution.py:34
  98.9 3.7 %collective-permute-done.7.refs_1_ = f32[4,320,128]{2,1,0:T(8,128)} collective-permute-done((f32[4,320,128]{2,1,0:T(8,128)}, f32[4,320,128]{2,1,0:T(8,128)}, u32[]{:S(2)}, u32[]{:S(2)}) %collective-permute-start.7) | collective-permute-done | bytes 655392 | tf_op jit(solution)/shard_map/ppermute | solution.py:34
  102.6 7.8 %shard_map.68 = (f32[640,1280]{1,0:T(8,128)}, f32[640,1280]{1,0:T(8,128)}) custom-call(s32[3]{0:T(128)} %pad_add_fusion.at, f32[4,320,128]{2,1,0:T(8,128)} %pad_maximum_fusion.2.refs_0_, f32[4,320,128]{2,1,0:T(8,128)} %collective-permute-done.7.refs_1_, f32[4,320,128]{2,1,0:T(8,128)} %collective-permute-done.8.refs_2_, ...), custom_call_target="tpu_custom_call" | custom-call | tf_op jit(solution)/shard_map/pallas_call | solution.py:69
  110.3 18.0 %all_to_all.30 = f32[8,20,256]{2,1,0:T(8,128)S(1)} all-to-all(f32[8,20,256]{2,1,0:T(8,128)S(1)} %broadcast_in_dim.16), channel_id=1, replica_groups=mesh['z'=8,'x'=4,'c'=2,'tp'=4] {'z'}, dimensions={0} | all-to-all | bytes 327680 | tf_op jit(solution)/shard_map/all_to_all | solution.py:202
  128.4 13.3 %all_to_all.31 = f32[4,160,256]{2,1,0:T(8,128)S(1)} all-to-all(f32[4,160,256]{2,1,0:T(8,128)S(1)} %broadcast_in_dim.18), channel_id=1, replica_groups=mesh['z'=8,'x'=4,'c'=2,'tp'=4] {'x'}, dimensions={0} | all-to-all | bytes 1310720 | tf_op jit(solution)/shard_map/all_to_all | solution.py:202
  146.6 4.8 %shard_map.69 = f32[256,256]{1,0:T(8,128)} custom-call(s32[3]{0:T(128)} %pad_add_fusion.at, f32[640,256]{1,0:T(8,128)} %bitcast.38, f32[640,256]{1,0:T(8,128)} %copy-done.3), custom_call_target="tpu_custom_call" | custom-call | tf_op jit(solution)/shard_map/pallas_call | solution.py:69
  151.4 5.0 %add.152 = f32[640,1280]{1,0:T(8,128)} add(f32[640,1280]{1,0:T(8,128)} %get-tuple-element.19, f32[640,1280]{1,0:T(8,128)} %collective-permute-done.10) | non-fusion elementwise | flops 819200 | bytes 9830400 | tf_op jit(solution)/shard_map/add | solution.py:252
  160.2 2.2 collective-permute-done.18
  162.4 1.9 convolution_add_fusion
  165.3 34.9 %all_to_all.32 = f32[32,20,256]{2,1,0:T(8,128)S(1)} all-to-all(f32[32,20,256]{2,1,0:T(8,128)} %reshape.33), channel_id=1, replica_groups=mesh['z'=8,'x'=4,'c'=2,'tp'=4] {'x','z'}, dimensions={0} | all-to-all | bytes 1310720 | tf_op jit(solution)/shard_map/all_to_all | solution.py:196
  200.2 17.7 %all_to_all.33 = f32[8,20,256]{2,1,0:T(8,128)S(1)} all-to-all(f32[8,20,256]{2,1,0:T(8,128)S(1)} %broadcast_in_dim.39), channel_id=1, replica_groups=mesh['z'=8,'x'=4,'c'=2,'tp'=4] {'z'}, dimensions={0} | all-to-all | bytes 327680 | tf_op jit(solution)/shard_map/all_to_all | solution.py:202
  218.8 4.6 %all-to-all-start.5 = ((f32[4,160,256]{2,1,0:T(8,128)}), f32[4,160,256]{2,1,0:T(8,128)S(1)}, u32[]{:S(2)}, u32[]{:S(2)}) async-start(f32[4,160,256]{2,1,0:T(8,128)} %broadcast_in_dim.41), calls=%async_computation.6 | async-start | bytes 1310720 | tf_op jit(solution)/shard_map/all_to_all | solution.py:202
  227.7 3.9 %all-to-all-done.5 = f32[4,160,256]{2,1,0:T(8,128)S(1)} async-done(((f32[4,160,256]{2,1,0:T(8,128)}), f32[4,160,256]{2,1,0:T(8,128)S(1)}, u32[]{:S(2)}, u32[]{:S(2)}) %all-to-all-start.5) | async-done | bytes 655392 | tf_op jit(solution)/shard_map/all_to_all | solution.py:202
  232.4 2.5 collective-permute-done.16
  235.0 2.8 collective-permute-done.15
  240.5 15.8 %shard_map.70 = (f32[256,512]{1,0:T(8,128)}, f32[256,256]{1,0:T(8,128)}) custom-call(s32[1]{0:T(128)} %constant.57.clone.1.at, f32[256,512]{1,0:T(8,128)} %pad_maximum_fusion.5.work_in, f32[256,256]{1,0:T(8,128)} %broadcast_in_dim.38.done), custom_call_target="tpu_custom_call" | custom-call | tf_op jit(solution)/shard_map/pallas_call | solution.py:69
  256.3 15.8 %shard_map.71 = (f32[256,512]{1,0:T(8,128)}, f32[256,256]{1,0:T(8,128)}) custom-call(s32[1]{0:T(128)} %constant.56.clone.1.at, f32[256,512]{1,0:T(8,128)} %get-tuple-element.24.work_in, f32[256,256]{1,0:T(8,128)} %get-tuple-element.25.done), custom_call_target="tpu_custom_call" | custom-call | tf_op jit(solution)/shard_map/pallas_call | solution.py:69
  276.7 1.8 collective-permute-start.21
  282.2 2.6 collective-permute-done.20
  287.0 1.8 fusion.8
  (106 shorter events, 44.9 us)
Async XLA Ops:
  7.2 95.4 %all-gather.2.cloned.1.call-start = ((), (), s32[]{:S(2)}) async-start(), calls=%async_computation.7 | async-start | bytes 3276800 | tf_op jit(solution)/shard_map/all_gather | solution.py:222
  11.2 12.2 %collective-permute-start.2 = (f32[208,256]{1,0:T(8,128)S(1)}, f32[208,256]{1,0:T(8,128)S(1)}, u32[]{:S(2)}, u32[]{:S(2)}) collective-permute-start(f32[208,256]{1,0:T(8,128)S(1)} %fusion), channel_id=1, source_target_pairs={{0,3},{1,0},{2,1},{3,2},{4,7},{5,4},{6,5},{7,6},{8,11},{9,8},{10,9... | collective-permute-start | bytes 638984 | tf_op jit(solution)/shard_map/ppermute | solution.py:34
  14.3 9.8 %collective-permute-start.1 = (f32[208,256]{1,0:T(8,128)S(1)}, f32[208,256]{1,0:T(8,128)}, u32[]{:S(2)}, u32[]{:S(2)}) collective-permute-start(f32[208,256]{1,0:T(8,128)S(1)} %fusion), channel_id=1, source_target_pairs={{0,2},{1,3},{2,0},{3,1},{4,6},{5,7},{6,4},{7,5},{8,10},{9,11},{10,... | collective-permute-start | bytes 638984 | tf_op jit(solution)/shard_map/ppermute | solution.py:34
  14.9 12.3 %collective-permute-start = (f32[208,256]{1,0:T(8,128)S(1)}, f32[208,256]{1,0:T(8,128)}, u32[]{:S(2)}, u32[]{:S(2)}) collective-permute-start(f32[208,256]{1,0:T(8,128)S(1)} %fusion), channel_id=1, source_target_pairs={{0,1},{1,2},{2,3},{3,0},{4,5},{5,6},{6,7},{7,4},{8,9},{9,10},{10,1... | collective-permute-start | bytes 638984 | tf_op jit(solution)/shard_map/ppermute | solution.py:34
  17.0 13.0 %copy-start.5 = (f32[80,640]{1,0:T(8,128)}, f32[80,640]{1,0:T(8,128)S(1)}, u32[]{:S(2)}) copy-start(f32[80,640]{1,0:T(8,128)S(1)} %fusion.11) | copy-start | bytes 614404
  30.0 2.4 collective-permute-start.3
  35.2 36.9 %all-to-all-start = ((f32[32,20,256]{2,1,0:T(8,128)}), f32[32,20,256]{2,1,0:T(8,128)S(1)}, u32[]{:S(2)}, u32[]{:S(2)}) async-start(f32[32,20,256]{2,1,0:T(8,128)} %reshape.30), calls=%async_computation | async-start | bytes 1572864 | tf_op jit(solution)/shard_map/all_to_all | solution.py:196
  46.8 240.2 %reduce-scatter.2.cloned.1.call-start = ((), (), s32[]{:S(2)}) async-start(), calls=%async_computation.8 | async-start | bytes 3686400 | tf_op jit(solution)/shard_map/reduce_scatter | solution.py:253
  51.3 9.0 %collective-permute-start.6 = (f32[320,128]{1,0:T(8,128)S(1)}, f32[320,128]{1,0:T(8,128)S(1)}, u32[]{:S(2)}, u32[]{:S(2)}) collective-permute-start(f32[320,128]{1,0:T(8,128)S(1)} %get-tuple-element.32), channel_id=1, source_target_pairs={{0,24},{8,0},{16,8},{24,16},{1,25},{9,1},{17,9},{25,17},{2,26},{10... | collective-permute-start | bytes 491528 | tf_op jit(solution)/shard_map/ppermute | solution.py:34
  51.6 16.1 %collective-permute-start.5 = (f32[320,128]{1,0:T(8,128)S(1)}, f32[320,128]{1,0:T(8,128)S(1)}, u32[]{:S(2)}, u32[]{:S(2)}) collective-permute-start(f32[320,128]{1,0:T(8,128)S(1)} %get-tuple-element.33), channel_id=1, source_target_pairs={{0,16},{8,24},{16,0},{24,8},{1,17},{9,25},{17,1},{25,9},{2,18},{10... | collective-permute-start | bytes 491528 | tf_op jit(solution)/shard_map/ppermute | solution.py:34
  54.3 13.4 %collective-permute-start.4 = (f32[320,128]{1,0:T(8,128)S(1)}, f32[320,128]{1,0:T(8,128)S(1)}, u32[]{:S(2)}, u32[]{:S(2)}) collective-permute-start(f32[320,128]{1,0:T(8,128)S(1)} %get-tuple-element.34), channel_id=1, source_target_pairs={{0,8},{8,16},{16,24},{24,0},{1,9},{9,17},{17,25},{25,1},{2,10},{10... | collective-permute-start | bytes 491528 | tf_op jit(solution)/shard_map/ppermute | solution.py:34
  68.6 30.2 %collective-permute-start.9 = (f32[4,320,128]{2,1,0:T(8,128)}, f32[4,320,128]{2,1,0:T(8,128)}, u32[]{:S(2)}, u32[]{:S(2)}) collective-permute-start(f32[4,320,128]{2,1,0:T(8,128)} %pad_maximum_fusion.2.refs_0_), channel_id=1, source_target_pairs={{0,3},{1,0},{2,1},{3,2},{4,7},{5,4},{6,5},{7,6},{8,11},{9,8},{10,9... | collective-permute-start | bytes 1966088 | tf_op jit(solution)/shard_map/ppermute | solution.py:34
  70.5 28.4 %collective-permute-start.8 = (f32[4,320,128]{2,1,0:T(8,128)}, f32[4,320,128]{2,1,0:T(8,128)}, u32[]{:S(2)}, u32[]{:S(2)}) collective-permute-start(f32[4,320,128]{2,1,0:T(8,128)} %pad_maximum_fusion.2.refs_0_), channel_id=1, source_target_pairs={{0,2},{1,3},{2,0},{3,1},{4,6},{5,7},{6,4},{7,5},{8,10},{9,11},{10,... | collective-permute-start | bytes 1966088 | tf_op jit(solution)/shard_map/ppermute | solution.py:34
  71.3 31.3 %collective-permute-start.7 = (f32[4,320,128]{2,1,0:T(8,128)}, f32[4,320,128]{2,1,0:T(8,128)}, u32[]{:S(2)}, u32[]{:S(2)}) collective-permute-start(f32[4,320,128]{2,1,0:T(8,128)} %pad_maximum_fusion.2.refs_0_), channel_id=1, source_target_pairs={{0,1},{1,2},{2,3},{3,0},{4,5},{5,6},{6,7},{7,4},{8,9},{9,10},{10,1... | collective-permute-start | bytes 1966088 | tf_op jit(solution)/shard_map/ppermute | solution.py:34
  110.3 41.1 %collective-permute-start.10 = (f32[640,1280]{1,0:T(8,128)}, f32[640,1280]{1,0:T(8,128)}, u32[]{:S(2)}, u32[]{:S(2)}) collective-permute-start(f32[640,1280]{1,0:T(8,128)} %get-tuple-element.20), channel_id=1, source_target_pairs={{0,4},{4,0},{1,5},{5,1},{2,6},{6,2},{3,7},{7,3},{8,12},{12,8},{9,1... | collective-permute-start | bytes 9830408 | tf_op jit(solution)/shard_map/ppermute | solution.py:38
  128.3 13.4 %copy-start.8 = (f32[80,640]{1,0:T(8,128)S(1)}, f32[80,640]{1,0:T(8,128)}, u32[]{:S(2)}) copy-start(f32[80,640]{1,0:T(8,128)} %copy-done.7) | copy-start | bytes 614404
  128.4 15.4 %copy-start.6 = (f32[80,640]{1,0:T(8,128)S(1)}, f32[80,640]{1,0:T(8,128)}, u32[]{:S(2)}) copy-start(f32[80,640]{1,0:T(8,128)} %copy-done.5) | copy-start | bytes 614404
  141.7 2.1 collective-permute-start.11
  144.2 12.2 %collective-permute-start.14 = (f32[208,256]{1,0:T(8,128)S(1)}, f32[208,256]{1,0:T(8,128)S(1)}, u32[]{:S(2)}, u32[]{:S(2)}) collective-permute-start(f32[208,256]{1,0:T(8,128)S(1)} %convolution_add_fusion.2), channel_id=1, source_target_pairs={{0,3},{1,0},{2,1},{3,2},{4,7},{5,4},{6,5},{7,6},{8,11},{9,8},{10,9... | collective-permute-start | bytes 638984 | tf_op jit(solution)/shard_map/ppermute | solution.py:34
  144.9 11.5 %collective-permute-start.13 = (f32[208,256]{1,0:T(8,128)S(1)}, f32[208,256]{1,0:T(8,128)}, u32[]{:S(2)}, u32[]{:S(2)}) collective-permute-start(f32[208,256]{1,0:T(8,128)S(1)} %convolution_add_fusion.2), channel_id=1, source_target_pairs={{0,2},{1,3},{2,0},{3,1},{4,6},{5,7},{6,4},{7,5},{8,10},{9,11},{10,... | collective-permute-start | bytes 638984 | tf_op jit(solution)/shard_map/ppermute | solution.py:34
  145.7 12.4 %collective-permute-start.12 = (f32[208,256]{1,0:T(8,128)S(1)}, f32[208,256]{1,0:T(8,128)}, u32[]{:S(2)}, u32[]{:S(2)}) collective-permute-start(f32[208,256]{1,0:T(8,128)S(1)} %convolution_add_fusion.2), channel_id=1, source_target_pairs={{0,1},{1,2},{2,3},{3,0},{4,5},{5,6},{6,7},{7,4},{8,9},{9,10},{10,1... | collective-permute-start | bytes 638984 | tf_op jit(solution)/shard_map/ppermute | solution.py:34
  156.4 2.9 copy-start.1
  160.1 2.3 collective-permute-start.18
  217.9 5.5 %copy-start.10 = (f32[256,256]{1,0:T(8,128)S(1)}, f32[256,256]{1,0:T(8,128)}, u32[]{:S(2)}) copy-start(f32[256,256]{1,0:T(8,128)} %shard_map.69) | copy-start | bytes 786436
  218.8 12.8 %all-to-all-start.5 = ((f32[4,160,256]{2,1,0:T(8,128)}), f32[4,160,256]{2,1,0:T(8,128)S(1)}, u32[]{:S(2)}, u32[]{:S(2)}) async-start(f32[4,160,256]{2,1,0:T(8,128)} %broadcast_in_dim.41), calls=%async_computation.6 | async-start | bytes 1310720 | tf_op jit(solution)/shard_map/all_to_all | solution.py:202
  223.4 9.0 %collective-permute-start.17 = (f32[256,256]{1,0:T(8,128)S(1)}, f32[256,256]{1,0:T(8,128)S(1)}, u32[]{:S(2)}, u32[]{:S(2)}) collective-permute-start(f32[256,256]{1,0:T(8,128)S(1)} %copy-done.10), channel_id=1, source_target_pairs={{0,3},{1,0},{2,1},{3,2},{4,7},{5,4},{6,5},{7,6},{8,11},{9,8},{10,9... | collective-permute-start | bytes 786440 | tf_op jit(solution)/shard_map/ppermute | solution.py:34
  224.8 10.2 %collective-permute-start.16 = (f32[256,256]{1,0:T(8,128)S(1)}, f32[256,256]{1,0:T(8,128)}, u32[]{:S(2)}, u32[]{:S(2)}) collective-permute-start(f32[256,256]{1,0:T(8,128)S(1)} %copy-done.10), channel_id=1, source_target_pairs={{0,2},{1,3},{2,0},{3,1},{4,6},{5,7},{6,4},{7,5},{8,10},{9,11},{10,... | collective-permute-start | bytes 786440 | tf_op jit(solution)/shard_map/ppermute | solution.py:34
  226.3 11.5 %collective-permute-start.15 = (f32[256,256]{1,0:T(8,128)S(1)}, f32[256,256]{1,0:T(8,128)}, u32[]{:S(2)}, u32[]{:S(2)}) collective-permute-start(f32[256,256]{1,0:T(8,128)S(1)} %copy-done.10), channel_id=1, source_target_pairs={{0,1},{1,2},{2,3},{3,0},{4,5},{5,6},{6,7},{7,4},{8,9},{9,10},{10,1... | collective-permute-start | bytes 786440 | tf_op jit(solution)/shard_map/ppermute | solution.py:34
  231.6 43.4 %collective-permute-start.19 = (f32[640,256]{1,0:T(8,128)S(1)}, f32[640,256]{1,0:T(8,128)}, u32[]{:S(2)}, u32[]{:S(2)}) collective-permute-start(f32[640,256]{1,0:T(8,128)S(1)} %bitcast.39), channel_id=1, source_target_pairs={{0,4},{4,0},{1,5},{5,1},{2,6},{6,2},{3,7},{7,3},{8,12},{12,8},{9,1... | collective-permute-start | bytes 1966088 | tf_op jit(solution)/shard_map/ppermute | solution.py:38
  276.7 5.2 %collective-permute-start.21 = (f32[8,256]{1,0:T(8,128)S(1)}, f32[8,256]{1,0:T(8,128)S(1)}, u32[]{:S(2)}, u32[]{:S(2)}) collective-permute-start(f32[8,256]{1,0:T(8,128)S(1)} %broadcast_in_dim.42), channel_id=1, source_target_pairs={{0,2},{1,3},{2,0},{3,1},{4,6},{5,7},{6,4},{7,5},{8,10},{9,11},{10,... | collective-permute-start | bytes 24584 | tf_op jit(solution)/shard_map/ppermute | solution.py:34
  278.6 3.7 %collective-permute-start.22 = (f32[8,256]{1,0:T(8,128)S(1)}, f32[8,256]{1,0:T(8,128)S(1)}, u32[]{:S(2)}, u32[]{:S(2)}) collective-permute-start(f32[8,256]{1,0:T(8,128)S(1)} %broadcast_in_dim.42), channel_id=1, source_target_pairs={{0,3},{1,0},{2,1},{3,2},{4,7},{5,4},{6,5},{7,6},{8,11},{9,8},{10,9... | collective-permute-start | bytes 24584 | tf_op jit(solution)/shard_map/ppermute | solution.py:34
  279.9 4.9 %collective-permute-start.20 = (f32[8,256]{1,0:T(8,128)S(1)}, f32[8,256]{1,0:T(8,128)S(1)}, u32[]{:S(2)}, u32[]{:S(2)}) collective-permute-start(f32[8,256]{1,0:T(8,128)S(1)} %broadcast_in_dim.42), channel_id=1, source_target_pairs={{0,1},{1,2},{2,3},{3,0},{4,5},{5,6},{6,7},{7,4},{8,9},{9,10},{10,1... | collective-permute-start | bytes 24584 | tf_op jit(solution)/shard_map/ppermute | solution.py:34
  (7 other events, 14.3 us)
Sparse Core Ops, SparseCore 0:
  11.3 40.5 all-gather.1
  156.5 63.8 reduce-scatter.1

commit v4 on v3

--- a/solution.py
+++ b/solution.py
@@ -142,12 +142,12 @@
             work_ref[there, :] = pltpu.roll(left, 2 * R - EDGE, 1)
         return 0
 
-    lax.fori_loop(0, BLOCKS // 2, step, 0)
-
-
-def factor_step(first_block, work, done):
+    lax.fori_loop(0, at[1], step, 0)
+
+
+def factor_step(first_block, count, work, done):
     return call(
-        factor_kernel, jnp.full((1,), first_block, jnp.int32),
+        factor_kernel, jnp.array([first_block, count], jnp.int32),
         (shape(R, 2 * R), shape(R, R)), [whole((R, 2 * R)), whole((R, R))], work, done,
     )
 
@@ -168,13 +168,19 @@
             for k in range(NX):
                 lhs[:, k * TOKENS : (k + 1) * TOKENS] = source[k].astype(jnp.bfloat16)
 
-    total = plain(lhs[...], joined[...], ((1,), (0,)))
     first = at[C] == 0
-    for i in range(PAIR):
-        near = total[NC * i * ROWS : (NC * i + 1) * ROWS]
-        far = total[(NC * i + 1) * ROWS : (NC * i + 2) * ROWS]
-        kept[i * ROWS : (i + 1) * ROWS, :] = jnp.where(first, near, far)
-        given[i * ROWS : (i + 1) * ROWS, :] = jnp.where(first, far, near)
+
+    def columns(n, _):
+        here = pl.ds(pl.multiple_of(n * 2 * STEP, STEP), 2 * STEP)
+        total = plain(lhs[...], joined[:, here], ((1,), (0,)))
+        for i in range(PAIR):
+            near = total[NC * i * ROWS : (NC * i + 1) * ROWS]
+            far = total[(NC * i + 1) * ROWS : (NC * i + 2) * ROWS]
+            kept[i * ROWS : (i + 1) * ROWS, here] = jnp.where(first, near, far)
+            given[i * ROWS : (i + 1) * ROWS, here] = jnp.where(first, far, near)
+        return 0
+
+    lax.fori_loop(0, COLS // (2 * STEP), columns, 0)
 
 
 def core_products(at, outs, acts):
@@ -192,8 +198,10 @@
 
 
 def summed_piece(kept, given):
-    pieces = (kept + other_core(given)).reshape(NX * NZ, HALF // (NX * NZ), R)
-    arrived = lax.all_to_all(pieces, ("x", "z"), 0, 0, tiled=True)
+    pieces = (kept + other_core(given)).reshape(NX, HALF // NX, R)
+    arrived = lax.all_to_all(pieces, "x", 0, 0, tiled=True)
+    pieces = jnp.sum(arrived, axis=0).reshape(NZ, HALF // (NX * NZ), R)
+    arrived = lax.all_to_all(pieces, "z", 0, 0, tiled=True)
     return jnp.sum(arrived, axis=0)
 
 
@@ -246,12 +254,12 @@
     given = near_dot(spreads[1], first, ((0,), (0,)))
     kept = near_dot(spreads[0], first, ((0,), (0,)))
     piece = summed_piece(kept, given)
-    piece, at_left = lax.optimization_barrier((piece, at))
-    kept_grad, given_grad = core_products(at_left, outs, acts)
     near, far = gathered(piece)
+    seen = near_dot(spreads[0], near, ((1,), (0,))) + near_dot(spreads[1], far, ((1,), (0,)))
+    seen, at_seen = lax.optimization_barrier((seen, at))
+    kept_grad, given_grad = core_products(at_seen, outs, acts)
     summed_grad = kept_grad + other_core(given_grad)
     grad = lax.psum_scatter(summed_grad, "z", scatter_dimension=0, tiled=True)
-    seen = near_dot(spreads[0], near, ((1,), (0,))) + near_dot(spreads[1], far, ((1,), (0,)))
     second = over_tp(seen)
 
     gram = call(gram_kernel, at, shape(R, R), [whole((HALF, R))] * 2, near, far)
@@ -262,9 +270,10 @@
     kept = near_dot(helds[0], second, ((0,), (0,)))
     piece = summed_piece(kept, given)
     work = jnp.concatenate([gram, jnp.eye(R, dtype=F32)], axis=1)
-    work, done = factor_step(0, work, jnp.zeros((R, R), F32))
+    work, done = factor_step(0, 2, work, jnp.zeros((R, R), F32))
     near, far = gathered(piece)
-    _, inverse = factor_step(BLOCKS // 2, work, done)
+    work, done = factor_step(2, 1, work, done)
+    _, inverse = factor_step(3, 1, work, done)
     basis = near_dot(second[TOKENS:], inverse, ((1,), (1,)))
     rights = [near_dot(v, inverse, ((1,), (1,))) for v in (near, far)]
     squares = sum(jnp.sum(v * v, axis=0) for v in rights)

time: 297 us -> 299 us (level)
  starting transfers between devices: 39.9 us -> 29.9 us
  blocking collectives: 83.8 us -> 91.5 us
  Pallas kernels: 46.9 us -> 53.5 us
  waiting for transfers between devices: 72.9 us -> 69.6 us
    all_to_all x1 -> x4, blocking collectives: 34.9 us -> 66.9 us  [the longest x2 35.7 us: summed_piece(): arrived = lax.all_to_all(pieces, 'x', 0, 0, tiled=True)]
    all_to_all x3 -> x2, blocking collectives: 48.9 us -> 24.6 us  [spread_over(): lax.all_to_all(copies, axis, 0, 0, tiled=True).reshape(-1, v.shape[1])]
    all_to_all x1 -> x0, starting transfers between devices: 11.6 us -> none  [summed_piece(): arrived = lax.all_to_all(pieces, ('x', 'z'), 0, 0, tiled=True)]
    ppermute x18, waiting for transfers between devices: 62.9 us -> 55.7 us  [shifted(): return lax.ppermute(v, axis, [(i, (i + k) % n) for i in range(n)])]
    pallas_call x5 -> x6, Pallas kernels: 46.9 us -> 53.5 us  [call(): pl.pallas_call(kernel, out_shape=out_shape, grid_spec=pltpu.PrefetchScala...]
    all_to_all x1 -> x2, starting transfers between devices: 4.59 us -> 9.07 us  [spread_over(): lax.all_to_all(copies, axis, 0, 0, tiled=True).reshape(-1, v.shape[1])]
    ppermute x5, waiting for transfers between devices: 6.17 us -> 10.6 us  [other_core(): return lax.ppermute(v, 'c', [(0, 1), (1, 0)])]
  transfers between devices with their start and end apart: 27 -> 27, of which waited for: 18 -> 21; matrix products, arithmetic and copies ran while one was open for 11% -> 10% of each run, Pallas kernels for 13% -> 15%
where the time goes in v4:
time: 299 us; the launch traced here: 298 us
  blocking collectives  91.5 us (31%)
  waiting for transfers between devices  69.6 us (23%)
  Pallas kernels  53.5 us (18%)
  starting transfers between devices  29.9 us (10%)
  other arithmetic  16.9 us (6%)
  matrix products  14.6 us (5%)
  between operations  14.4 us (5%)
  local copies, waits for them, and re-layouts  7.81 us (3%)
    ppermute x18, waiting for transfers between devices, shifted(): return lax.ppermute(v, axis, [(i, (i + k) % n) for i in range(n)])  55.7 us
    pallas_call x6, Pallas kernels, call(): pl.pallas_call(kernel, out_shape=out_shape, grid_spec=pltpu.PrefetchScala...  53.5 us
    all_to_all x2, blocking collectives, summed_piece(): arrived = lax.all_to_all(pieces, 'x', 0, 0, tiled=True)  35.7 us
    all_to_all x2, blocking collectives, summed_piece(): arrived = lax.all_to_all(pieces, 'z', 0, 0, tiled=True)  31.3 us
    all_to_all x2, blocking collectives, spread_over(): lax.all_to_all(copies, axis, 0, 0, tiled=True).reshape(-1, v.shape[1])  24.6 us
    ppermute x18, starting transfers between devices, shifted(): return lax.ppermute(v, axis, [(i, (i + k) % n) for i in range(n)])  20.6 us
    dot_general x14, matrix products, near_dot(): lax.dot_general(a, b, (dims, ((), ())), precision=lax.Precision.HIGH, pre...  14.6 us
    ppermute x5, waiting for transfers between devices, other_core(): return lax.ppermute(v, 'c', [(0, 1), (1, 0)])  10.6 us
  transfers between devices with their start and end apart: 27, of which 21 were waited for; matrix products, arithmetic and copies ran while one was open for 10% of the time, Pallas kernels for 15%

profile of v4, /device:TPU:2, one launch (start us, length us, event | category | flops | bytes accessed | tf_op | source)
XLA Modules:
  0.0 298.1 jit_solution(18246495523999422829)
XLA Ops:
  10.3 3.1 %collective-permute-start.2 = (f32[208,256]{1,0:T(8,128)S(1)}, f32[208,256]{1,0:T(8,128)S(1)}, u32[]{:S(2)}, u32[]{:S(2)}) collective-permute-start(f32[208,256]{1,0:T(8,128)S(1)} %fusion), channel_id=1, source_target_pairs={{0,3},{1,0},{2,1},{3,2},{4,7},{5,4},{6,5},{7,6},{8,11},{9,8},{10,9... | collective-permute-start | bytes 638984 | tf_op jit(solution)/shard_map/ppermute | solution.py:34
  17.1 5.4 %collective-permute-done.2 = f32[208,256]{1,0:T(8,128)S(1)} collective-permute-done((f32[208,256]{1,0:T(8,128)S(1)}, f32[208,256]{1,0:T(8,128)S(1)}, u32[]{:S(2)}, u32[]{:S(2)}) %collective-permute-start.2) | collective-permute-done | bytes 213024 | tf_op jit(solution)/shard_map/ppermute | solution.py:34
  23.7 2.5 collective-permute-done
  29.1 2.3 collective-permute-done.3
  33.4 22.2 %all_to_all.40 = f32[4,160,256]{2,1,0:T(8,128)S(1)} all-to-all(f32[4,160,256]{2,1,0:T(8,128)S(1)} %bitcast.44), channel_id=1, replica_groups=mesh['z'=8,'x'=4,'c'=2,'tp'=4] {'x'}, dimensions={0} | all-to-all | bytes 1310720 | tf_op jit(solution)/shard_map/all_to_all | solution.py:202
  57.2 18.0 %all_to_all.41 = f32[8,20,256]{2,1,0:T(8,128)S(1)} all-to-all(f32[8,20,256]{2,1,0:T(8,128)S(1)} %reshape.37), channel_id=1, replica_groups=mesh['z'=8,'x'=4,'c'=2,'tp'=4] {'z'}, dimensions={0} | all-to-all | bytes 327680 | tf_op jit(solution)/shard_map/all_to_all | solution.py:204
  75.2 12.2 %all_to_all.42 = f32[8,20,256]{2,1,0:T(8,128)S(1)} all-to-all(f32[8,20,256]{2,1,0:T(8,128)S(1)} %broadcast_in_dim.16), channel_id=1, replica_groups=mesh['z'=8,'x'=4,'c'=2,'tp'=4] {'z'}, dimensions={0} | all-to-all | bytes 327680 | tf_op jit(solution)/shard_map/all_to_all | solution.py:210
  88.3 4.9 %all-to-all-start.3 = ((f32[4,160,256]{2,1,0:T(8,128)}), f32[4,160,256]{2,1,0:T(8,128)S(1)}, u32[]{:S(2)}, u32[]{:S(2)}) async-start(f32[4,160,256]{2,1,0:T(8,128)} %broadcast_in_dim.18), calls=%async_computation.3 | async-start | bytes 1310720 | tf_op jit(solution)/shard_map/all_to_all | solution.py:210
  93.9 2.6 shard_map.94
  98.6 2.8 collective-permute-start.6
  103.2 2.7 collective-permute-done.7
  112.7 14.2 %collective-permute-done.10.refs_3_ = f32[4,320,128]{2,1,0:T(8,128)S(1)} collective-permute-done((f32[4,320,128]{2,1,0:T(8,128)S(1)}, f32[4,320,128]{2,1,0:T(8,128)S(1)}, u32[]{:S(2)}, u32[]{:S(2)}) %collective-permute-start.10) | collective-permute-done | bytes 655392 | tf_op jit(solution)/shard_map/ppermute | solution.py:34
  126.8 2.1 collective-permute-done.9.refs_2_
  129.8 9.0 %collective-permute-done.8.refs_1_ = f32[4,320,128]{2,1,0:T(8,128)} collective-permute-done((f32[4,320,128]{2,1,0:T(8,128)S(1)}, f32[4,320,128]{2,1,0:T(8,128)}, u32[]{:S(2)}, u32[]{:S(2)}) %collective-permute-start.8) | collective-permute-done | bytes 655392 | tf_op jit(solution)/shard_map/ppermute | solution.py:34
  138.8 9.9 %shard_map.95 = (f32[640,1280]{1,0:T(8,128)}, f32[640,1280]{1,0:T(8,128)}) custom-call(s32[3]{0:T(128)} %pad_add_fusion.at, f32[4,320,128]{2,1,0:T(8,128)} %copy-done.4, f32[4,320,128]{2,1,0:T(8,128)} %collective-permute-done.8.refs_1_, f32[4,320,128]{2,1,0:T(8,128)} %copy-done.11, f32[4,320,128]{2,1,0:T(8,128)} %copy-done.10, ...), custom_call_target="tpu_custom_call" | custom-call | tf_op jit(solution)/shard_map/pallas_call | solution.py:69
  148.7 6.0 %collective-permute-done.11 = f32[640,1280]{1,0:T(8,128)S(1)} collective-permute-done((f32[640,1280]{1,0:T(8,128)}, f32[640,1280]{1,0:T(8,128)S(1)}, u32[]{:S(2)}, u32[]{:S(2)}) %collective-permute-start.11) | collective-permute-done | bytes 3276832 | tf_op jit(solution)/shard_map/ppermute | solution.py:38
  154.7 4.0 %add.153 = f32[640,1280]{1,0:T(8,128)} add(f32[640,1280]{1,0:T(8,128)} %get-tuple-element.21, f32[640,1280]{1,0:T(8,128)S(1)} %collective-permute-done.11) | non-fusion elementwise | flops 819200 | bytes 9830400 | tf_op jit(solution)/shard_map/add | solution.py:261
  161.4 4.9 %shard_map.96 = f32[256,256]{1,0:T(8,128)} custom-call(s32[3]{0:T(128)} %pad_add_fusion.at, f32[640,256]{1,0:T(8,128)} %bitcast.40, f32[640,256]{1,0:T(8,128)} %copy-done.3), custom_call_target="tpu_custom_call" | custom-call | tf_op jit(solution)/shard_map/pallas_call | solution.py:69
  167.0 3.1 %collective-permute-done.13 = f32[208,256]{1,0:T(8,128)S(1)} collective-permute-done((f32[208,256]{1,0:T(8,128)S(1)}, f32[208,256]{1,0:T(8,128)S(1)}, u32[]{:S(2)}, u32[]{:S(2)}) %collective-permute-start.13) | collective-permute-done | bytes 213024 | tf_op jit(solution)/shard_map/ppermute | solution.py:34
  170.1 3.2 %collective-permute-done.12 = f32[208,256]{1,0:T(8,128)S(1)} collective-permute-done((f32[208,256]{1,0:T(8,128)S(1)}, f32[208,256]{1,0:T(8,128)S(1)}, u32[]{:S(2)}, u32[]{:S(2)}) %collective-permute-start.12) | collective-permute-done | bytes 213024 | tf_op jit(solution)/shard_map/ppermute | solution.py:34
  174.2 2.2 collective-permute-done.18
  178.3 13.5 %all_to_all.43 = f32[4,160,256]{2,1,0:T(8,128)S(1)} all-to-all(f32[4,160,256]{2,1,0:T(8,128)S(1)} %bitcast.45), channel_id=1, replica_groups=mesh['z'=8,'x'=4,'c'=2,'tp'=4] {'x'}, dimensions={0} | all-to-all | bytes 1310720 | tf_op jit(solution)/shard_map/all_to_all | solution.py:202
  191.9 13.3 %all_to_all.44 = f32[8,20,256]{2,1,0:T(8,128)S(1)} all-to-all(f32[8,20,256]{2,1,0:T(8,128)S(1)} %reshape.41), channel_id=1, replica_groups=mesh['z'=8,'x'=4,'c'=2,'tp'=4] {'z'}, dimensions={0} | all-to-all | bytes 327680 | tf_op jit(solution)/shard_map/all_to_all | solution.py:204
  205.2 12.4 %all_to_all.45 = f32[8,20,256]{2,1,0:T(8,128)S(1)} all-to-all(f32[8,20,256]{2,1,0:T(8,128)S(1)} %broadcast_in_dim.39), channel_id=1, replica_groups=mesh['z'=8,'x'=4,'c'=2,'tp'=4] {'z'}, dimensions={0} | all-to-all | bytes 327680 | tf_op jit(solution)/shard_map/all_to_all | solution.py:210
  218.5 4.2 %all-to-all-start.7 = ((f32[4,160,256]{2,1,0:T(8,128)}), f32[4,160,256]{2,1,0:T(8,128)S(1)}, u32[]{:S(2)}, u32[]{:S(2)}) async-start(f32[4,160,256]{2,1,0:T(8,128)} %broadcast_in_dim.41), calls=%async_computation.8 | async-start | bytes 1310720 | tf_op jit(solution)/shard_map/all_to_all | solution.py:210
  222.7 2.1 collective-permute-start.17
  226.6 3.4 %all-to-all-done.7 = f32[4,160,256]{2,1,0:T(8,128)S(1)} async-done(((f32[4,160,256]{2,1,0:T(8,128)}), f32[4,160,256]{2,1,0:T(8,128)S(1)}, u32[]{:S(2)}, u32[]{:S(2)}) %all-to-all-start.7) | async-done | bytes 655392 | tf_op jit(solution)/shard_map/all_to_all | solution.py:210
  230.0 3.1 %collective-permute-done.17 = f32[256,256]{1,0:T(8,128)S(1)} collective-permute-done((f32[256,256]{1,0:T(8,128)S(1)}, f32[256,256]{1,0:T(8,128)S(1)}, u32[]{:S(2)}, u32[]{:S(2)}) %collective-permute-start.17) | collective-permute-done | bytes 262176 | tf_op jit(solution)/shard_map/ppermute | solution.py:34
  234.2 2.7 collective-permute-done.15
  239.6 16.5 %shard_map.97 = (f32[256,512]{1,0:T(8,128)}, f32[256,256]{1,0:T(8,128)}) custom-call(s32[2]{0:T(128)} %iota_multiply_fusion.at, f32[256,512]{1,0:T(8,128)} %pad_maximum_fusion.5.work_in, f32[256,256]{1,0:T(8,128)} %broadcast_in_dim.38.done), custom_call_target="tpu_custom_call" | custom-call | tf_op jit(solution)/shard_map/pallas_call | solution.py:69
  256.1 9.8 %shard_map.98 = (f32[256,512]{1,0:T(8,128)}, f32[256,256]{1,0:T(8,128)}) custom-call(s32[2]{0:T(128)} %constant.67.clone.at, f32[256,512]{1,0:T(8,128)} %get-tuple-element.26.work_in, f32[256,256]{1,0:T(8,128)} %get-tuple-element.27.done), custom_call_target="tpu_custom_call" | custom-call | tf_op jit(solution)/shard_map/pallas_call | solution.py:69
  266.0 9.6 %shard_map.99 = (f32[256,512]{1,0:T(8,128)}, f32[256,256]{1,0:T(8,128)}) custom-call(s32[2]{0:T(128)} %constant.68.clone.at, f32[256,512]{1,0:T(8,128)} %get-tuple-element.28.work_in, f32[256,256]{1,0:T(8,128)} %get-tuple-element.29.done), custom_call_target="tpu_custom_call" | custom-call | tf_op jit(solution)/shard_map/pallas_call | solution.py:69
  (114 shorter events, 55.8 us)
Async XLA Ops:
  7.2 131.6 %all-gather.2.cloned.1.call-start = ((), (), s32[]{:S(2)}) async-start(), calls=%async_computation.9 | async-start | bytes 3276800 | tf_op jit(solution)/shard_map/all_gather | solution.py:230
  8.6 6.4 %copy-start.8 = (bf16[128,1280]{1,0:T(8,128)(2,1)S(1)}, bf16[128,1280]{1,0:T(8,128)(2,1)}, u32[]{:S(2)}) copy-start(bf16[128,1280]{1,0:T(8,128)(2,1)} %param.7) | copy-start | bytes 983044
  10.3 12.2 %collective-permute-start.2 = (f32[208,256]{1,0:T(8,128)S(1)}, f32[208,256]{1,0:T(8,128)S(1)}, u32[]{:S(2)}, u32[]{:S(2)}) collective-permute-start(f32[208,256]{1,0:T(8,128)S(1)} %fusion), channel_id=1, source_target_pairs={{0,3},{1,0},{2,1},{3,2},{4,7},{5,4},{6,5},{7,6},{8,11},{9,8},{10,9... | collective-permute-start | bytes 638984 | tf_op jit(solution)/shard_map/ppermute | solution.py:34
  13.4 9.7 %collective-permute-start.1 = (f32[208,256]{1,0:T(8,128)S(1)}, f32[208,256]{1,0:T(8,128)S(1)}, u32[]{:S(2)}, u32[]{:S(2)}) collective-permute-start(f32[208,256]{1,0:T(8,128)S(1)} %fusion), channel_id=1, source_target_pairs={{0,2},{1,3},{2,0},{3,1},{4,6},{5,7},{6,4},{7,5},{8,10},{9,11},{10,... | collective-permute-start | bytes 638984 | tf_op jit(solution)/shard_map/ppermute | solution.py:34
  14.0 12.3 %collective-permute-start = (f32[208,256]{1,0:T(8,128)S(1)}, f32[208,256]{1,0:T(8,128)}, u32[]{:S(2)}, u32[]{:S(2)}) collective-permute-start(f32[208,256]{1,0:T(8,128)S(1)} %fusion), channel_id=1, source_target_pairs={{0,1},{1,2},{2,3},{3,0},{4,5},{5,6},{6,7},{7,4},{8,9},{9,10},{10,1... | collective-permute-start | bytes 638984 | tf_op jit(solution)/shard_map/ppermute | solution.py:34
  29.0 2.4 collective-permute-start.3
  88.3 14.9 %all-to-all-start.3 = ((f32[4,160,256]{2,1,0:T(8,128)}), f32[4,160,256]{2,1,0:T(8,128)S(1)}, u32[]{:S(2)}, u32[]{:S(2)}) async-start(f32[4,160,256]{2,1,0:T(8,128)} %broadcast_in_dim.18), calls=%async_computation.3 | async-start | bytes 1310720 | tf_op jit(solution)/shard_map/all_to_all | solution.py:210
  93.2 196.2 %reduce-scatter.2.cloned.1.call-start = ((), (), s32[]{:S(2)}) async-start(), calls=%async_computation.10 | async-start | bytes 3686400 | tf_op jit(solution)/shard_map/reduce_scatter | solution.py:262
  98.5 7.4 %collective-permute-start.7 = (f32[320,128]{1,0:T(8,128)}, f32[320,128]{1,0:T(8,128)}, u32[]{:S(2)}, u32[]{:S(2)}) collective-permute-start(f32[320,128]{1,0:T(8,128)} %get-tuple-element.36), channel_id=1, source_target_pairs={{0,24},{8,0},{16,8},{24,16},{1,25},{9,1},{17,9},{25,17},{2,26},{10... | collective-permute-start | bytes 491528 | tf_op jit(solution)/shard_map/ppermute | solution.py:34
  98.6 9.1 %collective-permute-start.6 = (f32[320,128]{1,0:T(8,128)}, f32[320,128]{1,0:T(8,128)}, u32[]{:S(2)}, u32[]{:S(2)}) collective-permute-start(f32[320,128]{1,0:T(8,128)} %get-tuple-element.37), channel_id=1, source_target_pairs={{0,16},{8,24},{16,0},{24,8},{1,17},{9,25},{17,1},{25,9},{2,18},{10... | collective-permute-start | bytes 491528 | tf_op jit(solution)/shard_map/ppermute | solution.py:34
  101.4 6.5 %collective-permute-start.5 = (f32[320,128]{1,0:T(8,128)}, f32[320,128]{1,0:T(8,128)}, u32[]{:S(2)}, u32[]{:S(2)}) collective-permute-start(f32[320,128]{1,0:T(8,128)} %get-tuple-element.38), channel_id=1, source_target_pairs={{0,8},{8,16},{16,24},{24,0},{1,9},{9,17},{17,25},{25,1},{2,10},{10... | collective-permute-start | bytes 491528 | tf_op jit(solution)/shard_map/ppermute | solution.py:34
  103.2 8.6 %copy-start.2 = (f32[4,160,256]{2,1,0:T(8,128)}, f32[4,160,256]{2,1,0:T(8,128)S(1)}, u32[]{:S(2)}) copy-start(f32[4,160,256]{2,1,0:T(8,128)S(1)} %all-to-all-done.3) | copy-start | bytes 1966084
  103.2 8.1 %copy-start.7 = (f32[80,640]{1,0:T(8,128)S(1)}, f32[80,640]{1,0:T(8,128)}, u32[]{:S(2)}) copy-start(f32[80,640]{1,0:T(8,128)} %copy-done.6) | copy-start | bytes 614404
  103.2 8.6 %collective-permute-start.4 = (f32[640,256]{1,0:T(8,128)S(1)}, f32[640,256]{1,0:T(8,128)S(1)}, u32[]{:S(2)}, u32[]{:S(2)}) collective-permute-start(f32[640,256]{1,0:T(8,128)S(1)} %bitcast.38), channel_id=1, source_target_pairs={{0,4},{4,0},{1,5},{5,1},{2,6},{6,2},{3,7},{7,3},{8,12},{12,8},{9,1... | collective-permute-start | bytes 1966088 | tf_op jit(solution)/shard_map/ppermute | solution.py:38
  109.2 17.7 %collective-permute-start.10 = (f32[4,320,128]{2,1,0:T(8,128)S(1)}, f32[4,320,128]{2,1,0:T(8,128)S(1)}, u32[]{:S(2)}, u32[]{:S(2)}) collective-permute-start(f32[4,320,128]{2,1,0:T(8,128)S(1)} %pad_maximum_fusion.2.refs_0_), channel_id=1, source_target_pairs={{0,3},{1,0},{2,1},{3,2},{4,7},{5,4},{6,5},{7,6},{8,11},{9,8},{10,9... | collective-permute-start | bytes 1966088 | tf_op jit(solution)/shard_map/ppermute | solution.py:34
  109.9 19.1 %collective-permute-start.9 = (f32[4,320,128]{2,1,0:T(8,128)S(1)}, f32[4,320,128]{2,1,0:T(8,128)S(1)}, u32[]{:S(2)}, u32[]{:S(2)}) collective-permute-start(f32[4,320,128]{2,1,0:T(8,128)S(1)} %pad_maximum_fusion.2.refs_0_), channel_id=1, source_target_pairs={{0,2},{1,3},{2,0},{3,1},{4,6},{5,7},{6,4},{7,5},{8,10},{9,11},{10,... | collective-permute-start | bytes 1966088 | tf_op jit(solution)/shard_map/ppermute | solution.py:34
  110.5 28.3 %collective-permute-start.8 = (f32[4,320,128]{2,1,0:T(8,128)S(1)}, f32[4,320,128]{2,1,0:T(8,128)}, u32[]{:S(2)}, u32[]{:S(2)}) collective-permute-start(f32[4,320,128]{2,1,0:T(8,128)S(1)} %pad_maximum_fusion.2.refs_0_), channel_id=1, source_target_pairs={{0,1},{1,2},{2,3},{3,0},{4,5},{5,6},{6,7},{7,4},{8,9},{9,10},{10,1... | collective-permute-start | bytes 1966088 | tf_op jit(solution)/shard_map/ppermute | solution.py:34
  148.7 6.1 %collective-permute-start.11 = (f32[640,1280]{1,0:T(8,128)}, f32[640,1280]{1,0:T(8,128)S(1)}, u32[]{:S(2)}, u32[]{:S(2)}) collective-permute-start(f32[640,1280]{1,0:T(8,128)} %get-tuple-element.22), channel_id=1, source_target_pairs={{0,4},{4,0},{1,5},{5,1},{2,6},{6,2},{3,7},{7,3},{8,12},{12,8},{9,1... | collective-permute-start | bytes 9830408 | tf_op jit(solution)/shard_map/ppermute | solution.py:38
  158.8 8.2 %collective-permute-start.14 = (f32[208,256]{1,0:T(8,128)S(1)}, f32[208,256]{1,0:T(8,128)S(1)}, u32[]{:S(2)}, u32[]{:S(2)}) collective-permute-start(f32[208,256]{1,0:T(8,128)S(1)} %convolution_add_fusion.2), channel_id=1, source_target_pairs={{0,3},{1,0},{2,1},{3,2},{4,7},{5,4},{6,5},{7,6},{8,11},{9,8},{10,9... | collective-permute-start | bytes 638984 | tf_op jit(solution)/shard_map/ppermute | solution.py:34
  160.5 9.6 %collective-permute-start.13 = (f32[208,256]{1,0:T(8,128)S(1)}, f32[208,256]{1,0:T(8,128)S(1)}, u32[]{:S(2)}, u32[]{:S(2)}) collective-permute-start(f32[208,256]{1,0:T(8,128)S(1)} %convolution_add_fusion.2), channel_id=1, source_target_pairs={{0,2},{1,3},{2,0},{3,1},{4,6},{5,7},{6,4},{7,5},{8,10},{9,11},{10,... | collective-permute-start | bytes 638984 | tf_op jit(solution)/shard_map/ppermute | solution.py:34
  160.5 12.8 %collective-permute-start.12 = (f32[208,256]{1,0:T(8,128)S(1)}, f32[208,256]{1,0:T(8,128)S(1)}, u32[]{:S(2)}, u32[]{:S(2)}) collective-permute-start(f32[208,256]{1,0:T(8,128)S(1)} %convolution_add_fusion.2), channel_id=1, source_target_pairs={{0,1},{1,2},{2,3},{3,0},{4,5},{5,6},{6,7},{7,4},{8,9},{9,10},{10,1... | collective-permute-start | bytes 638984 | tf_op jit(solution)/shard_map/ppermute | solution.py:34
  161.4 11.9 %copy-start.1 = (f32[80,1280]{1,0:T(8,128)S(1)}, f32[80,1280]{1,0:T(8,128)}, u32[]{:S(2)}) copy-start(f32[80,1280]{1,0:T(8,128)} %param.9) | copy-start | bytes 1228804
  174.1 2.3 collective-permute-start.18
  217.6 5.1 %copy-start.9 = (f32[256,256]{1,0:T(8,128)S(1)}, f32[256,256]{1,0:T(8,128)}, u32[]{:S(2)}) copy-start(f32[256,256]{1,0:T(8,128)} %shard_map.96) | copy-start | bytes 786436
  218.5 11.5 %all-to-all-start.7 = ((f32[4,160,256]{2,1,0:T(8,128)}), f32[4,160,256]{2,1,0:T(8,128)S(1)}, u32[]{:S(2)}, u32[]{:S(2)}) async-start(f32[4,160,256]{2,1,0:T(8,128)} %broadcast_in_dim.41), calls=%async_computation.8 | async-start | bytes 1310720 | tf_op jit(solution)/shard_map/all_to_all | solution.py:210
  222.7 10.4 %collective-permute-start.17 = (f32[256,256]{1,0:T(8,128)S(1)}, f32[256,256]{1,0:T(8,128)S(1)}, u32[]{:S(2)}, u32[]{:S(2)}) collective-permute-start(f32[256,256]{1,0:T(8,128)S(1)} %copy-done.9), channel_id=1, source_target_pairs={{0,3},{1,0},{2,1},{3,2},{4,7},{5,4},{6,5},{7,6},{8,11},{9,8},{10,9... | collective-permute-start | bytes 786440 | tf_op jit(solution)/shard_map/ppermute | solution.py:34
  224.8 9.4 %collective-permute-start.16 = (f32[256,256]{1,0:T(8,128)S(1)}, f32[256,256]{1,0:T(8,128)}, u32[]{:S(2)}, u32[]{:S(2)}) collective-permute-start(f32[256,256]{1,0:T(8,128)S(1)} %copy-done.9), channel_id=1, source_target_pairs={{0,2},{1,3},{2,0},{3,1},{4,6},{5,7},{6,4},{7,5},{8,10},{9,11},{10,... | collective-permute-start | bytes 786440 | tf_op jit(solution)/shard_map/ppermute | solution.py:34
  225.3 11.6 %collective-permute-start.15 = (f32[256,256]{1,0:T(8,128)S(1)}, f32[256,256]{1,0:T(8,128)}, u32[]{:S(2)}, u32[]{:S(2)}) collective-permute-start(f32[256,256]{1,0:T(8,128)S(1)} %copy-done.9), channel_id=1, source_target_pairs={{0,1},{1,2},{2,3},{3,0},{4,5},{5,6},{6,7},{7,4},{8,9},{9,10},{10,1... | collective-permute-start | bytes 786440 | tf_op jit(solution)/shard_map/ppermute | solution.py:34
  230.0 48.4 %collective-permute-start.19 = (f32[640,256]{1,0:T(8,128)S(1)}, f32[640,256]{1,0:T(8,128)}, u32[]{:S(2)}, u32[]{:S(2)}) collective-permute-start(f32[640,256]{1,0:T(8,128)S(1)} %bitcast.41), channel_id=1, source_target_pairs={{0,4},{4,0},{1,5},{5,1},{2,6},{6,2},{3,7},{7,3},{8,12},{12,8},{9,1... | collective-permute-start | bytes 1966088 | tf_op jit(solution)/shard_map/ppermute | solution.py:38
  280.2 5.2 %collective-permute-start.21 = (f32[8,256]{1,0:T(8,128)S(1)}, f32[8,256]{1,0:T(8,128)S(1)}, u32[]{:S(2)}, u32[]{:S(2)}) collective-permute-start(f32[8,256]{1,0:T(8,128)S(1)} %broadcast_in_dim.42), channel_id=1, source_target_pairs={{0,2},{1,3},{2,0},{3,1},{4,6},{5,7},{6,4},{7,5},{8,10},{9,11},{10,... | collective-permute-start | bytes 24584 | tf_op jit(solution)/shard_map/ppermute | solution.py:34
  281.1 4.3 %collective-permute-start.22 = (f32[8,256]{1,0:T(8,128)S(1)}, f32[8,256]{1,0:T(8,128)S(1)}, u32[]{:S(2)}, u32[]{:S(2)}) collective-permute-start(f32[8,256]{1,0:T(8,128)S(1)} %broadcast_in_dim.42), channel_id=1, source_target_pairs={{0,3},{1,0},{2,1},{3,2},{4,7},{5,4},{6,5},{7,6},{8,11},{9,8},{10,9... | collective-permute-start | bytes 24584 | tf_op jit(solution)/shard_map/ppermute | solution.py:34
  282.4 4.9 %collective-permute-start.20 = (f32[8,256]{1,0:T(8,128)S(1)}, f32[8,256]{1,0:T(8,128)S(1)}, u32[]{:S(2)}, u32[]{:S(2)}) collective-permute-start(f32[8,256]{1,0:T(8,128)S(1)} %broadcast_in_dim.42), channel_id=1, source_target_pairs={{0,1},{1,2},{2,3},{3,0},{4,5},{5,6},{6,7},{7,4},{8,9},{9,10},{10,1... | collective-permute-start | bytes 24584 | tf_op jit(solution)/shard_map/ppermute | solution.py:34
  (8 other events, 16.2 us)
Sparse Core Ops, SparseCore 0:
  16.0 45.8 all-gather.1
  158.9 42.8 reduce-scatter.1

commit v5 on v3

--- a/solution.py
+++ b/solution.py
@@ -119,15 +119,22 @@
 
         def group(g, carry):
             state, pivots = carry
-            live = rows < EDGE - GROUP * g
-            for k in range(GROUP):
-                column = jnp.broadcast_to(state[:, k : k + 1], (EDGE, 2 * EDGE))
-                pivot = column[k : k + 1, :]
-                line = state[k : k + 1, :] / pivot
-                pivots = jnp.where(rows == k, jnp.broadcast_to(pivot, rows.shape), pivots)
-                state = state - jnp.where((rows > k) & live, column, 0.0) * line
-            state = jnp.concatenate([state[GROUP:], state[:GROUP]], axis=0)
-            pivots = jnp.concatenate([pivots[GROUP:], pivots[:GROUP]], axis=0)
+            columns = [jnp.broadcast_to(state[:, j : j + 1], rows.shape) for j in range(GROUP)]
+            heads = [state[j : j + 1, :] for j in range(GROUP)]
+            found = []
+            for j in range(GROUP):
+                pivot = columns[j][j : j + 1, :]
+                found.append(pivot)
+                inverse = 1.0 / pivot
+                line = heads[j] * inverse
+                for i in range(j + 1, GROUP):
+                    heads[i] = heads[i] - columns[j][i : i + 1, :] * line
+                    columns[i] = columns[i] - columns[j] * (columns[i][j : j + 1, :] * inverse)
+                below = jnp.where(rows[:GROUP] > j, columns[j][:GROUP], 0.0)
+                state = state - jnp.concatenate([below, columns[j][GROUP:]], axis=0) * line
+            head = jnp.where(lanes[:GROUP] < EDGE - GROUP * g, 0.0, state[:GROUP])
+            state = jnp.concatenate([state[GROUP:], head], axis=0)
+            pivots = jnp.concatenate([pivots[GROUP:], *found], axis=0)
             return pltpu.roll(state, 2 * EDGE - GROUP, 1), pivots
 
         state, pivots = lax.fori_loop(0, EDGE // GROUP, group, (state, pivots))
@@ -142,12 +149,12 @@
             work_ref[there, :] = pltpu.roll(left, 2 * R - EDGE, 1)
         return 0
 
-    lax.fori_loop(0, BLOCKS // 2, step, 0)
-
-
-def factor_step(first_block, work, done):
+    lax.fori_loop(0, at[1], step, 0)
+
+
+def factor_step(first_block, count, work, done):
     return call(
-        factor_kernel, jnp.full((1,), first_block, jnp.int32),
+        factor_kernel, jnp.array([first_block, count], jnp.int32),
         (shape(R, 2 * R), shape(R, R)), [whole((R, 2 * R)), whole((R, R))], work, done,
     )
 
@@ -191,9 +198,17 @@
     )
 
 
-def summed_piece(kept, given):
+def summed_at_once(kept, given):
     pieces = (kept + other_core(given)).reshape(NX * NZ, HALF // (NX * NZ), R)
     arrived = lax.all_to_all(pieces, ("x", "z"), 0, 0, tiled=True)
+    return jnp.sum(arrived, axis=0)
+
+
+def summed_in_turn(kept, given):
+    pieces = (kept + other_core(given)).reshape(NX, HALF // NX, R)
+    arrived = lax.all_to_all(pieces, "x", 0, 0, tiled=True)
+    pieces = jnp.sum(arrived, axis=0).reshape(NZ, HALF // (NX * NZ), R)
+    arrived = lax.all_to_all(pieces, "z", 0, 0, tiled=True)
     return jnp.sum(arrived, axis=0)
 
 
@@ -245,13 +260,13 @@
 
     given = near_dot(spreads[1], first, ((0,), (0,)))
     kept = near_dot(spreads[0], first, ((0,), (0,)))
-    piece = summed_piece(kept, given)
+    piece = summed_at_once(kept, given)
     piece, at_left = lax.optimization_barrier((piece, at))
     kept_grad, given_grad = core_products(at_left, outs, acts)
     near, far = gathered(piece)
+    seen = near_dot(spreads[0], near, ((1,), (0,))) + near_dot(spreads[1], far, ((1,), (0,)))
     summed_grad = kept_grad + other_core(given_grad)
     grad = lax.psum_scatter(summed_grad, "z", scatter_dimension=0, tiled=True)
-    seen = near_dot(spreads[0], near, ((1,), (0,))) + near_dot(spreads[1], far, ((1,), (0,)))
     second = over_tp(seen)
 
     gram = call(gram_kernel, at, shape(R, R), [whole((HALF, R))] * 2, near, far)
@@ -260,11 +275,11 @@
 
     given = near_dot(helds[1], second, ((0,), (0,)))
     kept = near_dot(helds[0], second, ((0,), (0,)))
-    piece = summed_piece(kept, given)
+    piece = summed_in_turn(kept, given)
     work = jnp.concatenate([gram, jnp.eye(R, dtype=F32)], axis=1)
-    work, done = factor_step(0, work, jnp.zeros((R, R), F32))
+    work, done = factor_step(0, 2, work, jnp.zeros((R, R), F32))
     near, far = gathered(piece)
-    _, inverse = factor_step(BLOCKS // 2, work, done)
+    _, inverse = factor_step(2, 2, work, done)
     basis = near_dot(second[TOKENS:], inverse, ((1,), (1,)))
     rights = [near_dot(v, inverse, ((1,), (1,))) for v in (near, far)]
     squares = sum(jnp.sum(v * v, axis=0) for v in rights)

time: 297 us -> 271 us (0.912)
  blocking collectives: 83.8 us -> 70.1 us
  Pallas kernels: 46.9 us -> 33.5 us
  waiting for transfers between devices: 72.9 us -> 77 us
    pallas_call x5, Pallas kernels: 46.9 us -> 33.5 us  [call(): pl.pallas_call(kernel, out_shape=out_shape, grid_spec=pltpu.PrefetchScala...]
    all_to_all x1 -> x2, blocking collectives: 34.9 us -> 26.6 us  [the longest x1 13.9 us: summed_in_turn(): arrived = lax.all_to_all(pieces, 'x', 0, 0, tiled=True)]
    ppermute x18, waiting for transfers between devices: 62.9 us -> 68.3 us  [shifted(): return lax.ppermute(v, axis, [(i, (i + k) % n) for i in range(n)])]
    all_to_all x3, blocking collectives: 48.9 us -> 43.5 us  [spread_over(): lax.all_to_all(copies, axis, 0, 0, tiled=True).reshape(-1, v.shape[1])]
  transfers between devices with their start and end apart: 27 -> 27, of which waited for: 18 -> 18; matrix products, arithmetic and copies ran while one was open for 11% -> 11% of each run, Pallas kernels for 13% -> 10%
where the time goes in v5:
time: 271 us; the launch traced here: 270 us
  waiting for transfers between devices  77 us (28%)
  blocking collectives  70.1 us (26%)
  starting transfers between devices  38.1 us (14%)
  Pallas kernels  33.5 us (12%)
  other arithmetic  15.7 us (6%)
  matrix products  15.4 us (6%)
  between operations  14.4 us (5%)
  local copies, waits for them, and re-layouts  5.76 us (2%)
    ppermute x18, waiting for transfers between devices, shifted(): return lax.ppermute(v, axis, [(i, (i + k) % n) for i in range(n)])  68.3 us
    all_to_all x3, blocking collectives, spread_over(): lax.all_to_all(copies, axis, 0, 0, tiled=True).reshape(-1, v.shape[1])  43.5 us
    pallas_call x5, Pallas kernels, call(): pl.pallas_call(kernel, out_shape=out_shape, grid_spec=pltpu.PrefetchScala...  33.5 us
    ppermute x18, starting transfers between devices, shifted(): return lax.ppermute(v, axis, [(i, (i + k) % n) for i in range(n)])  21.2 us
    dot_general x14, matrix products, near_dot(): lax.dot_general(a, b, (dims, ((), ())), precision=lax.Precision.HIGH, pre...  15.4 us
    all_to_all x1, blocking collectives, summed_in_turn(): arrived = lax.all_to_all(pieces, 'x', 0, 0, tiled=True)  13.9 us
    all_to_all x1, blocking collectives, summed_in_turn(): arrived = lax.all_to_all(pieces, 'z', 0, 0, tiled=True)  12.7 us
    all_to_all x1, starting transfers between devices, summed_at_once(): arrived = lax.all_to_all(pieces, ('x', 'z'), 0, 0, tiled=True)  11.6 us
  transfers between devices with their start and end apart: 27, of which 18 were waited for; matrix products, arithmetic and copies ran while one was open for 11% of the time, Pallas kernels for 10%

profile of v5, /device:TPU:2, one launch (start us, length us, event | category | flops | bytes accessed | tf_op | source)
XLA Modules:
  0.0 269.9 jit_solution(8750762556170769941)
XLA Ops:
  11.2 3.1 %collective-permute-start.2 = (f32[208,256]{1,0:T(8,128)S(1)}, f32[208,256]{1,0:T(8,128)S(1)}, u32[]{:S(2)}, u32[]{:S(2)}) collective-permute-start(f32[208,256]{1,0:T(8,128)S(1)} %fusion), channel_id=1, source_target_pairs={{0,3},{1,0},{2,1},{3,2},{4,7},{5,4},{6,5},{7,6},{8,11},{9,8},{10,9... | collective-permute-start | bytes 638984 | tf_op jit(solution)/shard_map/ppermute | solution.py:34
  17.1 6.3 %collective-permute-done.2 = f32[208,256]{1,0:T(8,128)S(1)} collective-permute-done((f32[208,256]{1,0:T(8,128)S(1)}, f32[208,256]{1,0:T(8,128)S(1)}, u32[]{:S(2)}, u32[]{:S(2)}) %collective-permute-start.2) | collective-permute-done | bytes 213024 | tf_op jit(solution)/shard_map/ppermute | solution.py:34
  24.0 3.2 %collective-permute-done = f32[208,256]{1,0:T(8,128)} collective-permute-done((f32[208,256]{1,0:T(8,128)S(1)}, f32[208,256]{1,0:T(8,128)}, u32[]{:S(2)}, u32[]{:S(2)}) %collective-permute-start) | collective-permute-done | bytes 213024 | tf_op jit(solution)/shard_map/ppermute | solution.py:34
  29.2 2.1 collective-permute-done.3
  31.3 1.9 convolution_add_fusion.1
  34.1 11.6 %all-to-all-start = ((f32[32,20,256]{2,1,0:T(8,128)}), f32[32,20,256]{2,1,0:T(8,128)S(1)}, u32[]{:S(2)}, u32[]{:S(2)}) async-start(f32[32,20,256]{2,1,0:T(8,128)} %reshape.33), calls=%async_computation | async-start | bytes 1572864 | tf_op jit(solution)/shard_map/all_to_all | solution.py:203
  46.4 2.6 shard_map.85
  50.5 2.7 collective-permute-start.5
  55.0 4.3 %collective-permute-done.6 = f32[320,128]{1,0:T(8,128)S(1)} collective-permute-done((f32[320,128]{1,0:T(8,128)S(1)}, f32[320,128]{1,0:T(8,128)S(1)}, u32[]{:S(2)}, u32[]{:S(2)}) %collective-permute-start.6) | collective-permute-done | bytes 163872 | tf_op jit(solution)/shard_map/ppermute | solution.py:34
  59.3 7.6 %collective-permute-done.5 = f32[320,128]{1,0:T(8,128)S(1)} collective-permute-done((f32[320,128]{1,0:T(8,128)S(1)}, f32[320,128]{1,0:T(8,128)S(1)}, u32[]{:S(2)}, u32[]{:S(2)}) %collective-permute-start.5) | collective-permute-done | bytes 163872 | tf_op jit(solution)/shard_map/ppermute | solution.py:34
  67.7 2.7 %collective-permute-start.9 = (f32[4,320,128]{2,1,0:T(8,128)}, f32[4,320,128]{2,1,0:T(8,128)}, u32[]{:S(2)}, u32[]{:S(2)}) collective-permute-start(f32[4,320,128]{2,1,0:T(8,128)} %pad_maximum_fusion.2.refs_0_), channel_id=1, source_target_pairs={{0,3},{1,0},{2,1},{3,2},{4,7},{5,4},{6,5},{7,6},{8,11},{9,8},{10,9... | collective-permute-start | bytes 1966088 | tf_op jit(solution)/shard_map/ppermute | solution.py:34
  72.2 26.6 %collective-permute-done.9.refs_3_ = f32[4,320,128]{2,1,0:T(8,128)} collective-permute-done((f32[4,320,128]{2,1,0:T(8,128)}, f32[4,320,128]{2,1,0:T(8,128)}, u32[]{:S(2)}, u32[]{:S(2)}) %collective-permute-start.9) | collective-permute-done | bytes 655392 | tf_op jit(solution)/shard_map/ppermute | solution.py:34
  98.9 3.7 %collective-permute-done.7.refs_1_ = f32[4,320,128]{2,1,0:T(8,128)} collective-permute-done((f32[4,320,128]{2,1,0:T(8,128)}, f32[4,320,128]{2,1,0:T(8,128)}, u32[]{:S(2)}, u32[]{:S(2)}) %collective-permute-start.7) | collective-permute-done | bytes 655392 | tf_op jit(solution)/shard_map/ppermute | solution.py:34
  102.6 7.8 %shard_map.86 = (f32[640,1280]{1,0:T(8,128)}, f32[640,1280]{1,0:T(8,128)}) custom-call(s32[3]{0:T(128)} %pad_add_fusion.at, f32[4,320,128]{2,1,0:T(8,128)} %pad_maximum_fusion.2.refs_0_, f32[4,320,128]{2,1,0:T(8,128)} %collective-permute-done.7.refs_1_, f32[4,320,128]{2,1,0:T(8,128)} %collective-permute-done.8.refs_2_, ...), custom_call_target="tpu_custom_call" | custom-call | tf_op jit(solution)/shard_map/pallas_call | solution.py:69
  110.4 18.0 %all_to_all.35 = f32[8,20,256]{2,1,0:T(8,128)S(1)} all-to-all(f32[8,20,256]{2,1,0:T(8,128)S(1)} %broadcast_in_dim.16), channel_id=1, replica_groups=mesh['z'=8,'x'=4,'c'=2,'tp'=4] {'z'}, dimensions={0} | all-to-all | bytes 327680 | tf_op jit(solution)/shard_map/all_to_all | solution.py:217
  128.5 13.4 %all_to_all.36 = f32[4,160,256]{2,1,0:T(8,128)S(1)} all-to-all(f32[4,160,256]{2,1,0:T(8,128)S(1)} %broadcast_in_dim.18), channel_id=1, replica_groups=mesh['z'=8,'x'=4,'c'=2,'tp'=4] {'x'}, dimensions={0} | all-to-all | bytes 1310720 | tf_op jit(solution)/shard_map/all_to_all | solution.py:217
  143.0 4.0 %add.152 = f32[640,1280]{1,0:T(8,128)} add(f32[640,1280]{1,0:T(8,128)S(1)} %copy-done.3, f32[640,1280]{1,0:T(8,128)} %collective-permute-done.10) | non-fusion elementwise | flops 819200 | bytes 9830400 | tf_op jit(solution)/shard_map/add | solution.py:268
  151.9 5.0 %shard_map.87 = f32[256,256]{1,0:T(8,128)} custom-call(s32[3]{0:T(128)} %pad_add_fusion.at, f32[640,256]{1,0:T(8,128)} %bitcast.39, f32[640,256]{1,0:T(8,128)} %collective-permute-done.11.far), custom_call_target="tpu_custom_call" | custom-call | tf_op jit(solution)/shard_map/pallas_call | solution.py:69
  157.8 2.2 collective-permute-done.13
  160.0 3.8 %collective-permute-done.12 = f32[208,256]{1,0:T(8,128)S(1)} collective-permute-done((f32[208,256]{1,0:T(8,128)S(1)}, f32[208,256]{1,0:T(8,128)S(1)}, u32[]{:S(2)}, u32[]{:S(2)}) %collective-permute-start.12) | collective-permute-done | bytes 213024 | tf_op jit(solution)/shard_map/ppermute | solution.py:34
  164.8 2.1 collective-permute-done.18
  166.9 1.9 convolution_add_fusion
  168.8 13.9 %all_to_all.37 = f32[4,160,256]{2,1,0:T(8,128)S(1)} all-to-all(f32[4,160,256]{2,1,0:T(8,128)S(1)} %bitcast.43), channel_id=1, replica_groups=mesh['z'=8,'x'=4,'c'=2,'tp'=4] {'x'}, dimensions={0} | all-to-all | bytes 1310720 | tf_op jit(solution)/shard_map/all_to_all | solution.py:209
  182.7 12.7 %all_to_all.38 = f32[8,20,256]{2,1,0:T(8,128)S(1)} all-to-all(f32[8,20,256]{2,1,0:T(8,128)S(1)} %reshape.37), channel_id=1, replica_groups=mesh['z'=8,'x'=4,'c'=2,'tp'=4] {'z'}, dimensions={0} | all-to-all | bytes 327680 | tf_op jit(solution)/shard_map/all_to_all | solution.py:211
  195.5 12.2 %all_to_all.39 = f32[8,20,256]{2,1,0:T(8,128)S(1)} all-to-all(f32[8,20,256]{2,1,0:T(8,128)S(1)} %broadcast_in_dim.39), channel_id=1, replica_groups=mesh['z'=8,'x'=4,'c'=2,'tp'=4] {'z'}, dimensions={0} | all-to-all | bytes 327680 | tf_op jit(solution)/shard_map/all_to_all | solution.py:217
  208.6 4.8 %all-to-all-start.6 = ((f32[4,160,256]{2,1,0:T(8,128)}), f32[4,160,256]{2,1,0:T(8,128)S(1)}, u32[]{:S(2)}, u32[]{:S(2)}) async-start(f32[4,160,256]{2,1,0:T(8,128)} %broadcast_in_dim.41), calls=%async_computation.7 | async-start | bytes 1310720 | tf_op jit(solution)/shard_map/all_to_all | solution.py:217
  216.2 4.5 %all-to-all-done.6 = f32[4,160,256]{2,1,0:T(8,128)S(1)} async-done(((f32[4,160,256]{2,1,0:T(8,128)}), f32[4,160,256]{2,1,0:T(8,128)S(1)}, u32[]{:S(2)}, u32[]{:S(2)}) %all-to-all-start.6) | async-done | bytes 655392 | tf_op jit(solution)/shard_map/all_to_all | solution.py:217
  221.0 2.8 %collective-permute-done.16 = f32[256,256]{1,0:T(8,128)} collective-permute-done((f32[256,256]{1,0:T(8,128)S(1)}, f32[256,256]{1,0:T(8,128)}, u32[]{:S(2)}, u32[]{:S(2)}) %collective-permute-start.16) | collective-permute-done | bytes 262176 | tf_op jit(solution)/shard_map/ppermute | solution.py:34
  223.8 2.6 collective-permute-done.15
  229.1 9.0 %shard_map.88 = (f32[256,512]{1,0:T(8,128)}, f32[256,256]{1,0:T(8,128)}) custom-call(s32[2]{0:T(128)} %iota_multiply_fusion.at, f32[256,512]{1,0:T(8,128)} %pad_maximum_fusion.5.work_in, f32[256,256]{1,0:T(8,128)} %broadcast_in_dim.38.done), custom_call_target="tpu_custom_call" | custom-call | tf_op jit(solution)/shard_map/pallas_call | solution.py:69
  238.5 9.2 %shard_map.89 = (f32[256,512]{1,0:T(8,128)}, f32[256,256]{1,0:T(8,128)}) custom-call(s32[2]{0:T(128)} %call_exported.1.at, f32[256,512]{1,0:T(8,128)} %get-tuple-element.24.work_in, f32[256,256]{1,0:T(8,128)} %get-tuple-element.25.done), custom_call_target="tpu_custom_call" | custom-call | tf_op jit(solution)/shard_map/pallas_call | solution.py:69
  255.7 1.9 collective-permute-done.21
  (110 shorter events, 45.6 us)
Async XLA Ops:
  7.2 95.4 %all-gather.2.cloned.1.call-start = ((), (), s32[]{:S(2)}) async-start(), calls=%async_computation.8 | async-start | bytes 3276800 | tf_op jit(solution)/shard_map/all_gather | solution.py:237
  11.2 12.2 %collective-permute-start.2 = (f32[208,256]{1,0:T(8,128)S(1)}, f32[208,256]{1,0:T(8,128)S(1)}, u32[]{:S(2)}, u32[]{:S(2)}) collective-permute-start(f32[208,256]{1,0:T(8,128)S(1)} %fusion), channel_id=1, source_target_pairs={{0,3},{1,0},{2,1},{3,2},{4,7},{5,4},{6,5},{7,6},{8,11},{9,8},{10,9... | collective-permute-start | bytes 638984 | tf_op jit(solution)/shard_map/ppermute | solution.py:34
  14.3 9.7 %collective-permute-start.1 = (f32[208,256]{1,0:T(8,128)S(1)}, f32[208,256]{1,0:T(8,128)S(1)}, u32[]{:S(2)}, u32[]{:S(2)}) collective-permute-start(f32[208,256]{1,0:T(8,128)S(1)} %fusion), channel_id=1, source_target_pairs={{0,2},{1,3},{2,0},{3,1},{4,6},{5,7},{6,4},{7,5},{8,10},{9,11},{10,... | collective-permute-start | bytes 638984 | tf_op jit(solution)/shard_map/ppermute | solution.py:34
  14.9 12.3 %collective-permute-start = (f32[208,256]{1,0:T(8,128)S(1)}, f32[208,256]{1,0:T(8,128)}, u32[]{:S(2)}, u32[]{:S(2)}) collective-permute-start(f32[208,256]{1,0:T(8,128)S(1)} %fusion), channel_id=1, source_target_pairs={{0,1},{1,2},{2,3},{3,0},{4,5},{5,6},{6,7},{7,4},{8,9},{9,10},{10,1... | collective-permute-start | bytes 638984 | tf_op jit(solution)/shard_map/ppermute | solution.py:34
  17.0 12.0 %copy-start.4 = (f32[128,640]{1,0:T(8,128)}, f32[128,640]{1,0:T(8,128)S(1)}, u32[]{:S(2)}) copy-start(f32[128,640]{1,0:T(8,128)S(1)} %get-tuple-element.30) | copy-start | bytes 983044
  29.0 2.3 collective-permute-start.3
  34.1 38.0 %all-to-all-start = ((f32[32,20,256]{2,1,0:T(8,128)}), f32[32,20,256]{2,1,0:T(8,128)S(1)}, u32[]{:S(2)}, u32[]{:S(2)}) async-start(f32[32,20,256]{2,1,0:T(8,128)} %reshape.33), calls=%async_computation | async-start | bytes 1572864 | tf_op jit(solution)/shard_map/all_to_all | solution.py:203
  45.7 215.5 %reduce-scatter.2.cloned.1.call-start = ((), (), s32[]{:S(2)}) async-start(), calls=%async_computation.9 | async-start | bytes 3686400 | tf_op jit(solution)/shard_map/reduce_scatter | solution.py:269
  50.2 9.1 %collective-permute-start.6 = (f32[320,128]{1,0:T(8,128)S(1)}, f32[320,128]{1,0:T(8,128)S(1)}, u32[]{:S(2)}, u32[]{:S(2)}) collective-permute-start(f32[320,128]{1,0:T(8,128)S(1)} %get-tuple-element.32), channel_id=1, source_target_pairs={{0,24},{8,0},{16,8},{24,16},{1,25},{9,1},{17,9},{25,17},{2,26},{10... | collective-permute-start | bytes 491528 | tf_op jit(solution)/shard_map/ppermute | solution.py:34
  50.5 16.4 %collective-permute-start.5 = (f32[320,128]{1,0:T(8,128)S(1)}, f32[320,128]{1,0:T(8,128)S(1)}, u32[]{:S(2)}, u32[]{:S(2)}) collective-permute-start(f32[320,128]{1,0:T(8,128)S(1)} %get-tuple-element.33), channel_id=1, source_target_pairs={{0,16},{8,24},{16,0},{24,8},{1,17},{9,25},{17,1},{25,9},{2,18},{10... | collective-permute-start | bytes 491528 | tf_op jit(solution)/shard_map/ppermute | solution.py:34
  53.2 13.7 %collective-permute-start.4 = (f32[320,128]{1,0:T(8,128)S(1)}, f32[320,128]{1,0:T(8,128)S(1)}, u32[]{:S(2)}, u32[]{:S(2)}) collective-permute-start(f32[320,128]{1,0:T(8,128)S(1)} %get-tuple-element.34), channel_id=1, source_target_pairs={{0,8},{8,16},{16,24},{24,0},{1,9},{9,17},{17,25},{25,1},{2,10},{10... | collective-permute-start | bytes 491528 | tf_op jit(solution)/shard_map/ppermute | solution.py:34
  67.7 31.1 %collective-permute-start.9 = (f32[4,320,128]{2,1,0:T(8,128)}, f32[4,320,128]{2,1,0:T(8,128)}, u32[]{:S(2)}, u32[]{:S(2)}) collective-permute-start(f32[4,320,128]{2,1,0:T(8,128)} %pad_maximum_fusion.2.refs_0_), channel_id=1, source_target_pairs={{0,3},{1,0},{2,1},{3,2},{4,7},{5,4},{6,5},{7,6},{8,11},{9,8},{10,9... | collective-permute-start | bytes 1966088 | tf_op jit(solution)/shard_map/ppermute | solution.py:34
  70.5 28.4 %collective-permute-start.8 = (f32[4,320,128]{2,1,0:T(8,128)}, f32[4,320,128]{2,1,0:T(8,128)}, u32[]{:S(2)}, u32[]{:S(2)}) collective-permute-start(f32[4,320,128]{2,1,0:T(8,128)} %pad_maximum_fusion.2.refs_0_), channel_id=1, source_target_pairs={{0,2},{1,3},{2,0},{3,1},{4,6},{5,7},{6,4},{7,5},{8,10},{9,11},{10,... | collective-permute-start | bytes 1966088 | tf_op jit(solution)/shard_map/ppermute | solution.py:34
  71.3 31.3 %collective-permute-start.7 = (f32[4,320,128]{2,1,0:T(8,128)}, f32[4,320,128]{2,1,0:T(8,128)}, u32[]{:S(2)}, u32[]{:S(2)}) collective-permute-start(f32[4,320,128]{2,1,0:T(8,128)} %pad_maximum_fusion.2.refs_0_), channel_id=1, source_target_pairs={{0,1},{1,2},{2,3},{3,0},{4,5},{5,6},{6,7},{7,4},{8,9},{9,10},{10,1... | collective-permute-start | bytes 1966088 | tf_op jit(solution)/shard_map/ppermute | solution.py:34
  110.3 32.6 %collective-permute-start.10 = (f32[640,1280]{1,0:T(8,128)}, f32[640,1280]{1,0:T(8,128)}, u32[]{:S(2)}, u32[]{:S(2)}) collective-permute-start(f32[640,1280]{1,0:T(8,128)} %get-tuple-element.20), channel_id=1, source_target_pairs={{0,4},{4,0},{1,5},{5,1},{2,6},{6,2},{3,7},{7,3},{8,12},{12,8},{9,1... | collective-permute-start | bytes 9830408 | tf_op jit(solution)/shard_map/ppermute | solution.py:38
  128.4 13.5 %copy-start.8 = (f32[80,640]{1,0:T(8,128)S(1)}, f32[80,640]{1,0:T(8,128)}, u32[]{:S(2)}) copy-start(f32[80,640]{1,0:T(8,128)} %copy-done.7) | copy-start | bytes 614404
  128.4 14.6 %copy-start.3 = (f32[640,1280]{1,0:T(8,128)S(1)}, f32[640,1280]{1,0:T(8,128)}, u32[]{:S(2)}) copy-start(f32[640,1280]{1,0:T(8,128)} %get-tuple-element.19) | copy-start | bytes 9830404
  141.8 5.2 %collective-permute-start.11 = (f32[640,256]{1,0:T(8,128)S(1)}, f32[640,256]{1,0:T(8,128)}, u32[]{:S(2)}, u32[]{:S(2)}) collective-permute-start(f32[640,256]{1,0:T(8,128)S(1)} %bitcast.37), channel_id=1, source_target_pairs={{0,4},{4,0},{1,5},{5,1},{2,6},{6,2},{3,7},{7,3},{8,12},{12,8},{9,1... | collective-permute-start | bytes 1966088 | tf_op jit(solution)/shard_map/ppermute | solution.py:38
  149.6 8.2 %collective-permute-start.14 = (f32[208,256]{1,0:T(8,128)S(1)}, f32[208,256]{1,0:T(8,128)S(1)}, u32[]{:S(2)}, u32[]{:S(2)}) collective-permute-start(f32[208,256]{1,0:T(8,128)S(1)} %convolution_add_fusion.2), channel_id=1, source_target_pairs={{0,3},{1,0},{2,1},{3,2},{4,7},{5,4},{6,5},{7,6},{8,11},{9,8},{10,9... | collective-permute-start | bytes 638984 | tf_op jit(solution)/shard_map/ppermute | solution.py:34
  150.3 9.7 %collective-permute-start.13 = (f32[208,256]{1,0:T(8,128)S(1)}, f32[208,256]{1,0:T(8,128)S(1)}, u32[]{:S(2)}, u32[]{:S(2)}) collective-permute-start(f32[208,256]{1,0:T(8,128)S(1)} %convolution_add_fusion.2), channel_id=1, source_target_pairs={{0,2},{1,3},{2,0},{3,1},{4,6},{5,7},{6,4},{7,5},{8,10},{9,11},{10,... | collective-permute-start | bytes 638984 | tf_op jit(solution)/shard_map/ppermute | solution.py:34
  151.1 12.7 %collective-permute-start.12 = (f32[208,256]{1,0:T(8,128)S(1)}, f32[208,256]{1,0:T(8,128)S(1)}, u32[]{:S(2)}, u32[]{:S(2)}) collective-permute-start(f32[208,256]{1,0:T(8,128)S(1)} %convolution_add_fusion.2), channel_id=1, source_target_pairs={{0,1},{1,2},{2,3},{3,0},{4,5},{5,6},{6,7},{7,4},{8,9},{9,10},{10,1... | collective-permute-start | bytes 638984 | tf_op jit(solution)/shard_map/ppermute | solution.py:34
  151.9 11.9 %copy-start.1 = (f32[80,1280]{1,0:T(8,128)S(1)}, f32[80,1280]{1,0:T(8,128)}, u32[]{:S(2)}) copy-start(f32[80,1280]{1,0:T(8,128)} %param.8) | copy-start | bytes 1228804
  164.6 2.3 collective-permute-start.18
  207.7 5.7 %copy-start.10 = (f32[256,256]{1,0:T(8,128)S(1)}, f32[256,256]{1,0:T(8,128)}, u32[]{:S(2)}) copy-start(f32[256,256]{1,0:T(8,128)} %shard_map.87) | copy-start | bytes 786436
  208.6 12.1 %all-to-all-start.6 = ((f32[4,160,256]{2,1,0:T(8,128)}), f32[4,160,256]{2,1,0:T(8,128)S(1)}, u32[]{:S(2)}, u32[]{:S(2)}) async-start(f32[4,160,256]{2,1,0:T(8,128)} %broadcast_in_dim.41), calls=%async_computation.7 | async-start | bytes 1310720 | tf_op jit(solution)/shard_map/all_to_all | solution.py:217
  213.4 7.6 %collective-permute-start.17 = (f32[256,256]{1,0:T(8,128)S(1)}, f32[256,256]{1,0:T(8,128)S(1)}, u32[]{:S(2)}, u32[]{:S(2)}) collective-permute-start(f32[256,256]{1,0:T(8,128)S(1)} %copy-done.10), channel_id=1, source_target_pairs={{0,3},{1,0},{2,1},{3,2},{4,7},{5,4},{6,5},{7,6},{8,11},{9,8},{10,9... | collective-permute-start | bytes 786440 | tf_op jit(solution)/shard_map/ppermute | solution.py:34
  214.2 9.6 %collective-permute-start.16 = (f32[256,256]{1,0:T(8,128)S(1)}, f32[256,256]{1,0:T(8,128)}, u32[]{:S(2)}, u32[]{:S(2)}) collective-permute-start(f32[256,256]{1,0:T(8,128)S(1)} %copy-done.10), channel_id=1, source_target_pairs={{0,2},{1,3},{2,0},{3,1},{4,6},{5,7},{6,4},{7,5},{8,10},{9,11},{10,... | collective-permute-start | bytes 786440 | tf_op jit(solution)/shard_map/ppermute | solution.py:34
  214.5 11.9 %collective-permute-start.15 = (f32[256,256]{1,0:T(8,128)S(1)}, f32[256,256]{1,0:T(8,128)}, u32[]{:S(2)}, u32[]{:S(2)}) collective-permute-start(f32[256,256]{1,0:T(8,128)S(1)} %copy-done.10), channel_id=1, source_target_pairs={{0,1},{1,2},{2,3},{3,0},{4,5},{5,6},{6,7},{7,4},{8,9},{9,10},{10,1... | collective-permute-start | bytes 786440 | tf_op jit(solution)/shard_map/ppermute | solution.py:34
  220.7 29.9 %collective-permute-start.19 = (f32[640,256]{1,0:T(8,128)S(1)}, f32[640,256]{1,0:T(8,128)}, u32[]{:S(2)}, u32[]{:S(2)}) collective-permute-start(f32[640,256]{1,0:T(8,128)S(1)} %bitcast.40), channel_id=1, source_target_pairs={{0,4},{4,0},{1,5},{5,1},{2,6},{6,2},{3,7},{7,3},{8,12},{12,8},{9,1... | collective-permute-start | bytes 1966088 | tf_op jit(solution)/shard_map/ppermute | solution.py:38
  252.3 5.2 %collective-permute-start.21 = (f32[8,256]{1,0:T(8,128)S(1)}, f32[8,256]{1,0:T(8,128)S(1)}, u32[]{:S(2)}, u32[]{:S(2)}) collective-permute-start(f32[8,256]{1,0:T(8,128)S(1)} %broadcast_in_dim.42), channel_id=1, source_target_pairs={{0,2},{1,3},{2,0},{3,1},{4,6},{5,7},{6,4},{7,5},{8,10},{9,11},{10,... | collective-permute-start | bytes 24584 | tf_op jit(solution)/shard_map/ppermute | solution.py:34
  253.0 4.6 %collective-permute-start.22 = (f32[8,256]{1,0:T(8,128)S(1)}, f32[8,256]{1,0:T(8,128)S(1)}, u32[]{:S(2)}, u32[]{:S(2)}) collective-permute-start(f32[8,256]{1,0:T(8,128)S(1)} %broadcast_in_dim.42), channel_id=1, source_target_pairs={{0,3},{1,0},{2,1},{3,2},{4,7},{5,4},{6,5},{7,6},{8,11},{9,8},{10,9... | collective-permute-start | bytes 24584 | tf_op jit(solution)/shard_map/ppermute | solution.py:34
  254.2 4.9 %collective-permute-start.20 = (f32[8,256]{1,0:T(8,128)S(1)}, f32[8,256]{1,0:T(8,128)S(1)}, u32[]{:S(2)}, u32[]{:S(2)}) collective-permute-start(f32[8,256]{1,0:T(8,128)S(1)} %broadcast_in_dim.42), channel_id=1, source_target_pairs={{0,1},{1,2},{2,3},{3,0},{4,5},{5,6},{6,7},{7,4},{8,9},{9,10},{10,1... | collective-permute-start | bytes 24584 | tf_op jit(solution)/shard_map/ppermute | solution.py:34
  (7 other events, 15.3 us)
Sparse Core Ops, SparseCore 0:
  11.3 41.9 all-gather.1
  147.2 40.6 reduce-scatter.1

commit v6 on v5

--- a/solution.py
+++ b/solution.py
@@ -276,8 +276,9 @@
     given = near_dot(helds[1], second, ((0,), (0,)))
     kept = near_dot(helds[0], second, ((0,), (0,)))
     piece = summed_in_turn(kept, given)
-    work = jnp.concatenate([gram, jnp.eye(R, dtype=F32)], axis=1)
-    work, done = factor_step(0, 2, work, jnp.zeros((R, R), F32))
+    identity = jnp.eye(R, dtype=F32)
+    work = jnp.concatenate([gram, identity], axis=1)
+    work, done = factor_step(0, 2, work, identity)
     near, far = gathered(piece)
     _, inverse = factor_step(2, 2, work, done)
     basis = near_dot(second[TOKENS:], inverse, ((1,), (1,)))

time: 271 us -> 270 us (level)
  no operation moved by 1% of the time
where the time goes in v6:
time: 270 us; the launch traced here: 269 us
  waiting for transfers between devices  77.3 us (29%)
  blocking collectives  70 us (26%)
  starting transfers between devices  38 us (14%)
  Pallas kernels  33.5 us (12%)
  other arithmetic  15.7 us (6%)
  matrix products  15.4 us (6%)
  between operations  14.4 us (5%)
  local copies, waits for them, and re-layouts  5.05 us (2%)
    ppermute x18, waiting for transfers between devices, shifted(): return lax.ppermute(v, axis, [(i, (i + k) % n) for i in range(n)])  68.3 us
    all_to_all x3, blocking collectives, spread_over(): lax.all_to_all(copies, axis, 0, 0, tiled=True).reshape(-1, v.shape[1])  43.6 us
    pallas_call x5, Pallas kernels, call(): pl.pallas_call(kernel, out_shape=out_shape, grid_spec=pltpu.PrefetchScala...  33.5 us
    ppermute x18, starting transfers between devices, shifted(): return lax.ppermute(v, axis, [(i, (i + k) % n) for i in range(n)])  21.1 us
    dot_general x14, matrix products, near_dot(): lax.dot_general(a, b, (dims, ((), ())), precision=lax.Precision.HIGH, pre...  15.4 us
    all_to_all x1, blocking collectives, summed_in_turn(): arrived = lax.all_to_all(pieces, 'x', 0, 0, tiled=True)  13.9 us
    all_to_all x1, blocking collectives, summed_in_turn(): arrived = lax.all_to_all(pieces, 'z', 0, 0, tiled=True)  12.6 us
    all_to_all x1, starting transfers between devices, summed_at_once(): arrived = lax.all_to_all(pieces, ('x', 'z'), 0, 0, tiled=True)  11.6 us
  transfers between devices with their start and end apart: 27, of which 18 were waited for; matrix products, arithmetic and copies ran while one was open for 11% of the time, Pallas kernels for 10%

profile of v6, /device:TPU:2, one launch (start us, length us, event | category | flops | bytes accessed | tf_op | source)
XLA Modules:
  0.0 269.4 jit_solution(3871230318247432328)
XLA Ops:
  11.2 3.1 %collective-permute-start.2 = (f32[208,256]{1,0:T(8,128)S(1)}, f32[208,256]{1,0:T(8,128)S(1)}, u32[]{:S(2)}, u32[]{:S(2)}) collective-permute-start(f32[208,256]{1,0:T(8,128)S(1)} %fusion), channel_id=1, source_target_pairs={{0,3},{1,0},{2,1},{3,2},{4,7},{5,4},{6,5},{7,6},{8,11},{9,8},{10,9... | collective-permute-start | bytes 638984 | tf_op jit(solution)/shard_map/ppermute | solution.py:34
  17.1 6.3 %collective-permute-done.2 = f32[208,256]{1,0:T(8,128)S(1)} collective-permute-done((f32[208,256]{1,0:T(8,128)S(1)}, f32[208,256]{1,0:T(8,128)S(1)}, u32[]{:S(2)}, u32[]{:S(2)}) %collective-permute-start.2) | collective-permute-done | bytes 213024 | tf_op jit(solution)/shard_map/ppermute | solution.py:34
  24.0 3.2 %collective-permute-done = f32[208,256]{1,0:T(8,128)} collective-permute-done((f32[208,256]{1,0:T(8,128)S(1)}, f32[208,256]{1,0:T(8,128)}, u32[]{:S(2)}, u32[]{:S(2)}) %collective-permute-start) | collective-permute-done | bytes 213024 | tf_op jit(solution)/shard_map/ppermute | solution.py:34
  29.2 2.1 collective-permute-done.3
  31.3 1.9 convolution_add_fusion.1
  34.1 11.6 %all-to-all-start = ((f32[32,20,256]{2,1,0:T(8,128)}), f32[32,20,256]{2,1,0:T(8,128)S(1)}, u32[]{:S(2)}, u32[]{:S(2)}) async-start(f32[32,20,256]{2,1,0:T(8,128)} %reshape.33), calls=%async_computation | async-start | bytes 1572864 | tf_op jit(solution)/shard_map/all_to_all | solution.py:203
  46.4 2.6 shard_map.85
  50.5 2.7 %collective-permute-start.5 = (f32[320,128]{1,0:T(8,128)S(1)}, f32[320,128]{1,0:T(8,128)S(1)}, u32[]{:S(2)}, u32[]{:S(2)}) collective-permute-start(f32[320,128]{1,0:T(8,128)S(1)} %get-tuple-element.33), channel_id=1, source_target_pairs={{0,16},{8,24},{16,0},{24,8},{1,17},{9,25},{17,1},{25,9},{2,18},{10... | collective-permute-start | bytes 491528 | tf_op jit(solution)/shard_map/ppermute | solution.py:34
  55.0 4.2 %collective-permute-done.6 = f32[320,128]{1,0:T(8,128)S(1)} collective-permute-done((f32[320,128]{1,0:T(8,128)S(1)}, f32[320,128]{1,0:T(8,128)S(1)}, u32[]{:S(2)}, u32[]{:S(2)}) %collective-permute-start.6) | collective-permute-done | bytes 163872 | tf_op jit(solution)/shard_map/ppermute | solution.py:34
  59.3 7.6 %collective-permute-done.5 = f32[320,128]{1,0:T(8,128)S(1)} collective-permute-done((f32[320,128]{1,0:T(8,128)S(1)}, f32[320,128]{1,0:T(8,128)S(1)}, u32[]{:S(2)}, u32[]{:S(2)}) %collective-permute-start.5) | collective-permute-done | bytes 163872 | tf_op jit(solution)/shard_map/ppermute | solution.py:34
  67.7 2.7 %collective-permute-start.9 = (f32[4,320,128]{2,1,0:T(8,128)}, f32[4,320,128]{2,1,0:T(8,128)}, u32[]{:S(2)}, u32[]{:S(2)}) collective-permute-start(f32[4,320,128]{2,1,0:T(8,128)} %pad_maximum_fusion.2.refs_0_), channel_id=1, source_target_pairs={{0,3},{1,0},{2,1},{3,2},{4,7},{5,4},{6,5},{7,6},{8,11},{9,8},{10,9... | collective-permute-start | bytes 1966088 | tf_op jit(solution)/shard_map/ppermute | solution.py:34
  72.2 26.6 %collective-permute-done.9.refs_3_ = f32[4,320,128]{2,1,0:T(8,128)} collective-permute-done((f32[4,320,128]{2,1,0:T(8,128)}, f32[4,320,128]{2,1,0:T(8,128)}, u32[]{:S(2)}, u32[]{:S(2)}) %collective-permute-start.9) | collective-permute-done | bytes 655392 | tf_op jit(solution)/shard_map/ppermute | solution.py:34
  98.9 3.7 %collective-permute-done.7.refs_1_ = f32[4,320,128]{2,1,0:T(8,128)} collective-permute-done((f32[4,320,128]{2,1,0:T(8,128)}, f32[4,320,128]{2,1,0:T(8,128)}, u32[]{:S(2)}, u32[]{:S(2)}) %collective-permute-start.7) | collective-permute-done | bytes 655392 | tf_op jit(solution)/shard_map/ppermute | solution.py:34
  102.6 7.8 %shard_map.86 = (f32[640,1280]{1,0:T(8,128)}, f32[640,1280]{1,0:T(8,128)}) custom-call(s32[3]{0:T(128)} %pad_add_fusion.at, f32[4,320,128]{2,1,0:T(8,128)} %pad_maximum_fusion.2.refs_0_, f32[4,320,128]{2,1,0:T(8,128)} %collective-permute-done.7.refs_1_, f32[4,320,128]{2,1,0:T(8,128)} %collective-permute-done.8.refs_2_, ...), custom_call_target="tpu_custom_call" | custom-call | tf_op jit(solution)/shard_map/pallas_call | solution.py:69
  110.4 18.0 %all_to_all.35 = f32[8,20,256]{2,1,0:T(8,128)S(1)} all-to-all(f32[8,20,256]{2,1,0:T(8,128)S(1)} %broadcast_in_dim.14), channel_id=1, replica_groups=mesh['z'=8,'x'=4,'c'=2,'tp'=4] {'z'}, dimensions={0} | all-to-all | bytes 327680 | tf_op jit(solution)/shard_map/all_to_all | solution.py:217
  128.5 13.4 %all_to_all.36 = f32[4,160,256]{2,1,0:T(8,128)S(1)} all-to-all(f32[4,160,256]{2,1,0:T(8,128)S(1)} %broadcast_in_dim.16), channel_id=1, replica_groups=mesh['z'=8,'x'=4,'c'=2,'tp'=4] {'x'}, dimensions={0} | all-to-all | bytes 1310720 | tf_op jit(solution)/shard_map/all_to_all | solution.py:217
  143.0 4.0 %add.152 = f32[640,1280]{1,0:T(8,128)} add(f32[640,1280]{1,0:T(8,128)S(1)} %copy-done.3, f32[640,1280]{1,0:T(8,128)} %collective-permute-done.10) | non-fusion elementwise | flops 819200 | bytes 9830400 | tf_op jit(solution)/shard_map/add | solution.py:268
  151.9 5.0 %shard_map.87 = f32[256,256]{1,0:T(8,128)} custom-call(s32[3]{0:T(128)} %pad_add_fusion.at, f32[640,256]{1,0:T(8,128)} %bitcast.39, f32[640,256]{1,0:T(8,128)} %collective-permute-done.11.far), custom_call_target="tpu_custom_call" | custom-call | tf_op jit(solution)/shard_map/pallas_call | solution.py:69
  157.8 2.2 collective-permute-done.13
  160.0 3.8 %collective-permute-done.12 = f32[208,256]{1,0:T(8,128)S(1)} collective-permute-done((f32[208,256]{1,0:T(8,128)S(1)}, f32[208,256]{1,0:T(8,128)S(1)}, u32[]{:S(2)}, u32[]{:S(2)}) %collective-permute-start.12) | collective-permute-done | bytes 213024 | tf_op jit(solution)/shard_map/ppermute | solution.py:34
  164.9 2.1 collective-permute-done.18
  166.9 1.9 convolution_add_fusion
  168.8 13.9 %all_to_all.37 = f32[4,160,256]{2,1,0:T(8,128)S(1)} all-to-all(f32[4,160,256]{2,1,0:T(8,128)S(1)} %bitcast.43), channel_id=1, replica_groups=mesh['z'=8,'x'=4,'c'=2,'tp'=4] {'x'}, dimensions={0} | all-to-all | bytes 1310720 | tf_op jit(solution)/shard_map/all_to_all | solution.py:209
  182.8 12.6 %all_to_all.38 = f32[8,20,256]{2,1,0:T(8,128)S(1)} all-to-all(f32[8,20,256]{2,1,0:T(8,128)S(1)} %reshape.37), channel_id=1, replica_groups=mesh['z'=8,'x'=4,'c'=2,'tp'=4] {'z'}, dimensions={0} | all-to-all | bytes 327680 | tf_op jit(solution)/shard_map/all_to_all | solution.py:211
  195.4 12.2 %all_to_all.39 = f32[8,20,256]{2,1,0:T(8,128)S(1)} all-to-all(f32[8,20,256]{2,1,0:T(8,128)S(1)} %broadcast_in_dim.17), channel_id=1, replica_groups=mesh['z'=8,'x'=4,'c'=2,'tp'=4] {'z'}, dimensions={0} | all-to-all | bytes 327680 | tf_op jit(solution)/shard_map/all_to_all | solution.py:217
  208.5 4.9 %all-to-all-start.6 = ((f32[4,160,256]{2,1,0:T(8,128)}), f32[4,160,256]{2,1,0:T(8,128)S(1)}, u32[]{:S(2)}, u32[]{:S(2)}) async-start(f32[4,160,256]{2,1,0:T(8,128)} %broadcast_in_dim.37), calls=%async_computation.7 | async-start | bytes 1310720 | tf_op jit(solution)/shard_map/all_to_all | solution.py:217
  216.0 4.8 %all-to-all-done.6 = f32[4,160,256]{2,1,0:T(8,128)S(1)} async-done(((f32[4,160,256]{2,1,0:T(8,128)}), f32[4,160,256]{2,1,0:T(8,128)S(1)}, u32[]{:S(2)}, u32[]{:S(2)}) %all-to-all-start.6) | async-done | bytes 655392 | tf_op jit(solution)/shard_map/all_to_all | solution.py:217
  221.0 2.7 %collective-permute-done.16 = f32[256,256]{1,0:T(8,128)} collective-permute-done((f32[256,256]{1,0:T(8,128)S(1)}, f32[256,256]{1,0:T(8,128)}, u32[]{:S(2)}, u32[]{:S(2)}) %collective-permute-start.16) | collective-permute-done | bytes 262176 | tf_op jit(solution)/shard_map/ppermute | solution.py:34
  223.7 2.8 %collective-permute-done.15 = f32[256,256]{1,0:T(8,128)} collective-permute-done((f32[256,256]{1,0:T(8,128)S(1)}, f32[256,256]{1,0:T(8,128)}, u32[]{:S(2)}, u32[]{:S(2)}) %collective-permute-start.15) | collective-permute-done | bytes 262176 | tf_op jit(solution)/shard_map/ppermute | solution.py:34
  228.5 9.0 %shard_map.88 = (f32[256,512]{1,0:T(8,128)}, f32[256,256]{1,0:T(8,128)}) custom-call(s32[2]{0:T(128)} %iota_multiply_fusion.at, f32[256,512]{1,0:T(8,128)} %pad_maximum_fusion.5.work_in, f32[256,256]{1,0:T(8,128)} %copy-done.6), custom_call_target="tpu_custom_call" | custom-call | tf_op jit(solution)/shard_map/pallas_call | solution.py:69
  237.9 9.2 %shard_map.89 = (f32[256,512]{1,0:T(8,128)}, f32[256,256]{1,0:T(8,128)}) custom-call(s32[2]{0:T(128)} %call_exported.1.at, f32[256,512]{1,0:T(8,128)} %get-tuple-element.24.work_in, f32[256,256]{1,0:T(8,128)} %get-tuple-element.25.done), custom_call_target="tpu_custom_call" | custom-call | tf_op jit(solution)/shard_map/pallas_call | solution.py:69
  260.8 1.8 fusion.8
  (111 shorter events, 44.8 us)
Async XLA Ops:
  7.2 95.4 %all-gather.2.cloned.1.call-start = ((), (), s32[]{:S(2)}) async-start(), calls=%async_computation.8 | async-start | bytes 3276800 | tf_op jit(solution)/shard_map/all_gather | solution.py:237
  11.2 12.2 %collective-permute-start.2 = (f32[208,256]{1,0:T(8,128)S(1)}, f32[208,256]{1,0:T(8,128)S(1)}, u32[]{:S(2)}, u32[]{:S(2)}) collective-permute-start(f32[208,256]{1,0:T(8,128)S(1)} %fusion), channel_id=1, source_target_pairs={{0,3},{1,0},{2,1},{3,2},{4,7},{5,4},{6,5},{7,6},{8,11},{9,8},{10,9... | collective-permute-start | bytes 638984 | tf_op jit(solution)/shard_map/ppermute | solution.py:34
  14.3 9.7 %collective-permute-start.1 = (f32[208,256]{1,0:T(8,128)S(1)}, f32[208,256]{1,0:T(8,128)S(1)}, u32[]{:S(2)}, u32[]{:S(2)}) collective-permute-start(f32[208,256]{1,0:T(8,128)S(1)} %fusion), channel_id=1, source_target_pairs={{0,2},{1,3},{2,0},{3,1},{4,6},{5,7},{6,4},{7,5},{8,10},{9,11},{10,... | collective-permute-start | bytes 638984 | tf_op jit(solution)/shard_map/ppermute | solution.py:34
  14.9 12.3 %collective-permute-start = (f32[208,256]{1,0:T(8,128)S(1)}, f32[208,256]{1,0:T(8,128)}, u32[]{:S(2)}, u32[]{:S(2)}) collective-permute-start(f32[208,256]{1,0:T(8,128)S(1)} %fusion), channel_id=1, source_target_pairs={{0,1},{1,2},{2,3},{3,0},{4,5},{5,6},{6,7},{7,4},{8,9},{9,10},{10,1... | collective-permute-start | bytes 638984 | tf_op jit(solution)/shard_map/ppermute | solution.py:34
  17.0 12.0 %copy-start.4 = (f32[128,640]{1,0:T(8,128)}, f32[128,640]{1,0:T(8,128)S(1)}, u32[]{:S(2)}) copy-start(f32[128,640]{1,0:T(8,128)S(1)} %get-tuple-element.30) | copy-start | bytes 983044
  29.0 2.3 collective-permute-start.3
  34.1 38.0 %all-to-all-start = ((f32[32,20,256]{2,1,0:T(8,128)}), f32[32,20,256]{2,1,0:T(8,128)S(1)}, u32[]{:S(2)}, u32[]{:S(2)}) async-start(f32[32,20,256]{2,1,0:T(8,128)} %reshape.33), calls=%async_computation | async-start | bytes 1572864 | tf_op jit(solution)/shard_map/all_to_all | solution.py:203
  45.7 215.0 %reduce-scatter.2.cloned.1.call-start = ((), (), s32[]{:S(2)}) async-start(), calls=%async_computation.9 | async-start | bytes 3686400 | tf_op jit(solution)/shard_map/reduce_scatter | solution.py:269
  50.2 9.1 %collective-permute-start.6 = (f32[320,128]{1,0:T(8,128)S(1)}, f32[320,128]{1,0:T(8,128)S(1)}, u32[]{:S(2)}, u32[]{:S(2)}) collective-permute-start(f32[320,128]{1,0:T(8,128)S(1)} %get-tuple-element.32), channel_id=1, source_target_pairs={{0,24},{8,0},{16,8},{24,16},{1,25},{9,1},{17,9},{25,17},{2,26},{10... | collective-permute-start | bytes 491528 | tf_op jit(solution)/shard_map/ppermute | solution.py:34
  50.5 16.3 %collective-permute-start.5 = (f32[320,128]{1,0:T(8,128)S(1)}, f32[320,128]{1,0:T(8,128)S(1)}, u32[]{:S(2)}, u32[]{:S(2)}) collective-permute-start(f32[320,128]{1,0:T(8,128)S(1)} %get-tuple-element.33), channel_id=1, source_target_pairs={{0,16},{8,24},{16,0},{24,8},{1,17},{9,25},{17,1},{25,9},{2,18},{10... | collective-permute-start | bytes 491528 | tf_op jit(solution)/shard_map/ppermute | solution.py:34
  53.2 13.6 %collective-permute-start.4 = (f32[320,128]{1,0:T(8,128)S(1)}, f32[320,128]{1,0:T(8,128)S(1)}, u32[]{:S(2)}, u32[]{:S(2)}) collective-permute-start(f32[320,128]{1,0:T(8,128)S(1)} %get-tuple-element.34), channel_id=1, source_target_pairs={{0,8},{8,16},{16,24},{24,0},{1,9},{9,17},{17,25},{25,1},{2,10},{10... | collective-permute-start | bytes 491528 | tf_op jit(solution)/shard_map/ppermute | solution.py:34
  67.7 31.1 %collective-permute-start.9 = (f32[4,320,128]{2,1,0:T(8,128)}, f32[4,320,128]{2,1,0:T(8,128)}, u32[]{:S(2)}, u32[]{:S(2)}) collective-permute-start(f32[4,320,128]{2,1,0:T(8,128)} %pad_maximum_fusion.2.refs_0_), channel_id=1, source_target_pairs={{0,3},{1,0},{2,1},{3,2},{4,7},{5,4},{6,5},{7,6},{8,11},{9,8},{10,9... | collective-permute-start | bytes 1966088 | tf_op jit(solution)/shard_map/ppermute | solution.py:34
  70.5 28.4 %collective-permute-start.8 = (f32[4,320,128]{2,1,0:T(8,128)}, f32[4,320,128]{2,1,0:T(8,128)}, u32[]{:S(2)}, u32[]{:S(2)}) collective-permute-start(f32[4,320,128]{2,1,0:T(8,128)} %pad_maximum_fusion.2.refs_0_), channel_id=1, source_target_pairs={{0,2},{1,3},{2,0},{3,1},{4,6},{5,7},{6,4},{7,5},{8,10},{9,11},{10,... | collective-permute-start | bytes 1966088 | tf_op jit(solution)/shard_map/ppermute | solution.py:34
  71.3 31.3 %collective-permute-start.7 = (f32[4,320,128]{2,1,0:T(8,128)}, f32[4,320,128]{2,1,0:T(8,128)}, u32[]{:S(2)}, u32[]{:S(2)}) collective-permute-start(f32[4,320,128]{2,1,0:T(8,128)} %pad_maximum_fusion.2.refs_0_), channel_id=1, source_target_pairs={{0,1},{1,2},{2,3},{3,0},{4,5},{5,6},{6,7},{7,4},{8,9},{9,10},{10,1... | collective-permute-start | bytes 1966088 | tf_op jit(solution)/shard_map/ppermute | solution.py:34
  110.4 32.6 %collective-permute-start.10 = (f32[640,1280]{1,0:T(8,128)}, f32[640,1280]{1,0:T(8,128)}, u32[]{:S(2)}, u32[]{:S(2)}) collective-permute-start(f32[640,1280]{1,0:T(8,128)} %get-tuple-element.20), channel_id=1, source_target_pairs={{0,4},{4,0},{1,5},{5,1},{2,6},{6,2},{3,7},{7,3},{8,12},{12,8},{9,1... | collective-permute-start | bytes 9830408 | tf_op jit(solution)/shard_map/ppermute | solution.py:38
  128.4 13.5 %copy-start.9 = (f32[80,640]{1,0:T(8,128)S(1)}, f32[80,640]{1,0:T(8,128)}, u32[]{:S(2)}) copy-start(f32[80,640]{1,0:T(8,128)} %copy-done.8) | copy-start | bytes 614404
  128.4 14.6 %copy-start.3 = (f32[640,1280]{1,0:T(8,128)S(1)}, f32[640,1280]{1,0:T(8,128)}, u32[]{:S(2)}) copy-start(f32[640,1280]{1,0:T(8,128)} %get-tuple-element.19) | copy-start | bytes 9830404
  141.9 5.2 %collective-permute-start.11 = (f32[640,256]{1,0:T(8,128)S(1)}, f32[640,256]{1,0:T(8,128)}, u32[]{:S(2)}, u32[]{:S(2)}) collective-permute-start(f32[640,256]{1,0:T(8,128)S(1)} %bitcast.37), channel_id=1, source_target_pairs={{0,4},{4,0},{1,5},{5,1},{2,6},{6,2},{3,7},{7,3},{8,12},{12,8},{9,1... | collective-permute-start | bytes 1966088 | tf_op jit(solution)/shard_map/ppermute | solution.py:38
  149.6 8.2 %collective-permute-start.14 = (f32[208,256]{1,0:T(8,128)S(1)}, f32[208,256]{1,0:T(8,128)S(1)}, u32[]{:S(2)}, u32[]{:S(2)}) collective-permute-start(f32[208,256]{1,0:T(8,128)S(1)} %convolution_add_fusion.2), channel_id=1, source_target_pairs={{0,3},{1,0},{2,1},{3,2},{4,7},{5,4},{6,5},{7,6},{8,11},{9,8},{10,9... | collective-permute-start | bytes 638984 | tf_op jit(solution)/shard_map/ppermute | solution.py:34
  150.3 9.7 %collective-permute-start.13 = (f32[208,256]{1,0:T(8,128)S(1)}, f32[208,256]{1,0:T(8,128)S(1)}, u32[]{:S(2)}, u32[]{:S(2)}) collective-permute-start(f32[208,256]{1,0:T(8,128)S(1)} %convolution_add_fusion.2), channel_id=1, source_target_pairs={{0,2},{1,3},{2,0},{3,1},{4,6},{5,7},{6,4},{7,5},{8,10},{9,11},{10,... | collective-permute-start | bytes 638984 | tf_op jit(solution)/shard_map/ppermute | solution.py:34
  151.1 12.7 %collective-permute-start.12 = (f32[208,256]{1,0:T(8,128)S(1)}, f32[208,256]{1,0:T(8,128)S(1)}, u32[]{:S(2)}, u32[]{:S(2)}) collective-permute-start(f32[208,256]{1,0:T(8,128)S(1)} %convolution_add_fusion.2), channel_id=1, source_target_pairs={{0,1},{1,2},{2,3},{3,0},{4,5},{5,6},{6,7},{7,4},{8,9},{9,10},{10,1... | collective-permute-start | bytes 638984 | tf_op jit(solution)/shard_map/ppermute | solution.py:34
  151.9 11.9 %copy-start.1 = (f32[80,1280]{1,0:T(8,128)S(1)}, f32[80,1280]{1,0:T(8,128)}, u32[]{:S(2)}) copy-start(f32[80,1280]{1,0:T(8,128)} %param.8) | copy-start | bytes 1228804
  164.6 2.3 collective-permute-start.18
  208.5 12.2 %all-to-all-start.6 = ((f32[4,160,256]{2,1,0:T(8,128)}), f32[4,160,256]{2,1,0:T(8,128)S(1)}, u32[]{:S(2)}, u32[]{:S(2)}) async-start(f32[4,160,256]{2,1,0:T(8,128)} %broadcast_in_dim.37), calls=%async_computation.7 | async-start | bytes 1310720 | tf_op jit(solution)/shard_map/all_to_all | solution.py:217
  213.4 7.6 %collective-permute-start.17 = (f32[256,256]{1,0:T(8,128)S(1)}, f32[256,256]{1,0:T(8,128)S(1)}, u32[]{:S(2)}, u32[]{:S(2)}) collective-permute-start(f32[256,256]{1,0:T(8,128)S(1)} %copy-done.11), channel_id=1, source_target_pairs={{0,3},{1,0},{2,1},{3,2},{4,7},{5,4},{6,5},{7,6},{8,11},{9,8},{10,9... | collective-permute-start | bytes 786440 | tf_op jit(solution)/shard_map/ppermute | solution.py:34
  214.0 9.8 %collective-permute-start.16 = (f32[256,256]{1,0:T(8,128)S(1)}, f32[256,256]{1,0:T(8,128)}, u32[]{:S(2)}, u32[]{:S(2)}) collective-permute-start(f32[256,256]{1,0:T(8,128)S(1)} %copy-done.11), channel_id=1, source_target_pairs={{0,2},{1,3},{2,0},{3,1},{4,6},{5,7},{6,4},{7,5},{8,10},{9,11},{10,... | collective-permute-start | bytes 786440 | tf_op jit(solution)/shard_map/ppermute | solution.py:34
  214.7 11.8 %collective-permute-start.15 = (f32[256,256]{1,0:T(8,128)S(1)}, f32[256,256]{1,0:T(8,128)}, u32[]{:S(2)}, u32[]{:S(2)}) collective-permute-start(f32[256,256]{1,0:T(8,128)S(1)} %copy-done.11), channel_id=1, source_target_pairs={{0,1},{1,2},{2,3},{3,0},{4,5},{5,6},{6,7},{7,4},{8,9},{9,10},{10,1... | collective-permute-start | bytes 786440 | tf_op jit(solution)/shard_map/ppermute | solution.py:34
  216.0 12.5 %copy-start.6 = (f32[256,256]{1,0:T(8,128)}, f32[256,256]{1,0:T(8,128)S(1)}, u32[]{:S(2)}) copy-start(f32[256,256]{1,0:T(8,128)S(1)} %fusion.9.done) | copy-start | bytes 786436
  220.7 29.2 %collective-permute-start.19 = (f32[640,256]{1,0:T(8,128)S(1)}, f32[640,256]{1,0:T(8,128)}, u32[]{:S(2)}, u32[]{:S(2)}) collective-permute-start(f32[640,256]{1,0:T(8,128)S(1)} %bitcast.40), channel_id=1, source_target_pairs={{0,4},{4,0},{1,5},{5,1},{2,6},{6,2},{3,7},{7,3},{8,12},{12,8},{9,1... | collective-permute-start | bytes 1966088 | tf_op jit(solution)/shard_map/ppermute | solution.py:38
  251.7 5.2 %collective-permute-start.21 = (f32[8,256]{1,0:T(8,128)S(1)}, f32[8,256]{1,0:T(8,128)S(1)}, u32[]{:S(2)}, u32[]{:S(2)}) collective-permute-start(f32[8,256]{1,0:T(8,128)S(1)} %broadcast_in_dim.38), channel_id=1, source_target_pairs={{0,2},{1,3},{2,0},{3,1},{4,6},{5,7},{6,4},{7,5},{8,10},{9,11},{10,... | collective-permute-start | bytes 24584 | tf_op jit(solution)/shard_map/ppermute | solution.py:34
  252.5 4.5 %collective-permute-start.22 = (f32[8,256]{1,0:T(8,128)S(1)}, f32[8,256]{1,0:T(8,128)S(1)}, u32[]{:S(2)}, u32[]{:S(2)}) collective-permute-start(f32[8,256]{1,0:T(8,128)S(1)} %broadcast_in_dim.38), channel_id=1, source_target_pairs={{0,3},{1,0},{2,1},{3,2},{4,7},{5,4},{6,5},{7,6},{8,11},{9,8},{10,9... | collective-permute-start | bytes 24584 | tf_op jit(solution)/shard_map/ppermute | solution.py:34
  253.7 4.9 %collective-permute-start.20 = (f32[8,256]{1,0:T(8,128)S(1)}, f32[8,256]{1,0:T(8,128)S(1)}, u32[]{:S(2)}, u32[]{:S(2)}) collective-permute-start(f32[8,256]{1,0:T(8,128)S(1)} %broadcast_in_dim.38), channel_id=1, source_target_pairs={{0,1},{1,2},{2,3},{3,0},{4,5},{5,6},{6,7},{7,4},{8,9},{9,10},{10,1... | collective-permute-start | bytes 24584 | tf_op jit(solution)/shard_map/ppermute | solution.py:34
  (8 other events, 21.1 us)
Sparse Core Ops, SparseCore 0:
  11.3 41.9 all-gather.1
  147.2 40.6 reduce-scatter.1
